TPU v7x, 32 devices: a whole 2x2x4 slice. The times are simulated.
32 devices in a mesh: dp: 4 (over x, core), tensor: 8 (over z, y).
Axes of the slice: x: 2, y: 2, z: 4, core: 2. Of those that a mesh axis runs over, the one named last changes fastest.
Arguments:
- activations: bfloat16 [4, 2048, 512], P('dp', 'tensor'), may hold values from -6 to 6
- out_grad: bfloat16 [4, 2048, 28672], P('dp', None, 'tensor'), may hold values from -0.125 to 0.125
- residual: float32 [4, 512, 28672], P('dp', None, 'tensor'), may hold values from -4 to 4
- chosen: int32 [4, 8, 896], P(None, 'tensor'), may hold values from 0 to 3583, as said below
- master: float32 [512, 28672], P('dp', 'tensor'), may hold values from -6 to 6
- moment_one: float32 [512, 28672], P('dp', 'tensor'), may hold values from -4 to 4
- moment_two: float32 [512, 28672], P('dp', 'tensor'), may hold values from 0.01 to 1
- params: bfloat16 [512, 28672], P(None, 'tensor'), may hold values from -6 to 6
Outputs:
- new_residual: float32 [4, 512, 28672], P('dp', None, 'tensor')
- new_moment_one: float32 [512, 28672], P('dp', 'tensor')
- new_moment_two: float32 [512, 28672], P('dp', 'tensor')
- new_master: float32 [512, 28672], P('dp', 'tensor')
- new_params: bfloat16 [512, 28672], P(None, 'tensor')
Inputs may be any that keep to these rules, and one draw needn't show every extreme that they name: For each owner o and column shard t, chosen[o, t] holds 896 distinct span numbers of that owner's rows and that shard's columns, the same for every replica.
All inputs are finite; a program needn't handle non-finite values.
Results may differ from a plain program's by a relative error of at most 0.001.
Values may be sent and summed in bfloat16 or wider, within the bound.
No kernel may reach another device: no remote copies, remote signals or barrier semaphores. Data moves between devices by JAX's collectives and lax.ppermute only.
A program may use at most 128 MiB of HBM per device.

v0:
```python
import jax
import jax.numpy as jnp
from jax import lax
from jax.sharding import PartitionSpec as P

beta_one = 0.9
beta_two = 0.999
learn_rate = 0.01
decay_rate = 0.1
epsilon = 1e-08


def local(activations, out_grad, residual, chosen, master, moment_one, moment_two, params):
    token_grad = out_grad[0]
    row_count = activations.shape[2]
    column_count = token_grad.shape[1]
    weight_grad = lax.dot_general(
        lax.all_gather(activations, "tensor", axis=1, tiled=True)[0],
        token_grad,
        (((0,), (0,)), ((), ())),
        preferred_element_type=jnp.float32,
    )
    accumulated = residual[0] + weight_grad
    dp_count = lax.axis_size("dp")
    owner_rows = row_count // dp_count
    per_owner = owner_rows * (column_count // 128)
    span_ids = chosen[:, 0, :]
    blocks = accumulated.reshape(dp_count, per_owner, 128)
    packed = jnp.take_along_axis(blocks, span_ids[:, :, None], axis=1)
    owner_range = jnp.arange(dp_count, dtype=jnp.int32)[:, None]
    chosen_mask = jnp.zeros((dp_count, per_owner), jnp.float32).at[owner_range, span_ids].set(1.0)
    new_residual = (blocks * (1.0 - chosen_mask[:, :, None])).reshape(1, row_count, column_count)
    received = lax.all_to_all(
        packed.astype(jnp.bfloat16), "dp", split_axis=0, concat_axis=0, tiled=True
    ).astype(packed.dtype)
    mean_grad = jnp.sum(received, axis=0) / dp_count
    owner_index = lax.axis_index("dp")
    own_ids = lax.dynamic_index_in_dim(span_ids, owner_index, 0, keepdims=False)

    def select(values):
        return jnp.take(values.reshape(per_owner, 128), own_ids, axis=0)

    def replace(values, update):
        return values.reshape(per_owner, 128).at[own_ids].set(update).reshape(values.shape)

    moment_next = beta_one * select(moment_one) + (1.0 - beta_one) * mean_grad
    second_next = beta_two * select(moment_two) + (1.0 - beta_two) * mean_grad * mean_grad
    weights_now = select(master)
    master_next = weights_now - learn_rate * (
        moment_next / (jnp.sqrt(second_next) + epsilon) + decay_rate * weights_now
    )
    rounded = master_next.astype(jnp.bfloat16)
    new_moment_one = replace(moment_one, moment_next)
    new_moment_two = replace(moment_two, second_next)
    new_master = replace(master, master_next)
    own_params = lax.dynamic_slice_in_dim(params, owner_index * owner_rows, owner_rows, 0)
    own_params = replace(own_params, rounded)
    new_params = lax.all_gather(own_params, "dp", axis=0, tiled=True)
    return (new_residual, new_moment_one, new_moment_two, new_master, new_params)


def solution(mesh):
    in_specs = (
        P("dp", "tensor", None),
        P("dp", None, "tensor"),
        P("dp", None, "tensor"),
        P(None, "tensor", None),
        P("dp", "tensor"),
        P("dp", "tensor"),
        P("dp", "tensor"),
        P(None, "tensor"),
    )
    out_specs = (
        P("dp", None, "tensor"),
        P("dp", "tensor"),
        P("dp", "tensor"),
        P("dp", "tensor"),
        P(None, "tensor"),
    )
    return jax.shard_map(local, mesh=mesh, in_specs=in_specs, out_specs=out_specs, check_vma=False)
```

profile of v0, /device:TPU:0, one launch (start us, length us, event | category | flops | bytes accessed | tf_op | source)
XLA Modules:
  0.0 254.2 jit_solution(10884798870354926355)
XLA Ops:
  9.6 3.1 %reshape.136 = f32[3584,128]{1,0:T(8,128)} reshape(f32[128,3584]{1,0:T(8,128)} %param.16) | data formatting | bytes 3670016 | tf_op jit(solution)/shard_map/reshape | solution.py:44
  14.6 3.4 %gather_fusion.2 = f32[896,128]{1,0:T(8,128)S(1)} fusion(f32[3584,128]{1,0:T(8,128)} %reshape.136, s32[1024]{0:T(1024)S(1)} %pad_clamp_fusion), kind=kCustom, calls=%fused_computation.1.clone | custom fusion | bytes 921088 | tf_op jit(solution)/shard_map/jit(_take)/gather | solution.py:41
  19.6 2.8 %gather_fusion.3 = f32[896,128]{1,0:T(8,128)} fusion(f32[3584,128]{1,0:T(8,128)S(1)} %reshape.138, s32[1024]{0:T(1024)S(1)} %pad_clamp_fusion), kind=kCustom, calls=%fused_computation.2.clone | custom fusion | bytes 921088 | tf_op jit(solution)/shard_map/jit(_take)/gather | solution.py:41
  22.4 39.8 %all-gather.3.cloned.1.call-done = bf16[1,2048,512]{2,1,0:T(8,128)(2,1)} async-done(((bf16[1,256,512]{2,1,0:T(8,128)(2,1)}), bf16[1,2048,512]{2,1,0:T(8,128)(2,1)}) %all-gather.3.cloned.1.call-update) | async-done | bytes 2097168 | tf_op jit(solution)/shard_map/all_gather | solution.py:18
  62.2 14.7 %bitcast_add_fusion = f32[512,3584]{1,0:T(8,128)} fusion(f32[1,512,3584]{2,1,0:T(8,128)} %param.12, bf16[1,2048,3584]{2,1,0:T(8,128)(2,1)} %param.11, bf16[1,2048,512]{2,1,0:T(8,128)(2,1)} %all-gather.3.cloned.1.call-done), kind=kOutput, calls=%fused_computation.11 | convolution fusion | flops 7518027776 | bytes 31457280 | tf_op jit(solution)/shard_map/dot_general | solution.py:17
  76.8 8.3 %reshape.134 = bf16[4,3584,128]{2,1,0:T(8,128)(2,1)} reshape(f32[512,3584]{1,0:T(8,128)} %bitcast_add_fusion) | data formatting | bytes 11010048 | tf_op jit(solution)/shard_map/reshape | solution.py:28
  85.1 61.4 %gather_fusion = bf16[3584,128]{1,0:T(8,128)(2,1)} fusion(bf16[4,3584,128]{2,1,0:T(8,128)(2,1)} %reshape.134, s32[3584]{0:T(1024)S(1)} %reshape.172), kind=kCustom, calls=%fused_computation.3 | custom fusion | bytes 1863680 | tf_op jit(solution)/shard_map/jit(take_along_axis)/gather | solution.py:29
  146.5 2.4 select_convert_fusion
  148.9 4.2 %all-to-all-start = ((bf16[4,896,128]{2,1,0:T(8,128)(2,1)}), bf16[4,896,128]{2,1,0:T(8,128)(2,1)}, u32[]{:S(2)}, u32[]{:S(2)}) async-start(bf16[4,896,128]{2,1,0:T(8,128)(2,1)} %select_convert_fusion), calls=%async_computation | async-start | bytes 1835008 | tf_op jit(solution)/shard_map/all_to_all | solution.py:33
  155.6 3.0 %reshape.140 = bf16[3584,128]{1,0:T(8,128)(2,1)} reshape(bf16[128,3584]{1,0:T(8,128)(2,1)} %constant_dynamic-slice_fusion) | data formatting | bytes 1835008 | tf_op jit(solution)/shard_map/reshape | solution.py:44
  158.6 7.7 %all-to-all-done = bf16[4,896,128]{2,1,0:T(8,128)(2,1)} async-done(((bf16[4,896,128]{2,1,0:T(8,128)(2,1)}), bf16[4,896,128]{2,1,0:T(8,128)(2,1)}, u32[]{:S(2)}, u32[]{:S(2)}) %all-to-all-start) | async-done | bytes 917536 | tf_op jit(solution)/shard_map/all_to_all | solution.py:33
  167.6 2.2 multiply_subtract_fusion
  169.9 6.9 %scatter_custom_fusion.3 = bf16[3584,128]{1,0:T(8,128)(2,1)} fusion(bf16[3584,128]{1,0:T(8,128)(2,1)} %reshape.140, s32[896]{0:T(1024)S(1)} %fusion.13, f32[896,128]{1,0:T(8,128)} %multiply_subtract_fusion), kind=kCustom, calls=%fused_computation.21 | custom fusion | flops 114688 | bytes 1376256 | tf_op jit(solution)/shard_map/scatter | solution.py:44
  176.8 2.9 %reshape.141 = bf16[128,3584]{1,0:T(8,128)(2,1)} reshape(bf16[3584,128]{1,0:T(8,128)(2,1)} %scatter_custom_fusion.3) | data formatting | bytes 1835008 | tf_op jit(solution)/shard_map/reshape | solution.py:44
  179.9 13.7 %scatter_custom_fusion.4 = f32[14336]{0:T(1024)S(1)} fusion(s32[3584]{0:T(1024)S(1)} %reshape.210, f32[3584]{0:T(1024)S(1)} %broadcast.95, f32[]{:T(128)} %constant.18.clone.1), kind=kCustom, calls=%fused_computation.28 | custom fusion | bytes 57348
  193.7 4.3 %mul.52 = f32[4,3584,128]{2,1,0:T(8,128)} broadcast(f32[4,3584]{1,0:T(4,128)S(1)} %reshape.147), dimensions={0,1} | broadcast | bytes 7397376 | tf_op jit(solution)/shard_map/mul | solution.py:32
  198.0 8.4 %mul.53 = f32[512,3584]{1,0:T(8,128)} reshape(f32[4,3584,128]{2,1,0:T(8,128)} %mul.52) | data formatting | bytes 14680064 | tf_op jit(solution)/shard_map/mul | solution.py:32
  206.4 9.6 %multiply_bitcast_fusion = f32[1,512,3584]{2,1,0:T(8,128)} fusion(f32[512,3584]{1,0:T(8,128)} %bitcast_add_fusion, f32[512,3584]{1,0:T(8,128)} %mul.53), kind=kLoop, calls=%fused_computation.12 | loop fusion | flops 1835008 | bytes 22020096 | tf_op jit(solution)/shard_map/mul | solution.py:32
  215.9 5.5 %scatter_fusion = f32[3584,128]{1,0:T(8,128)S(1)} fusion(f32[3584,128]{1,0:T(8,128)S(1)} %reshape.138, s32[896]{0:T(1024)S(1)} %fusion.13, f32[896,128]{1,0:T(8,128)} %multiply_subtract_fusion), kind=kCustom, calls=%fused_computation.6 | custom fusion | bytes 1379840 | tf_op jit(solution)/shard_map/scatter | solution.py:44
  221.4 7.5 %scatter_custom_fusion = f32[3584,128]{1,0:T(8,128)} fusion(f32[3584,128]{1,0:T(8,128)} %copy-done, s32[896]{0:T(1024)S(1)} %fusion.13, f32[896,128]{1,0:T(8,128)S(1)} %gather_fusion.1, f32[896,128]{1,0:T(8,128)S(1)} %convert_reduce_fusion, f32[]{:T(128)} %constant.23.clone.1, f32[]{:T(128)} %constant.24.clone.1, f32[]{:T(128)} %constant.32.clone.1, ...), kind=kCustom, calls=%fused_computation.35 | custom fusion | flops 458752 | bytes 2755072 | tf_op jit(solution)/shard_map/scatter | solution.py:44
  228.9 2.7 %reshape.135 = f32[128,3584]{1,0:T(8,128)} reshape(f32[3584,128]{1,0:T(8,128)} %scatter_custom_fusion) | data formatting | bytes 3670016 | tf_op jit(solution)/shard_map/reshape | solution.py:44
  231.6 7.5 %scatter_custom_fusion.1 = f32[3584,128]{1,0:T(8,128)} fusion(f32[3584,128]{1,0:T(8,128)} %reshape.136, s32[896]{0:T(1024)S(1)} %fusion.13, f32[896,128]{1,0:T(8,128)S(1)} %gather_fusion.2, f32[896,128]{1,0:T(8,128)S(1)} %convert_reduce_fusion, f32[]{:T(128)} %constant.23.clone.1, f32[]{:T(128)} %constant.37.clone.1, f32[]{:T(128)} %constant.36.clone.1, ...), kind=kCustom, calls=%fused_computation.42 | custom fusion | flops 688128 | bytes 2755072 | tf_op jit(solution)/shard_map/scatter | solution.py:44
  239.1 2.7 %reshape.137 = f32[128,3584]{1,0:T(8,128)} reshape(f32[3584,128]{1,0:T(8,128)} %scatter_custom_fusion.1) | data formatting | bytes 3670016 | tf_op jit(solution)/shard_map/reshape | solution.py:44
  243.3 4.1 %copy.22 = bf16[512,3584]{1,0:T(8,128)(2,1)} copy(bf16[512,3584]{1,0:T(8,128)(2,1)} %all-gather.5.cloned.1.call-done) | data formatting | bytes 7340032
  (35 shorter events, 11.4 us)
Async XLA Ops:
  7.2 55.0 %all-gather.3.cloned.1.call-start = ((), (), s32[]{:S(2)}) async-start(), calls=%async_computation.1 | async-start | bytes 2359296 | tf_op jit(solution)/shard_map/all_gather | solution.py:18
  7.9 1.6 copy-start.1
  9.4 3.3 %copy-start = (f32[3584,128]{1,0:T(8,128)}, f32[3584,128]{1,0:T(8,128)S(1)}, u32[]{:S(2)}) copy-start(f32[3584,128]{1,0:T(8,128)S(1)} %reshape.133) | copy-start | bytes 5505028
  148.9 17.3 %all-to-all-start = ((bf16[4,896,128]{2,1,0:T(8,128)(2,1)}), bf16[4,896,128]{2,1,0:T(8,128)(2,1)}, u32[]{:S(2)}, u32[]{:S(2)}) async-start(bf16[4,896,128]{2,1,0:T(8,128)(2,1)} %select_convert_fusion), calls=%async_computation | async-start | bytes 1835008 | tf_op jit(solution)/shard_map/all_to_all | solution.py:33
  153.2 90.1 %all-gather.5.cloned.1.call-start = ((), (), s32[]{:S(2)}) async-start(), calls=%async_computation.2 | async-start | bytes 4587520 | tf_op jit(solution)/shard_map/all_gather | solution.py:58
  169.9 9.8 %copy-start.3 = (s32[2]{0:T(128)S(1)}, s32[2]{0:T(128)}, u32[]{:S(2)}) copy-start(s32[2]{0:T(128)} %constant.75) | copy-start | bytes 28
  169.9 9.9 %copy-start.2 = (s32[2]{0:T(128)S(1)}, s32[2]{0:T(128)}, u32[]{:S(2)}) copy-start(s32[2]{0:T(128)} %constant.78) | copy-start | bytes 28
Sparse Core Ops, SparseCore 0:
  10.1 51.9 all-gather.2
  179.7 29.0 all-gather.4
where the time goes:
time: 256 us; the launch traced here: 254 us
  local copies, waits for them, and re-layouts  135 us (53%)
  waiting for transfers between devices  48.2 us (19%)
  other arithmetic  37.9 us (15%)
  matrix products  14.7 us (6%)
  between operations  14.2 us (6%)
  starting transfers between devices  4.46 us (2%)
    gather x1, local copies, waits for them, and re-layouts, local(): packed = jnp.take_along_axis(blocks, span_ids[:, :, None], axis=1)  61.4 us
    all_gather x1, waiting for transfers between devices, local(): lax.all_gather(activations, 'tensor', axis=1, tiled=True)[0]  39.8 us
    scatter x3, other arithmetic, replace(): values.reshape(per_owner, 128).at[own_ids].set(update).reshape(values.shape)  21.9 us
    reshape x8, local copies, waits for them, and re-layouts, replace(): values.reshape(per_owner, 128).at[own_ids].set(update).reshape(values.shape)  18.8 us
    unnamed x12, local copies, waits for them, and re-layouts  17.8 us
    dot_general x1, matrix products, local(): lax.dot_general(lax.all_gather(activations, 'tensor', axis=1, tiled=True)...  14.7 us
    mul x2, local copies, waits for them, and re-layouts, local(): blocks * (1.0 - chosen_mask[:, :, None])  12.7 us
    mul x1, other arithmetic, local(): blocks * (1.0 - chosen_mask[:, :, None])  9.57 us
  transfers between devices with their start and end apart: 3, of which 2 were waited for; matrix products, arithmetic and copies ran while one was open for 33% of the time, Pallas kernels for 0%

commit v1 on v0

v1 whole, which is shorter than its diff:
```python
import functools
import jax
import jax.numpy as jnp
import numpy as np
from jax import lax
from jax.experimental import pallas as pl
from jax.experimental.pallas import tpu as pltpu
from jax.sharding import PartitionSpec as P

beta_one = 0.9
beta_two = 0.999
learn_rate = 0.01
decay_rate = 0.1
epsilon = 1e-08
LANES = 128
SUBLANES = 8
UNROLL = 16


def ring_order(count):
    inner = 4 if count % 16 == 0 else 2
    outer = count // inner
    cells = []
    for row in range(outer):
        steps = range(1, inner) if row % 2 == 0 else range(inner - 1, 0, -1)
        cells += [row * inner + step for step in steps]
    return cells + [row * inner for row in range(outer - 1, -1, -1)]


def plan_table(dp_count, tensor_count):
    ring = ring_order(tensor_count)
    place = {cell: i for i, cell in enumerate(ring)}
    chips = dp_count // 2
    table = np.zeros((dp_count, tensor_count, tensor_count + dp_count), np.int32)
    for d in range(dp_count):
        owners = [((d // 2 + k) % chips) * 2 + ((d % 2) ^ j) for k in range(chips) for j in range(2)]
        for t in range(tensor_count):
            table[d, t, :tensor_count] = [ring[(place[t] + j) % tensor_count] for j in range(tensor_count)]
            table[d, t, tensor_count:] = owners
    return table


def tiles(values):
    rows, columns = values.shape
    split = values.reshape(rows // SUBLANES, SUBLANES, columns // LANES, LANES)
    return split.transpose(0, 2, 1, 3).reshape(rows * columns // LANES, LANES)


def untiles(values, rows, columns):
    split = values.reshape(rows // SUBLANES, columns // LANES, SUBLANES, LANES)
    return split.transpose(0, 2, 1, 3).reshape(rows, columns)


def params_of(limit_mib):
    return pltpu.CompilerParams(vmem_limit_bytes=limit_mib << 20)


def whole(shape):
    return pl.BlockSpec(shape, lambda i, *_: (0,) * len(shape))


def each_row(count, body):
    def step(i, carry):
        for k in range(UNROLL):
            body(i * UNROLL + k)
        return carry

    lax.fori_loop(0, count // UNROLL, step, 0)


def accumulate_body(chunk_count, plan_ref, base_ref, *refs):
    total = base_ref[...]
    for j in range(chunk_count):
        total = total + lax.dot_general(
            refs[j][...], refs[chunk_count + j][...], (((0,), (0,)), ((), ())), preferred_element_type=jnp.float32
        )
    refs[-1][...] = total


def accumulate(plan, base, chunks, places, token_grad):
    rows, columns = base.shape
    tokens = chunks[0].shape[0]
    width = columns // 7
    grad_specs = [pl.BlockSpec((tokens, width), lambda i, plan, j=j: (plan[j], i)) for j in places]
    return pl.pallas_call(
        functools.partial(accumulate_body, len(chunks)),
        out_shape=jax.ShapeDtypeStruct(base.shape, jnp.float32),
        grid_spec=pltpu.PrefetchScalarGridSpec(
            num_scalar_prefetch=1,
            grid=(columns // width,),
            in_specs=[pl.BlockSpec((rows, width), lambda i, plan: (0, i))]
            + [whole((tokens, rows))] * len(chunks)
            + grad_specs,
            out_specs=pl.BlockSpec((rows, width), lambda i, plan: (0, i)),
        ),
        cost_estimate=pl.CostEstimate(
            flops=2 * rows * columns * tokens * len(chunks),
            bytes_accessed=8 * rows * columns + 2 * tokens * columns * len(chunks),
            transcendentals=0,
        ),
        compiler_params=params_of(24),
        name="accumulate",
    )(plan, base, *chunks, *([token_grad] * len(chunks)))


def finish_body(sizes, first, plan_ref, ids_ref, base_ref, front_ref, back_ref, grad_ref, *refs):
    per_owner, owner_rows, count, place = sizes
    out_ref, packed_ref, rows_ref, part_ref = refs[-4:]
    half, columns = front_ref.shape[0], grad_ref.shape[1]
    owner = plan_ref[place]
    blocks = columns // LANES
    wide = 2 * LANES
    offset = pl.multiple_of(lax.rem(owner * owner_rows, front_ref.shape[1]), SUBLANES)
    for start in range(0, columns, wide):
        part = lax.dot_general(
            front_ref[...], grad_ref[:half, start : start + wide], (((0,), (0,)), ((), ())), preferred_element_type=jnp.float32
        ) + lax.dot_general(
            back_ref[...], grad_ref[half:, start : start + wide], (((0,), (0,)), ((), ())), preferred_element_type=jnp.float32
        )
        if front_ref.shape[1] != owner_rows:
            part_ref[...] = part
            part = part_ref[pl.ds(offset, owner_rows), :]
        for r in range(owner_rows // SUBLANES):
            for c in range(wide // LANES):
                at = (r * blocks + start // LANES + c) * SUBLANES
                out_ref[at : at + SUBLANES, :] = (
                    base_ref[at : at + SUBLANES, :]
                    + part[r * SUBLANES : (r + 1) * SUBLANES, c * LANES : (c + 1) * LANES]
                )
    zero = jnp.zeros((1, LANES), jnp.float32)
    begin = owner * count

    def move(i):
        at = ids_ref[begin + i]
        rows_ref[pl.ds(i, 1), :] = out_ref[pl.ds(at, 1), :]
        out_ref[pl.ds(at, 1), :] = zero

    each_row(count, move)
    packed_ref[...] = rows_ref[...].astype(packed_ref.dtype)


def finish(plan, ids, base, front, back, token_grad, residual, place, origin, count, kind):
    dp_count = ids.shape[0] // count
    per_owner = base.shape[0] // dp_count
    half, rows = front.shape
    owner_rows = rows // dp_count
    columns = token_grad.shape[1]
    lanes = max(LANES, owner_rows)
    ratio = lanes // owner_rows
    first = residual is None
    operands = [plan, ids, base, front, back, token_grad]
    in_specs = [
        pl.BlockSpec((per_owner, LANES), lambda i, plan, ids: (plan[place], 0)),
        pl.BlockSpec((half, lanes), lambda i, plan, ids: (0, plan[place] // ratio)),
        pl.BlockSpec((half, lanes), lambda i, plan, ids: (0, plan[place] // ratio)),
        pl.BlockSpec((2 * half, columns), lambda i, plan, ids: (plan[origin], 0)),
    ]
    aliases = {}
    if not first:
        aliases = {len(operands): 0}
        operands.append(residual)
        in_specs.append(pl.BlockSpec(memory_space=pl.ANY))
    return pl.pallas_call(
        functools.partial(finish_body, (per_owner, owner_rows, count, place), first),
        out_shape=[jax.ShapeDtypeStruct(base.shape, jnp.float32), jax.ShapeDtypeStruct((count, LANES), kind)],
        grid_spec=pltpu.PrefetchScalarGridSpec(
            num_scalar_prefetch=2,
            grid=(1,),
            in_specs=in_specs,
            out_specs=[
                pl.BlockSpec((per_owner, LANES), lambda i, plan, ids: (plan[place], 0)),
                whole((count, LANES)),
            ],
            scratch_shapes=[pltpu.VMEM((count, LANES), jnp.float32), pltpu.VMEM((lanes, 2 * LANES), jnp.float32)],
        ),
        input_output_aliases=aliases,
        cost_estimate=pl.CostEstimate(
            flops=4 * half * per_owner * LANES + 5000 * count * LANES,
            bytes_accessed=8 * per_owner * LANES + 4 * half * columns,
            transcendentals=0,
        ),
        compiler_params=params_of(24),
        name="finish",
    )(*operands)


def fetch_body(count, place, plan_ref, ids_ref, one_ref, two_ref, master_ref, *outs):
    begin = plan_ref[place] * count

    def move(i):
        at = ids_ref[begin + i]
        for source, target in zip((one_ref, two_ref, master_ref), outs):
            target[pl.ds(i, 1), :] = source[pl.ds(at, 1), :]

    each_row(count, move)


def fetch(plan, ids, states, place, count):
    size = states[0].shape
    return pl.pallas_call(
        functools.partial(fetch_body, count, place),
        out_shape=[jax.ShapeDtypeStruct((count, LANES), jnp.float32)] * 3,
        grid_spec=pltpu.PrefetchScalarGridSpec(
            num_scalar_prefetch=2,
            grid=(1,),
            in_specs=[whole(size)] * 3,
            out_specs=[whole((count, LANES))] * 3,
        ),
        cost_estimate=pl.CostEstimate(flops=0, bytes_accessed=12 * size[0] * LANES, transcendentals=0),
        compiler_params=params_of(24),
        name="fetch",
    )(plan, ids, *states)


def store_body(count, place, plan_ref, ids_ref, *refs):
    old, new, outs = refs[:3], refs[3:6], refs[6:]
    begin = plan_ref[place] * count
    for source, target in zip(old, outs):
        target[...] = source[...]

    def move(i):
        at = ids_ref[begin + i]
        for source, target in zip(new, outs):
            target[pl.ds(at, 1), :] = source[pl.ds(i, 1), :]

    each_row(count, move)


def store(plan, ids, states, updates, place, count):
    size = states[0].shape
    return pl.pallas_call(
        functools.partial(store_body, count, place),
        out_shape=[jax.ShapeDtypeStruct(size, jnp.float32)] * 3,
        grid_spec=pltpu.PrefetchScalarGridSpec(
            num_scalar_prefetch=2,
            grid=(1,),
            in_specs=[whole(size)] * 3 + [whole((count, LANES))] * 3,
            out_specs=[whole(size)] * 3,
        ),
        cost_estimate=pl.CostEstimate(flops=0, bytes_accessed=24 * size[0] * LANES, transcendentals=0),
        compiler_params=params_of(32),
        name="store",
    )(plan, ids, *states, *updates)


def spread_body(count, place, plan_ref, ids_ref, params_ref, update_ref, *refs):
    out_ref, dense_ref, rows_ref = refs[-3:]
    begin = plan_ref[place] * count
    dense_ref[...] = params_ref[...].astype(jnp.float32)
    rows_ref[...] = update_ref[...].astype(jnp.float32)

    def move(i):
        at = ids_ref[begin + i]
        dense_ref[pl.ds(at, 1), :] = rows_ref[pl.ds(i, 1), :]

    each_row(count, move)
    out_ref[...] = dense_ref[...].astype(out_ref.dtype)


def spread(plan, ids, weights, update, earlier, place, count):
    dp_count = ids.shape[0] // count
    per_owner = weights.shape[0] // dp_count
    operands = [plan, ids, weights, update]
    mine = pl.BlockSpec((per_owner, LANES), lambda i, plan, ids: (plan[place], 0))
    in_specs = [mine, whole((count, LANES))]
    aliases = {}
    if earlier is not None:
        aliases = {len(operands): 0}
        operands.append(earlier)
        in_specs.append(pl.BlockSpec(memory_space=pl.ANY))
    return pl.pallas_call(
        functools.partial(spread_body, count, place),
        out_shape=jax.ShapeDtypeStruct(weights.shape, weights.dtype),
        grid_spec=pltpu.PrefetchScalarGridSpec(
            num_scalar_prefetch=2,
            grid=(1,),
            in_specs=in_specs,
            out_specs=mine,
            scratch_shapes=[pltpu.VMEM((per_owner, LANES), jnp.float32), pltpu.VMEM((count, LANES), jnp.float32)],
        ),
        input_output_aliases=aliases,
        cost_estimate=pl.CostEstimate(
            flops=0, bytes_accessed=12 * per_owner * LANES, transcendentals=0
        ),
        compiler_params=params_of(24),
        name="spread",
    )(*operands)


def local(table, ring, activations, out_grad, residual, chosen, master, moment_one, moment_two, params):
    token_grad = out_grad[0]
    own = activations[0]
    tokens, row_count = own.shape
    column_count = token_grad.shape[1]
    dp_count, tensor_count = table.shape[:2]
    chips = dp_count // 2
    owner_rows = row_count // dp_count
    count = chosen.shape[2]
    blocks = column_count // LANES

    plan = jnp.asarray(table)[lax.axis_index("dp"), lax.axis_index("tensor")]
    spans = chosen[:, 0, :]
    row, column = spans // blocks, spans % blocks
    ids = ((row // SUBLANES * blocks + column) * SUBLANES + row % SUBLANES).reshape(-1)

    ahead = [(ring[i], ring[(i + 1) % tensor_count]) for i in range(tensor_count)]
    behind = [(b, a) for a, b in ahead]

    states = [tiles(v) for v in (moment_one, moment_two, master)]
    place_of = lambda k, j: tensor_count + 2 * k + j
    own_place = place_of(0, 0)

    total = accumulate(plan, residual[0], [own], [0], token_grad)
    front = back = own
    for hop in range(1, tensor_count // 2):
        front = lax.ppermute(front, "tensor", ahead)
        back = lax.ppermute(back, "tensor", behind)
        total = accumulate(plan, total, [front, back], [tensor_count - hop, hop], token_grad)
    front = lax.ppermute(front[: tokens // 2], "tensor", ahead)
    back = lax.ppermute(back[tokens // 2 :], "tensor", behind)

    picked = fetch(plan, ids, states, own_place, count)
    total = tiles(total)
    left = None

    def close(left, k, j, kind):
        return finish(
            plan, ids, total, front, back, token_grad, left, place_of(k, j), tensor_count // 2, count, kind
        )

    def swap(values):
        return lax.ppermute(values, "dp", [(d, d ^ 1) for d in range(dp_count)])

    def send(values, k):
        return lax.ppermute(
            values, "dp", [(d, ((d // 2 + k) % chips) * 2 + d % 2) for d in range(dp_count)]
        )

    received = []
    for k in range(1, chips):
        left, other = close(left, k, 1, jnp.bfloat16)
        other = swap(other)
        left, mine = close(left, k, 0, jnp.float32)
        received.append(send((mine + other.astype(jnp.float32)).astype(jnp.bfloat16), k))
    left, other = close(left, 0, 1, jnp.bfloat16)
    received.append(swap(other))
    left, mine = close(left, 0, 0, jnp.float32)
    for part in received:
        mine = mine + part.astype(jnp.float32)
    mean_grad = mine / dp_count

    one, two, weights = picked
    one = beta_one * one + (1.0 - beta_one) * mean_grad
    two = beta_two * two + (1.0 - beta_two) * mean_grad * mean_grad
    weights = weights - learn_rate * (one / (jnp.sqrt(two) + epsilon) + decay_rate * weights)
    rounded = weights.astype(jnp.bfloat16)

    far = [send(rounded, k) for k in range(1, chips)]
    near = swap(rounded)
    fresh = store(plan, ids, states, [one, two, weights], own_place, count)
    flat = tiles(params)
    out = spread(plan, ids, flat, rounded, None, own_place, count)
    out = spread(plan, ids, flat, near, out, place_of(0, 1), count)
    for k in range(1, chips):
        across = swap(far[k - 1])
        out = spread(plan, ids, flat, far[k - 1], out, place_of(chips - k, 0), count)
        out = spread(plan, ids, flat, across, out, place_of(chips - k, 1), count)

    new_one, new_two, new_master = (untiles(v, owner_rows, column_count) for v in fresh)
    return (
        untiles(left, row_count, column_count)[None],
        new_one,
        new_two,
        new_master,
        untiles(out, row_count, column_count),
    )


def solution(mesh):
    dp_count, tensor_count = mesh.shape["dp"], mesh.shape["tensor"]
    body = functools.partial(local, plan_table(dp_count, tensor_count), ring_order(tensor_count))
    in_specs = (
        P("dp", "tensor", None),
        P("dp", None, "tensor"),
        P("dp", None, "tensor"),
        P(None, "tensor", None),
        P("dp", "tensor"),
        P("dp", "tensor"),
        P("dp", "tensor"),
        P(None, "tensor"),
    )
    out_specs = (
        P("dp", None, "tensor"),
        P("dp", "tensor"),
        P("dp", "tensor"),
        P("dp", "tensor"),
        P(None, "tensor"),
    )
    return jax.shard_map(body, mesh=mesh, in_specs=in_specs, out_specs=out_specs, check_vma=False)
```

time: 256 us -> 114 us (0.45)
  local copies, waits for them, and re-layouts: 135 us -> 26 us
  Pallas kernels: 0 us -> 61.6 us
  waiting for transfers between devices: 48.2 us -> 11 us
  other arithmetic: 37.9 us -> 2.12 us
  matrix products: 14.7 us -> 0 us
  between operations: 14.2 us -> 0.83 us
  starting transfers between devices: 4.46 us -> 12 us
    gather x4 -> x0, local copies, waits for them, and re-layouts: 69.5 us -> none  [the longest x1 61.4 us: local(): packed = jnp.take_along_axis(blocks, span_ids[:, :, None], axis=1)]
    pallas_call x0 -> x14, Pallas kernels: none -> 61.6 us  [the longest x4 21.8 us: finish(): pl.pallas_call(functools.partial(finish_body, (per_owner, owner_rows, cou...]
    all_gather x2 -> x0, waiting for transfers between devices: 39.8 us -> none  [the longest x1 39.8 us: local(): lax.all_gather(activations, 'tensor', axis=1, tiled=True)[0]]
    reshape x9 -> x0, local copies, waits for them, and re-layouts: 27.1 us -> none  [the longest x8 18.8 us: replace(): values.reshape(per_owner, 128).at[own_ids].set(update).reshape(values.shape)]
    scatter x3 -> x0, other arithmetic: 21.9 us -> none  [replace(): values.reshape(per_owner, 128).at[own_ids].set(update).reshape(values.shape)]
    dot_general x1 -> x0, matrix products: 14.7 us -> none  [local(): lax.dot_general(lax.all_gather(activations, 'tensor', axis=1, tiled=True)...]
    mul x2 -> x0, local copies, waits for them, and re-layouts: 12.7 us -> none  [local(): blocks * (1.0 - chosen_mask[:, :, None])]
    ppermute x0 -> x14, starting transfers between devices: none -> 12 us  [the longest x3 6.43 us: local(): front = lax.ppermute(front, 'tensor', ahead)]
  transfers between devices with their start and end apart: 3 -> 14, of which waited for: 2 -> 2; matrix products, arithmetic and copies ran while one was open for 33% -> 2% of each run, Pallas kernels for 0% -> 47%
where the time goes in v1:
time: 114 us
  Pallas kernels  61.6 us (54%)
  local copies, waits for them, and re-layouts  26 us (23%)
  starting transfers between devices  12 us (11%)
  waiting for transfers between devices  11 us (10%)
  other arithmetic  2.12 us (2%)
    unnamed x34, local copies, waits for them, and re-layouts  25.3 us
    pallas_call x4, Pallas kernels, finish(): pl.pallas_call(functools.partial(finish_body, (per_owner, owner_rows, cou...  21.8 us
    pallas_call x4, Pallas kernels, accumulate(): pl.pallas_call(functools.partial(accumulate_body, len(chunks)), out_shape...  19.8 us
    pallas_call x4, Pallas kernels, spread(): pl.pallas_call(functools.partial(spread_body, count, place), out_shape=ja...  12.3 us
    ppermute x2, waiting for transfers between devices, send(): lax.ppermute(values, 'dp', [(d, (d // 2 + k) % chips * 2 + d % 2) for d i...  6.86 us
    ppermute x3, starting transfers between devices, local(): front = lax.ppermute(front, 'tensor', ahead)  6.43 us
    pallas_call x1, Pallas kernels, store(): pl.pallas_call(functools.partial(store_body, count, place), out_shape=[ja...  5.24 us
    ppermute x3, waiting for transfers between devices, local(): front = lax.ppermute(front, 'tensor', ahead)  4.14 us
  transfers between devices with their start and end apart: 14, of which 2 were waited for; matrix products, arithmetic and copies ran while one was open for 2% of the time, Pallas kernels for 47%

profile of v1, /device:TPU:0, one launch (start us, length us, event | category | flops | bytes accessed | tf_op | source)
XLA Modules:
  0.0 113.7 jit_solution(13603527474880799829)
XLA Ops:
  0.6 3.0 %collective-permute-start = (bf16[256,512]{1,0:T(8,128)(2,1)}, bf16[256,512]{1,0:T(8,128)(2,1)S(1)}, u32[]{:S(2)}, u32[]{:S(2)}) collective-permute-start(bf16[256,512]{1,0:T(8,128)(2,1)} %bitcast.83), channel_id=1, source_target_pairs={{1,3},{3,5},{5,7},{7,6},{6,4},{4,2},{2,0},{0,1},{9,11},{11,13},{13... | collective-permute-start | bytes 786440 | tf_op jit(solution)/shard_map/ppermute | solution.py:316
  6.1 4.1 %collective-permute-done.refs_0_ = bf16[256,512]{1,0:T(8,128)(2,1)S(1)} collective-permute-done((bf16[256,512]{1,0:T(8,128)(2,1)}, bf16[256,512]{1,0:T(8,128)(2,1)S(1)}, u32[]{:S(2)}, u32[]{:S(2)}) %collective-permute-start) | collective-permute-done | bytes 262176 | tf_op jit(solution)/shard_map/ppermute | solution.py:316
  12.3 5.2 %copy-done = bf16[1,2048,3584]{2,1,0:T(8,128)(2,1)S(1)} copy-done((bf16[1,2048,3584]{2,1,0:T(8,128)(2,1)S(1)}, bf16[1,2048,3584]{2,1,0:T(8,128)(2,1)}, u32[]{:S(2)}) %copy-start) | copy-done | bytes 14680088
  17.4 3.1 %copy-done.11 = f32[1,512,3584]{2,1,0:T(8,128)S(1)} copy-done((f32[1,512,3584]{2,1,0:T(8,128)S(1)}, f32[1,512,3584]{2,1,0:T(8,128)}, u32[]{:S(2)}) %copy-start.11) | copy-done | bytes 7340056
  21.5 4.1 %accumulate.4.base_ref = f32[512,3584]{1,0:T(8,128)S(1)} custom-call(s32[12]{0:T(128)S(1)} %dynamic-slice_bitcast_fusion.plan_ref, f32[512,3584]{1,0:T(8,128)S(1)} %bitcast.82, bf16[256,512]{1,0:T(8,128)(2,1)S(1)} %bitcast.85, bf16[2048,3584]{1,0:T(8,128)(2,1)S(1)} %bitcast.55), custom_call_target="tpu_custom_call" | custom-call | flops 939524096 | bytes 16515072 | tf_op jit(solution)/shard_map/accumulate/pallas_call | solution.py:85
  25.5 3.0 %copy-done.5 = f32[512,3584]{1,0:T(8,128)} copy-done((f32[512,3584]{1,0:T(8,128)}, f32[512,3584]{1,0:T(8,128)S(1)}, u32[]{:S(2)}) %copy-start.5) | copy-done | bytes 7340056
  28.7 1.7 %collective-permute-start.4 = (bf16[256,512]{1,0:T(8,128)(2,1)S(1)}, bf16[256,512]{1,0:T(8,128)(2,1)S(1)}, u32[]{:S(2)}, u32[]{:S(2)}) collective-permute-start(bf16[256,512]{1,0:T(8,128)(2,1)S(1)} %collective-permute-done.2.refs_0_), channel_id=1, source_target_pairs={{1,3},{3,5},{5,7},{7,6},{6,4},{4,2},{2,0},{0,1},{9,11},{11,13},{13... | collective-permute-start | bytes 786440 | tf_op jit(solution)/shard_map/ppermute | solution.py:316
  30.8 5.2 %copy-done.1 = bf16[1,2048,3584]{2,1,0:T(8,128)(2,1)S(1)} copy-done((bf16[1,2048,3584]{2,1,0:T(8,128)(2,1)S(1)}, bf16[1,2048,3584]{2,1,0:T(8,128)(2,1)}, u32[]{:S(2)}) %copy-start.1) | copy-done | bytes 14680088
  35.9 3.1 %copy-done.6 = f32[512,3584]{1,0:T(8,128)S(1)} copy-done((f32[512,3584]{1,0:T(8,128)S(1)}, f32[512,3584]{1,0:T(8,128)}, u32[]{:S(2)}) %copy-start.6) | copy-done | bytes 7340056
  39.0 5.2 %accumulate.5.base_ref = f32[512,3584]{1,0:T(8,128)S(1)} custom-call(s32[12]{0:T(128)S(1)} %dynamic-slice_bitcast_fusion.plan_ref, f32[512,3584]{1,0:T(8,128)S(1)} %copy-done.6, bf16[256,512]{1,0:T(8,128)(2,1)S(1)} %collective-permute-done.refs_0_, bf16[256,512]{1,0:T(8,128)(2,1)S(1)} %collective-permute-done.1.refs_1_, bf16[2048,3584]{1,0:T(8,128)(2,1)S(1)} %bitcast.56, ...), custom_call_target="tpu_custom_call" | custom-call | flops 1879048192 | bytes 18350080 | tf_op jit(solution)/shard_map/accumulate/pallas_call | solution.py:85
  44.3 5.2 %accumulate.6.base_ref = f32[512,3584]{1,0:T(8,128)S(1)} custom-call(s32[12]{0:T(128)S(1)} %dynamic-slice_bitcast_fusion.plan_ref, f32[512,3584]{1,0:T(8,128)S(1)} %accumulate.5.base_ref, bf16[256,512]{1,0:T(8,128)(2,1)S(1)} %collective-permute-done.2.refs_0_, bf16[256,512]{1,0:T(8,128)(2,1)S(1)} %collective-permute-done.3.refs_1_, ...), custom_call_target="tpu_custom_call" | custom-call | flops 1879048192 | bytes 18350080 | tf_op jit(solution)/shard_map/accumulate/pallas_call | solution.py:85
  51.7 5.2 %accumulate.7 = f32[512,3584]{1,0:T(8,128)S(1)} custom-call(s32[12]{0:T(128)S(1)} %dynamic-slice_bitcast_fusion.plan_ref, f32[512,3584]{1,0:T(8,128)S(1)} %accumulate.6.base_ref, bf16[256,512]{1,0:T(8,128)(2,1)S(1)} %collective-permute-done.4.refs_0_, bf16[256,512]{1,0:T(8,128)(2,1)S(1)} %collective-permute-done.5.refs_1_, bf16[2048,3584]{1,0:T(8,128)(2,1)S(1)} %bitcast.60, ...), custom_call_target="tpu_custom_call" | custom-call | flops 1879048192 | bytes 18350080 | tf_op jit(solution)/shard_map/accumulate/pallas_call | solution.py:85
  57.0 5.5 %finish.4 = (f32[14336,128]{1,0:T(8,128)}, bf16[896,128]{1,0:T(8,128)(2,1)S(1)}) custom-call(s32[12]{0:T(128)S(1)} %dynamic-slice_bitcast_fusion.plan_ref, s32[3584]{0:T(1024)S(1)} %fusion.3.ids_ref, f32[14336,128]{1,0:T(8,128)S(1)} %bitcast.68, bf16[128,512]{1,0:T(8,128)(2,1)S(1)} %collective-permute-done.6.front_ref, ...), custom_call_target="tpu_custom_call" | custom-call | flops 808321024 | bytes 5505024 | tf_op jit(solution)/shard_map/finish/pallas_call | solution.py:163
  62.4 5.4 %finish.5 = (f32[14336,128]{1,0:T(8,128)}, f32[896,128]{1,0:T(8,128)S(1)}) custom-call(s32[12]{0:T(128)S(1)} %dynamic-slice_bitcast_fusion.plan_ref, s32[3584]{0:T(1024)S(1)} %fusion.3.ids_ref, f32[14336,128]{1,0:T(8,128)S(1)} %bitcast.69, bf16[128,512]{1,0:T(8,128)(2,1)S(1)} %collective-permute-done.6.front_ref, ...), custom_call_target="tpu_custom_call", output_to_operand_aliasing={{0}: (6, {})} | custom-call | flops 808321024 | bytes 5505024 | tf_op jit(solution)/shard_map/finish/pallas_call | solution.py:163
  67.9 3.2 %copy-done.3 = f32[512,3584]{1,0:T(8,128)S(1)} copy-done((f32[512,3584]{1,0:T(8,128)S(1)}, f32[512,3584]{1,0:T(8,128)}, u32[]{:S(2)}) %copy-start.3) | copy-done | bytes 7340056
  71.1 5.5 %finish.6 = (f32[14336,128]{1,0:T(8,128)}, bf16[896,128]{1,0:T(8,128)(2,1)S(1)}) custom-call(s32[12]{0:T(128)S(1)} %dynamic-slice_bitcast_fusion.plan_ref, s32[3584]{0:T(1024)S(1)} %fusion.3.ids_ref, f32[14336,128]{1,0:T(8,128)S(1)} %bitcast.70, bf16[128,512]{1,0:T(8,128)(2,1)S(1)} %collective-permute-done.6.front_ref, ...), custom_call_target="tpu_custom_call", output_to_operand_aliasing={{0}: (6, {})} | custom-call | flops 808321024 | bytes 5505024 | tf_op jit(solution)/shard_map/finish/pallas_call | solution.py:163
  80.4 2.5 %fetch.1 = (f32[896,128]{1,0:T(8,128)S(1)}, f32[896,128]{1,0:T(8,128)S(1)}, f32[896,128]{1,0:T(8,128)S(1)}) custom-call(s32[12]{0:T(128)S(1)} %dynamic-slice_bitcast_fusion.plan_ref, s32[3584]{0:T(1024)S(1)} %fusion.3.ids_ref, f32[3584,128]{1,0:T(8,128)S(1)} %bitcast.76, f32[3584,128]{1,0:T(8,128)S(1)} %bitcast.78, f32[3584,128]{1,0:T(8,128)S(1)} %bitcast.80), custom_call_target="tpu_custom_call" | custom-call | bytes 5505024 | tf_op jit(solution)/shard_map/fetch/pallas_call | solution.py:200
  82.9 5.5 %finish.7 = (f32[14336,128]{1,0:T(8,128)}, f32[896,128]{1,0:T(8,128)S(1)}) custom-call(s32[12]{0:T(128)S(1)} %dynamic-slice_bitcast_fusion.plan_ref, s32[3584]{0:T(1024)S(1)} %fusion.3.ids_ref, f32[14336,128]{1,0:T(8,128)S(1)} %bitcast.71, bf16[128,512]{1,0:T(8,128)(2,1)S(1)} %collective-permute-done.6.front_ref, ...), custom_call_target="tpu_custom_call", output_to_operand_aliasing={{0}: (6, {})} | custom-call | flops 808321024 | bytes 5505024 | tf_op jit(solution)/shard_map/finish/pallas_call | solution.py:163
  89.2 6.9 %collective-permute-done.11.update_ref = bf16[896,128]{1,0:T(8,128)(2,1)S(1)} collective-permute-done((bf16[896,128]{1,0:T(8,128)(2,1)S(1)}, bf16[896,128]{1,0:T(8,128)(2,1)S(1)}, u32[]{:S(2)}, u32[]{:S(2)}) %collective-permute-start.11) | collective-permute-done | bytes 229408 | tf_op jit(solution)/shard_map/ppermute | solution.py:335
  96.1 3.1 %spread.4.refs_0_ = bf16[14336,128]{1,0:T(8,128)(2,1)} custom-call(s32[12]{0:T(128)S(1)} %dynamic-slice_bitcast_fusion.plan_ref, s32[3584]{0:T(1024)S(1)} %fusion.3.ids_ref, bf16[14336,128]{1,0:T(8,128)(2,1)S(1)} %bitcast.72, bf16[896,128]{1,0:T(8,128)(2,1)S(1)} %get-tuple-element.35.update_ref), custom_call_target="tpu_custom_call" | custom-call | bytes 5505024 | tf_op jit(solution)/shard_map/spread/pallas_call | solution.py:271
  99.2 5.2 %store.1 = (f32[3584,128]{1,0:T(8,128)}, f32[3584,128]{1,0:T(8,128)}, f32[3584,128]{1,0:T(8,128)}) custom-call(s32[12]{0:T(128)S(1)} %dynamic-slice_bitcast_fusion.plan_ref, s32[3584]{0:T(1024)S(1)} %fusion.3.ids_ref, f32[3584,128]{1,0:T(8,128)S(1)} %bitcast.77, f32[3584,128]{1,0:T(8,128)S(1)} %bitcast.79, f32[3584,128]{1,0:T(8,128)S(1)} %bitcast.81, ...), custom_call_target="tpu_custom_call" | custom-call | bytes 11010048 | tf_op jit(solution)/shard_map/store/pallas_call | solution.py:231
  104.4 3.1 %spread.5.refs_0_ = bf16[14336,128]{1,0:T(8,128)(2,1)} custom-call(s32[12]{0:T(128)S(1)} %dynamic-slice_bitcast_fusion.plan_ref, s32[3584]{0:T(1024)S(1)} %fusion.3.ids_ref, bf16[14336,128]{1,0:T(8,128)(2,1)S(1)} %bitcast.73, bf16[896,128]{1,0:T(8,128)(2,1)S(1)} %collective-permute-done.13.update_ref, ...), custom_call_target="tpu_custom_call", output_to_operand_aliasing={{}: (4, {})} | custom-call | bytes 5505024 | tf_op jit(solution)/shard_map/spread/pallas_call | solution.py:271
  107.5 3.1 %spread.6.refs_0_ = bf16[14336,128]{1,0:T(8,128)(2,1)} custom-call(s32[12]{0:T(128)S(1)} %dynamic-slice_bitcast_fusion.plan_ref, s32[3584]{0:T(1024)S(1)} %fusion.3.ids_ref, bf16[14336,128]{1,0:T(8,128)(2,1)S(1)} %bitcast.74, bf16[896,128]{1,0:T(8,128)(2,1)S(1)} %collective-permute-done.11.update_ref, ...), custom_call_target="tpu_custom_call", output_to_operand_aliasing={{}: (4, {})} | custom-call | bytes 5505024 | tf_op jit(solution)/shard_map/spread/pallas_call | solution.py:271
  110.6 3.1 %spread.7 = bf16[14336,128]{1,0:T(8,128)(2,1)} custom-call(s32[12]{0:T(128)S(1)} %dynamic-slice_bitcast_fusion.plan_ref, s32[3584]{0:T(1024)S(1)} %fusion.3.ids_ref, bf16[14336,128]{1,0:T(8,128)(2,1)S(1)} %bitcast.75, bf16[896,128]{1,0:T(8,128)(2,1)S(1)} %collective-permute-done.12.update_ref, ...), custom_call_target="tpu_custom_call", output_to_operand_aliasing={{}: (4, {})} | custom-call | bytes 5505024 | tf_op jit(solution)/shard_map/spread/pallas_call | solution.py:271
  (64 shorter events, 12.7 us)
Async XLA Ops:
  0.6 9.6 %collective-permute-start = (bf16[256,512]{1,0:T(8,128)(2,1)}, bf16[256,512]{1,0:T(8,128)(2,1)S(1)}, u32[]{:S(2)}, u32[]{:S(2)}) collective-permute-start(bf16[256,512]{1,0:T(8,128)(2,1)} %bitcast.83), channel_id=1, source_target_pairs={{1,3},{3,5},{5,7},{7,6},{6,4},{4,2},{2,0},{0,1},{9,11},{11,13},{13... | collective-permute-start | bytes 786440 | tf_op jit(solution)/shard_map/ppermute | solution.py:316
  3.6 8.3 %collective-permute-start.1 = (bf16[256,512]{1,0:T(8,128)(2,1)}, bf16[256,512]{1,0:T(8,128)(2,1)S(1)}, u32[]{:S(2)}, u32[]{:S(2)}) collective-permute-start(bf16[256,512]{1,0:T(8,128)(2,1)} %bitcast.84), channel_id=1, source_target_pairs={{3,1},{5,3},{7,5},{6,7},{4,6},{2,4},{0,2},{1,0},{11,9},{13,11},{15... | collective-permute-start | bytes 786440 | tf_op jit(solution)/shard_map/ppermute | solution.py:317
  10.2 18.4 %collective-permute-start.2 = (bf16[256,512]{1,0:T(8,128)(2,1)S(1)}, bf16[256,512]{1,0:T(8,128)(2,1)S(1)}, u32[]{:S(2)}, u32[]{:S(2)}) collective-permute-start(bf16[256,512]{1,0:T(8,128)(2,1)S(1)} %collective-permute-done.refs_0_), channel_id=1, source_target_pairs={{1,3},{3,5},{5,7},{7,6},{6,4},{4,2},{2,0},{0,1},{9,11},{11,13},{13... | collective-permute-start | bytes 786440 | tf_op jit(solution)/shard_map/ppermute | solution.py:316
  11.9 18.5 %collective-permute-start.3 = (bf16[256,512]{1,0:T(8,128)(2,1)S(1)}, bf16[256,512]{1,0:T(8,128)(2,1)S(1)}, u32[]{:S(2)}, u32[]{:S(2)}) collective-permute-start(bf16[256,512]{1,0:T(8,128)(2,1)S(1)} %collective-permute-done.1.refs_1_), channel_id=1, source_target_pairs={{3,1},{5,3},{7,5},{6,7},{4,6},{2,4},{0,2},{1,0},{11,9},{13,11},{15... | collective-permute-start | bytes 786440 | tf_op jit(solution)/shard_map/ppermute | solution.py:317
  12.3 5.2 %copy-start = (bf16[1,2048,3584]{2,1,0:T(8,128)(2,1)S(1)}, bf16[1,2048,3584]{2,1,0:T(8,128)(2,1)}, u32[]{:S(2)}) copy-start(bf16[1,2048,3584]{2,1,0:T(8,128)(2,1)} %param.10) | copy-start | bytes 44040196
  28.7 20.8 %collective-permute-start.4 = (bf16[256,512]{1,0:T(8,128)(2,1)S(1)}, bf16[256,512]{1,0:T(8,128)(2,1)S(1)}, u32[]{:S(2)}, u32[]{:S(2)}) collective-permute-start(bf16[256,512]{1,0:T(8,128)(2,1)S(1)} %collective-permute-done.2.refs_0_), channel_id=1, source_target_pairs={{1,3},{3,5},{5,7},{7,6},{6,4},{4,2},{2,0},{0,1},{9,11},{11,13},{13... | collective-permute-start | bytes 786440 | tf_op jit(solution)/shard_map/ppermute | solution.py:316
  30.4 20.9 %collective-permute-start.5 = (bf16[256,512]{1,0:T(8,128)(2,1)S(1)}, bf16[256,512]{1,0:T(8,128)(2,1)S(1)}, u32[]{:S(2)}, u32[]{:S(2)}) collective-permute-start(bf16[256,512]{1,0:T(8,128)(2,1)S(1)} %collective-permute-done.3.refs_1_), channel_id=1, source_target_pairs={{3,1},{5,3},{7,5},{6,7},{4,6},{2,4},{0,2},{1,0},{11,9},{13,11},{15... | collective-permute-start | bytes 786440 | tf_op jit(solution)/shard_map/ppermute | solution.py:317
  30.8 5.2 %copy-start.1 = (bf16[1,2048,3584]{2,1,0:T(8,128)(2,1)S(1)}, bf16[1,2048,3584]{2,1,0:T(8,128)(2,1)}, u32[]{:S(2)}) copy-start(bf16[1,2048,3584]{2,1,0:T(8,128)(2,1)} %param.10) | copy-start | bytes 44040196
  49.5 7.4 %collective-permute-start.6 = (bf16[128,512]{1,0:T(8,128)(2,1)S(1)}, bf16[128,512]{1,0:T(8,128)(2,1)S(1)}, u32[]{:S(2)}, u32[]{:S(2)}) collective-permute-start(bf16[128,512]{1,0:T(8,128)(2,1)S(1)} %slice.8), channel_id=1, source_target_pairs={{1,3},{3,5},{5,7},{7,6},{6,4},{4,2},{2,0},{0,1},{9,11},{11,13},{13... | collective-permute-start | bytes 393224 | tf_op jit(solution)/shard_map/ppermute | solution.py:319
  51.3 5.7 %collective-permute-start.7 = (bf16[128,512]{1,0:T(8,128)(2,1)S(1)}, bf16[128,512]{1,0:T(8,128)(2,1)S(1)}, u32[]{:S(2)}, u32[]{:S(2)}) collective-permute-start(bf16[128,512]{1,0:T(8,128)(2,1)S(1)} %slice.9), channel_id=1, source_target_pairs={{3,1},{5,3},{7,5},{6,7},{4,6},{2,4},{0,2},{1,0},{11,9},{13,11},{15... | collective-permute-start | bytes 393224 | tf_op jit(solution)/shard_map/ppermute | solution.py:320
  56.9 5.5 %copy-start.2 = (f32[512,3584]{1,0:T(8,128)}, f32[512,3584]{1,0:T(8,128)S(1)}, u32[]{:S(2)}) copy-start(f32[512,3584]{1,0:T(8,128)S(1)} %accumulate.7) | copy-start | bytes 22020100
  62.4 14.7 %collective-permute-start.8 = (bf16[896,128]{1,0:T(8,128)(2,1)S(1)}, bf16[896,128]{1,0:T(8,128)(2,1)S(1)}, u32[]{:S(2)}, u32[]{:S(2)}) collective-permute-start(bf16[896,128]{1,0:T(8,128)(2,1)S(1)} %get-tuple-element.26), channel_id=1, source_target_pairs={{0,8},{8,0},{16,24},{24,16},{1,9},{9,1},{17,25},{25,17},{2,10},{10... | collective-permute-start | bytes 688136 | tf_op jit(solution)/shard_map/ppermute | solution.py:332
  67.9 15.0 %slice-start = ((s8[14680064]{0:T(1024)(128)(4,1)}), s8[4194304]{0:T(1024)(128)(4,1)S(1)}, s32[]{:S(2)}) async-start(s8[14680064]{0:T(1024)(128)(4,1)} %bitcast.65), calls=%async_computation | async-start | bytes 8388608
  71.1 7.8 %copy-start.7 = (f32[128,3584]{1,0:T(8,128)S(1)}, f32[128,3584]{1,0:T(8,128)}, u32[]{:S(2)}) copy-start(f32[128,3584]{1,0:T(8,128)} %param.14) | copy-start | bytes 5505028
  71.1 7.8 %copy-start.8 = (f32[128,3584]{1,0:T(8,128)S(1)}, f32[128,3584]{1,0:T(8,128)}, u32[]{:S(2)}) copy-start(f32[128,3584]{1,0:T(8,128)} %param.15) | copy-start | bytes 5505028
  71.1 11.8 %slice-start.1 = ((s8[14680064]{0:T(1024)(128)(4,1)}), s8[4194304]{0:T(1024)(128)(4,1)S(1)}, s32[]{:S(2)}) async-start(s8[14680064]{0:T(1024)(128)(4,1)} %bitcast.65), calls=%async_computation.1 | async-start | bytes 8388608
  71.1 11.8 %slice-start.2 = ((s8[14680064]{0:T(1024)(128)(4,1)}), s8[4194304]{0:T(1024)(128)(4,1)S(1)}, s32[]{:S(2)}) async-start(s8[14680064]{0:T(1024)(128)(4,1)} %bitcast.65), calls=%async_computation.2 | async-start | bytes 8388608
  71.1 11.8 %slice-start.3 = ((s8[14680064]{0:T(1024)(128)(4,1)}), s8[2097152]{0:T(1024)(128)(4,1)S(1)}, s32[]{:S(2)}) async-start(s8[14680064]{0:T(1024)(128)(4,1)} %bitcast.65), calls=%async_computation.3 | async-start | bytes 4194304
  76.6 11.8 %collective-permute-start.10 = (bf16[896,128]{1,0:T(8,128)(2,1)S(1)}, bf16[896,128]{1,0:T(8,128)(2,1)S(1)}, u32[]{:S(2)}, u32[]{:S(2)}) collective-permute-start(bf16[896,128]{1,0:T(8,128)(2,1)S(1)} %get-tuple-element.27), channel_id=1, source_target_pairs={{0,8},{8,0},{16,24},{24,16},{1,9},{9,1},{17,25},{25,17},{2,10},{10... | collective-permute-start | bytes 688136 | tf_op jit(solution)/shard_map/ppermute | solution.py:332
  77.2 11.2 %collective-permute-start.9 = (bf16[896,128]{1,0:T(8,128)(2,1)S(1)}, bf16[896,128]{1,0:T(8,128)(2,1)S(1)}, u32[]{:S(2)}, u32[]{:S(2)}) collective-permute-start(bf16[896,128]{1,0:T(8,128)(2,1)S(1)} %add_convert_fusion), channel_id=1, source_target_pairs={{0,16},{8,24},{16,0},{24,8},{1,17},{9,25},{17,1},{25,9},{2,18},{10... | collective-permute-start | bytes 688136 | tf_op jit(solution)/shard_map/ppermute | solution.py:335
  88.4 7.7 %copy-start.4 = (bf16[512,3584]{1,0:T(8,128)(2,1)S(1)}, bf16[512,3584]{1,0:T(8,128)(2,1)}, u32[]{:S(2)}) copy-start(bf16[512,3584]{1,0:T(8,128)(2,1)} %param.16) | copy-start | bytes 11010052
  88.8 7.3 %collective-permute-start.11 = (bf16[896,128]{1,0:T(8,128)(2,1)S(1)}, bf16[896,128]{1,0:T(8,128)(2,1)S(1)}, u32[]{:S(2)}, u32[]{:S(2)}) collective-permute-start(bf16[896,128]{1,0:T(8,128)(2,1)S(1)} %get-tuple-element.35.update_ref), channel_id=1, source_target_pairs={{0,16},{8,24},{16,0},{24,8},{1,17},{9,25},{17,1},{25,9},{2,18},{10... | collective-permute-start | bytes 688136 | tf_op jit(solution)/shard_map/ppermute | solution.py:335
  89.2 15.2 %collective-permute-start.13 = (bf16[896,128]{1,0:T(8,128)(2,1)S(1)}, bf16[896,128]{1,0:T(8,128)(2,1)S(1)}, u32[]{:S(2)}, u32[]{:S(2)}) collective-permute-start(bf16[896,128]{1,0:T(8,128)(2,1)S(1)} %get-tuple-element.35.update_ref), channel_id=1, source_target_pairs={{0,8},{8,0},{16,24},{24,16},{1,9},{9,1},{17,25},{25,17},{2,10},{10... | collective-permute-start | bytes 688136 | tf_op jit(solution)/shard_map/ppermute | solution.py:332
  96.1 14.5 %collective-permute-start.12 = (bf16[896,128]{1,0:T(8,128)(2,1)S(1)}, bf16[896,128]{1,0:T(8,128)(2,1)S(1)}, u32[]{:S(2)}, u32[]{:S(2)}) collective-permute-start(bf16[896,128]{1,0:T(8,128)(2,1)S(1)} %collective-permute-done.11.update_ref), channel_id=1, source_target_pairs={{0,8},{8,0},{16,24},{24,16},{1,9},{9,1},{17,25},{25,17},{2,10},{10... | collective-permute-start | bytes 688136 | tf_op jit(solution)/shard_map/ppermute | solution.py:332
  (7 other events, 18.0 us)

commit v2 on v0

v2 whole, which is shorter than its diff:
```python
import functools
import jax
import jax.numpy as jnp
import numpy as np
from jax import lax
from jax.experimental import pallas as pl
from jax.experimental.pallas import tpu as pltpu
from jax.sharding import PartitionSpec as P

beta_one = 0.9
beta_two = 0.999
learn_rate = 0.01
decay_rate = 0.1
epsilon = 1e-08
LANES = 128
SUBLANES = 8
UNROLL = 16


def ring_order(count):
    inner = 4 if count % 16 == 0 else 2
    outer = count // inner
    cells = []
    for row in range(outer):
        steps = range(1, inner) if row % 2 == 0 else range(inner - 1, 0, -1)
        cells += [row * inner + step for step in steps]
    return cells + [row * inner for row in range(outer - 1, -1, -1)]


def plan_table(dp_count, tensor_count):
    ring = ring_order(tensor_count)
    place = {cell: i for i, cell in enumerate(ring)}
    chips = dp_count // 2
    table = np.zeros((dp_count, tensor_count, tensor_count + dp_count), np.int32)
    for d in range(dp_count):
        owners = [((d // 2 + k) % chips) * 2 + ((d % 2) ^ j) for k in range(chips) for j in range(2)]
        for t in range(tensor_count):
            table[d, t, :tensor_count] = [ring[(place[t] + j) % tensor_count] for j in range(tensor_count)]
            table[d, t, tensor_count:] = owners
    return table


def tiles(values):
    rows, columns = values.shape
    split = values.reshape(rows // SUBLANES, SUBLANES, columns // LANES, LANES)
    return split.transpose(0, 2, 1, 3).reshape(rows * columns // LANES, LANES)


def untiles(values, rows, columns):
    split = values.reshape(rows // SUBLANES, columns // LANES, SUBLANES, LANES)
    return split.transpose(0, 2, 1, 3).reshape(rows, columns)


VMEM = pltpu.MemorySpace.VMEM
HELD = pl.BlockSpec(memory_space=VMEM)
AWAY = pl.BlockSpec(memory_space=pl.ANY)
DMA = pltpu.SemaphoreType.DMA
WIDTH = 896
WEIGHT = 24


def each_group(count, body):
    def step(i, carry):
        body([i * UNROLL + k for k in range(UNROLL)])
        return carry

    lax.fori_loop(0, count // UNROLL, step, 0)


def gather_rows(look, count, pairs):
    def move(rows):
        at = [look(i) for i in rows]
        for source, target in pairs:
            values = [source[pl.ds(a, 1), :] for a in at]
            for i, value in zip(rows, values):
                target[pl.ds(i, 1), :] = value

    each_group(count, move)


def scatter_rows(look, count, pairs):
    def move(rows):
        at = [look(i) for i in rows]
        for source, target in pairs:
            values = [source[pl.ds(i, 1), :] for i in rows]
            for a, value in zip(at, values):
                target[pl.ds(a, 1), :] = value

    each_group(count, move)


def product(a, b):
    return lax.dot_general(a, b, (((0,), (0,)), ((), ())), preferred_element_type=jnp.float32)


def add_products(total_in, total_out, grad_ref, terms):
    columns = grad_ref.shape[1]
    width = WIDTH if columns % WIDTH == 0 else LANES

    def step(i, carry):
        at = pl.ds(pl.multiple_of(i * width, LANES), width)
        total = total_in[:, at]
        for chunk, start in terms:
            total = total + product(chunk[...], grad_ref[pl.ds(start, chunk.shape[0]), at])
        total_out[:, at] = total
        return carry

    lax.fori_loop(0, columns // width, step, 0)


def split_copies(source, target, parts, sems, first=0):
    size = source.shape[0] // parts
    return [
        pltpu.make_async_copy(source.at[pl.ds(k * size, size)], target.at[pl.ds(k * size, size)], sems.at[first + k])
        for k in range(parts)
    ]


def start_all(copies):
    for copy in copies:
        copy.start()


def wait_all(copies):
    for copy in copies:
        copy.wait()


def away(values):
    return pltpu.with_memory_space_constraint(values, pltpu.MemorySpace.HBM)


def call(body, name, scalars, operands, outs, scratch=(), aliases=None, flops=0, traffic=0):
    return pl.pallas_call(
        body,
        out_shape=[
            pltpu.VMEM(shape, kind) if held else jax.ShapeDtypeStruct(shape, kind) for shape, kind, held in outs
        ],
        grid_spec=pltpu.PrefetchScalarGridSpec(
            num_scalar_prefetch=len(scalars),
            grid=(1,),
            in_specs=[held if isinstance(held, pl.BlockSpec) else HELD if held else AWAY for _, held in operands],
            out_specs=[HELD if held else AWAY for _, _, held in outs],
            scratch_shapes=list(scratch),
        ),
        input_output_aliases={len(scalars) + k: v for k, v in (aliases or {}).items()},
        cost_estimate=pl.CostEstimate(flops=flops, bytes_accessed=traffic, transcendentals=0),
        compiler_params=pltpu.CompilerParams(vmem_limit_bytes=6 << 20),
        name=name,
    )(*scalars, *(values for values, _ in operands))


def look_in(ids_ref):
    return lambda i: ids_ref[0, i]


def look_from(ids_ref, per_owner, count):
    begin = ids_ref[0, count] * per_owner
    return lambda i: ids_ref[0, i] - begin


def ids_of(ids, place):
    return ids, pl.BlockSpec((None, *ids.shape[1:]), lambda i, *_: (place, 0, 0), memory_space=pltpu.SMEM)


def order_ids(plan_ref, spans_ref, ids_ref, columns, rows):
    dp_count, _, count = spans_ref.shape
    blocks = columns // LANES
    per_owner = rows // dp_count * blocks
    factor = -(-(1 << 18) // blocks)
    assert per_owner * (factor * blocks - (1 << 18)) < 1 << 18
    for p in range(dp_count):
        owner = plan_ref[plan_ref.shape[0] - dp_count + p]
        spans = spans_ref[owner]
        row = lax.shift_right_logical(spans * factor, 18)
        column = spans - row * blocks
        tile = lax.shift_right_logical(row, 3) * blocks + column
        ids_ref[p, :, :count] = tile * SUBLANES + (row & 7) + owner * per_owner
        ids_ref[p, :, count:] = jnp.full((1, LANES), 1, jnp.int32) * owner


def grad_copies(plan_ref, places, tokens, grad_ref, held_ref, sems, first=0):
    half, copies = tokens // 2, []
    for n, j in enumerate(places):
        for k in range(2):
            at = pl.ds(pl.multiple_of(plan_ref[j] * tokens + k * half, half), half)
            copies.append(pltpu.make_async_copy(grad_ref.at[at], held_ref.at[at], sems.at[first + 2 * n + k]))
    return copies


def load_body(
    places, plan_ref, residual_ref, grad_ref, own_ref, spans_ref, total_ref, held_ref, ids_ref, own_held, spans_held, sems, own_sems
):
    tokens = own_ref.shape[0]
    spans_copy = pltpu.make_async_copy(spans_ref, spans_held, own_sems.at[1])
    spans_copy.start()
    first = [pltpu.make_async_copy(own_ref, own_held, own_sems.at[0])]
    first += grad_copies(plan_ref, [0], tokens, grad_ref, held_ref, sems, 8)
    first += split_copies(residual_ref, total_ref, 8, sems)
    later = grad_copies(plan_ref, places, tokens, grad_ref, held_ref, sems, 10)
    start_all(first)
    spans_copy.wait()
    order_ids(plan_ref, spans_held, ids_ref, total_ref.shape[1], total_ref.shape[0])
    wait_all(first)
    start_all(later)
    add_products(total_ref, total_ref, held_ref, [(own_held, pl.multiple_of(plan_ref[0] * tokens, tokens))])
    wait_all(later)


def load(plan, residual, token_grad, own, spans, places):
    return call(
        functools.partial(load_body, places),
        "load",
        [plan],
        [(away(residual), False), (away(token_grad), False), (away(own), False), (away(spans), False)],
        [
            (residual.shape, jnp.float32, True),
            (token_grad.shape, token_grad.dtype, True),
            ((*spans.shape[:2], spans.shape[2] + LANES), jnp.int32, True),
        ],
        [
            pltpu.VMEM(own.shape, own.dtype),
            pltpu.VMEM(spans.shape, jnp.int32),
            DMA((10 + 2 * len(places),)),
            DMA((2,)),
        ],
        flops=WEIGHT * own.size * residual.shape[1],
        traffic=WEIGHT * residual.size,
    )


def accumulate_body(places, coming, tokens, side, plan_ref, total_in, held_in, grad_ref, *refs):
    chunks, refs = refs[: len(places)], refs[len(places) :]
    starts = [pl.multiple_of(plan_ref[j] * tokens, tokens) for j in places]
    extra = {"states": 3, "params": 1, "pick": 4}.get(side, 0)
    sources, (total_out, held_ref), refs = refs[:extra], refs[extra : extra + 2], refs[extra + 2 :]
    sems = refs[-1]
    copies = grad_copies(plan_ref, coming, tokens, grad_ref, held_ref, sems, 6)
    if side == "states":
        helds = refs[:3]
        copies += [c for n in range(3) for c in split_copies(sources[n], helds[n], 2, sems, 2 * n)]
    if side == "params":
        wide_ref, narrow_ref = refs[:2]
        copies += split_copies(sources[0], narrow_ref, 4, sems)
    start_all(copies)
    add_products(total_in, total_out, held_ref, list(zip(chunks, starts)))
    wait_all(copies)
    if side == "pick":
        count = refs[0].shape[0]
        gather_rows(look_from(sources[3], sources[0].shape[0], count), count, list(zip(sources[:3], refs[:3])))
    if side == "params":
        wide_ref[...] = narrow_ref[...].astype(jnp.float32)


def accumulate(plan, total, chunks, places, held_grad, token_grad, coming, side=None, sources=()):
    tokens = chunks[0].shape[0]
    outs, scratch = [(total.shape, jnp.float32, True), (held_grad.shape, held_grad.dtype, True)], []
    inputs = []
    if side == "states":
        inputs = [(away(v), False) for v in sources]
        outs += [(sources[0].shape, jnp.float32, True)] * 3
    if side == "pick":
        count = sources[3][0].shape[2] - LANES
        inputs = [(v, True) for v in sources[:3]] + [sources[3]]
        outs += [((count, LANES), jnp.float32, True)] * 3
    if side == "params":
        inputs = [(away(sources[0]), False)]
        outs += [(sources[0].shape, jnp.float32, True)]
        scratch = [pltpu.VMEM(sources[0].shape, sources[0].dtype)]
    return call(
        functools.partial(accumulate_body, places, coming, tokens, side),
        "accumulate",
        [plan],
        [(total, True), (held_grad, True), (away(token_grad), False)] + [(c, True) for c in chunks] + inputs,
        outs,
        scratch + [DMA((6 + 2 * len(coming),))],
        {0: 0, 1: 1},
        flops=WEIGHT * tokens * total.size * len(chunks),
        traffic=WEIGHT * total.size,
    )


def last_body(place, plan_ref, total_in, grad_ref, front_ref, back_ref, total_out, chunk_ref):
    half = front_ref.shape[0]
    chunk_ref[:half] = front_ref[...]
    chunk_ref[half:] = back_ref[...]
    add_products(total_in, total_out, grad_ref, [(chunk_ref, pl.multiple_of(plan_ref[place] * 2 * half, 2 * half))])


def last(plan, total, front, back, place, held_grad):
    half, rows = front.shape
    return call(
        functools.partial(last_body, place),
        "last",
        [plan],
        [(total, True), (held_grad, True), (front, True), (back, True)],
        [(total.shape, jnp.float32, True)],
        [pltpu.VMEM((2 * half, rows), front.dtype)],
        {0: 0},
        flops=4 * half * total.size,
        traffic=8 * total.size,
    )[0]


def pack_body(ids_ref, total_ref, *refs):
    packed_ref, rows_ref = refs[-2:]
    if packed_ref.dtype == jnp.float32:
        gather_rows(look_in(ids_ref), packed_ref.shape[0], [(total_ref, packed_ref)])
    else:
        gather_rows(look_in(ids_ref), packed_ref.shape[0], [(total_ref, rows_ref)])
        packed_ref[...] = rows_ref[...].astype(packed_ref.dtype)


def pack(ids, total, place, kind, after=()):
    shape = (ids.shape[2] - LANES, LANES)
    return call(
        pack_body,
        "pack",
        [],
        [ids_of(ids, place), (total, True)] + [(v, True) for v in after],
        [(shape, kind, True)],
        [pltpu.VMEM(shape, jnp.float32)],
        traffic=40 * shape[0] * LANES,
    )[0]


def clear(ids_ref, total_ref):
    zero = jnp.zeros((1, LANES), jnp.float32)

    def body(rows):
        for at in [ids_ref[0, i] for i in rows]:
            total_ref[pl.ds(at, 1), :] = zero

    each_group(ids_ref.shape[1] - LANES, body)


def close_body(others, own_ids, *refs):
    total_ref, packed_ref = refs[-2:]
    gather_rows(look_in(own_ids), packed_ref.shape[0], [(total_ref, packed_ref)])
    for ids_ref in (own_ids, *refs[:others]):
        clear(ids_ref, total_ref)


def close(ids, total, place, others, after):
    return call(
        functools.partial(close_body, len(others)),
        "close",
        [],
        [ids_of(ids, p) for p in (place, *others)] + [(total, True)] + [(v, True) for v in after],
        [(total.shape, jnp.float32, True), ((ids.shape[2] - LANES, LANES), jnp.float32, True)],
        (),
        {1 + len(others): 0},
        traffic=WEIGHT * total.size,
    )


def spread_one(ids_ref, update_ref, wide_ref, out_ref, rows_ref, block_ref, sems, first):
    per_owner, count = block_ref.shape[0], update_ref.shape[0]
    at = pl.ds(pl.multiple_of(ids_ref[0, count] * per_owner, 2 * SUBLANES), per_owner)
    rows_ref[...] = update_ref[...].astype(jnp.float32)
    scatter_rows(look_in(ids_ref), count, [(rows_ref, wide_ref)])
    block_ref[...] = wide_ref[at, :].astype(block_ref.dtype)
    copies = split_copies(block_ref, out_ref.at[at], 2, sems, first)
    start_all(copies)
    return copies


def store_body(dp_count, ids_ref, total_ref, *refs):
    refs = refs[3:]
    new, update_ref, refs = refs[:3], refs[4], refs[5:]
    helds, wide_ref, residual_ref, outs, out_ref = refs[:3], refs[3], refs[4], refs[5:8], refs[8]
    rows_ref, block_ref, sems = refs[9:]
    per_owner, count = block_ref.shape[0], update_ref.shape[0]
    copies = []
    used = 0

    def begin(source, target, parts):
        nonlocal used
        copies.extend(split_copies(source, target, parts, sems, used))
        start_all(copies[-parts:])
        used += parts

    begin(total_ref, residual_ref, 2 * dp_count)
    begin_at = look_from(ids_ref, per_owner, count)
    for n in range(3):
        scatter_rows(begin_at, count, [(new[n], helds[n])])
        begin(helds[n], outs[n], 2)
    copies.extend(spread_one(ids_ref, update_ref, wide_ref, out_ref, rows_ref, block_ref, sems, used))
    wait_all(copies)


def store(ids, total, helds, updates, wide, rounded, place):
    size, count, dp_count = helds[0].shape, ids.shape[2] - LANES, ids.shape[0]
    out = call(
        functools.partial(store_body, dp_count),
        "store",
        [],
        [ids_of(ids, place)] + [(v, True) for v in [total, *helds, *updates, wide, rounded]],
        [(size, jnp.float32, True)] * 3
        + [(wide.shape, jnp.float32, True), (total.shape, jnp.float32, False)]
        + [(size, jnp.float32, False)] * 3
        + [(wide.shape, rounded.dtype, False)],
        [pltpu.VMEM((count, LANES), jnp.float32), pltpu.VMEM(size, rounded.dtype), DMA((8 + 2 * dp_count,))],
        {2: 0, 3: 1, 4: 2, 8: 3},
        traffic=4 * WEIGHT * size[0] * LANES,
    )
    return out[4], out[5:8], out[3], out[8]


def relay(values, after):
    return call(
        lambda *_: None,
        "relay",
        [],
        [(values, True), (away(after), False)],
        [(values.shape, values.dtype, True)],
        (),
        {0: 0},
    )[0]


def spread_body(count, *refs):
    ids, updates = refs[:count], refs[count + 1 : 2 * count + 1]
    wide_ref, out_ref, rows_ref, blocks_ref, sems = refs[2 * count + 2 :]
    copies = []
    for n in range(count):
        copies += spread_one(ids[n], updates[n], wide_ref, out_ref, rows_ref, blocks_ref.at[n], sems, 2 * n)
    wait_all(copies)


def spread(ids, wide, earlier, updates, places):
    dp_count, n = ids.shape[0], len(places)
    kind = updates[0].dtype
    return call(
        functools.partial(spread_body, n),
        "spread",
        [],
        [ids_of(ids, place) for place in places] + [(wide, True)] + [(v, True) for v in updates] + [(earlier, False)],
        [(wide.shape, jnp.float32, True), (wide.shape, kind, False)],
        [
            pltpu.VMEM(updates[0].shape, jnp.float32),
            pltpu.VMEM((n, wide.shape[0] // dp_count, LANES), kind),
            DMA((2 * n,)),
        ],
        {n: 0, 1 + 2 * n: 1},
        traffic=WEIGHT * wide.size,
    )


def local(table, ring, activations, out_grad, residual, chosen, master, moment_one, moment_two, params):
    token_grad = out_grad[0]
    own = activations[0]
    tokens, row_count = own.shape
    column_count = token_grad.shape[1]
    dp_count, tensor_count = table.shape[:2]
    chips = dp_count // 2
    owner_rows = row_count // dp_count

    plan = jnp.asarray(table)[lax.axis_index("dp"), lax.axis_index("tensor")]
    ahead = [(ring[i], ring[(i + 1) % tensor_count]) for i in range(tensor_count)]
    behind = [(b, a) for a, b in ahead]

    def place_of(k, j):
        return 2 * k + j

    def swap(values):
        return lax.ppermute(values, "dp", [(d, d ^ 1) for d in range(dp_count)])

    def send(values, k):
        return lax.ppermute(values, "dp", [(d, ((d // 2 + k) % chips) * 2 + d % 2) for d in range(dp_count)])

    own_place = place_of(0, 0)
    states = [tiles(v) for v in (moment_one, moment_two, master)]
    front, back = lax.ppermute(own, "tensor", ahead), lax.ppermute(own, "tensor", behind)
    def chunks_of(hop):
        return [tensor_count - hop, hop] if hop < tensor_count // 2 else [hop]

    total, held_grad, ids = load(plan, residual[0], token_grad, own, chosen, chunks_of(1))
    for hop in range(1, tensor_count // 2):
        chunks = [front, back]
        if hop == tensor_count // 2 - 1:
            front, back = front[: tokens // 2], back[tokens // 2 :]
        front, back = lax.ppermute(front, "tensor", ahead), lax.ppermute(back, "tensor", behind)
        side, sources = None, ()
        if hop == tensor_count // 2 - 1:
            side, sources = "pick", [*helds, ids_of(ids, own_place)]
        elif hop == 1:
            side, sources = "states", states
        elif hop == 2:
            side, sources = "params", [tiles(params)]
        total, held_grad, *fetched = accumulate(
            plan, total, chunks, chunks_of(hop), held_grad, token_grad, chunks_of(hop + 1), side, sources
        )
        if side == "states":
            helds = fetched
        if side == "params":
            (wide,) = fetched
        if side == "pick":
            picked = fetched
    total = tiles(last(plan, total, front, back, tensor_count // 2, held_grad))

    received, sums = [], []
    for k in range(1, chips):
        other = swap(pack(ids, total, place_of(k, 1), jnp.bfloat16))
        mine = pack(ids, total, place_of(k, 0), jnp.float32)
        sums.append((mine + other.astype(jnp.float32)).astype(jnp.bfloat16))
        received.append(send(sums[-1], k))
    other = pack(ids, total, place_of(0, 1), jnp.bfloat16, sums)
    received.append(swap(other))
    total, mine = close(ids, total, own_place, range(1, dp_count), [*sums, other])
    for part in received:
        mine = mine + part.astype(jnp.float32)
    mean_grad = mine / dp_count

    one, two, weights = picked
    one = beta_one * one + (1.0 - beta_one) * mean_grad
    two = beta_two * two + (1.0 - beta_two) * mean_grad * mean_grad
    weights = weights - learn_rate * (one / (jnp.sqrt(two) + epsilon) + decay_rate * weights)
    rounded = weights.astype(jnp.bfloat16)

    far = [send(rounded, k) for k in range(1, chips)]
    near = swap(rounded)
    new_residual, fresh, wide, out = store(
        ids, total, helds, [one, two, weights], wide, rounded, own_place
    )
    for k in range(1, chips):
        direct = relay(far[k - 1], out)
        across = swap(direct)
        updates, places = [direct], [place_of(chips - k, 0)]
        if k == 1:
            updates, places = [near, *updates], [place_of(0, 1), *places]
        wide, out = spread(ids, wide, out, updates, places)
        wide, out = spread(ids, wide, out, [across], [place_of(chips - k, 1)])

    new_one, new_two, new_master = (untiles(v, owner_rows, column_count) for v in fresh)
    return (
        untiles(new_residual, row_count, column_count)[None],
        new_one,
        new_two,
        new_master,
        untiles(out, row_count, column_count),
    )


def solution(mesh):
    dp_count, tensor_count = mesh.shape["dp"], mesh.shape["tensor"]
    body = functools.partial(local, plan_table(dp_count, tensor_count), ring_order(tensor_count))
    in_specs = (
        P("dp", "tensor", None),
        P("dp", None, "tensor"),
        P("dp", None, "tensor"),
        P(None, "tensor", None),
        P("dp", "tensor"),
        P("dp", "tensor"),
        P("dp", "tensor"),
        P(None, "tensor"),
    )
    out_specs = (
        P("dp", None, "tensor"),
        P("dp", "tensor"),
        P("dp", "tensor"),
        P("dp", "tensor"),
        P(None, "tensor"),
    )
    return jax.shard_map(body, mesh=mesh, in_specs=in_specs, out_specs=out_specs, check_vma=False)
```

time: 256 us -> 65.3 us (0.26)
  local copies, waits for them, and re-layouts: 135 us -> 0.71 us
  Pallas kernels: 0 us -> 47.1 us
  waiting for transfers between devices: 48.2 us -> 2.78 us
  other arithmetic: 37.9 us -> 0.48 us
  matrix products: 14.7 us -> 0 us
  between operations: 14.2 us -> 0.81 us
  starting transfers between devices: 4.46 us -> 13.2 us
    gather x4 -> x0, local copies, waits for them, and re-layouts: 69.5 us -> none  [the longest x1 61.4 us: local(): packed = jnp.take_along_axis(blocks, span_ids[:, :, None], axis=1)]
    pallas_call x0 -> x13, Pallas kernels: none -> 47.1 us  [call(): pl.pallas_call(body, out_shape=[pltpu.VMEM(shape, kind) if held else jax....]
    all_gather x2 -> x0, waiting for transfers between devices: 39.8 us -> none  [the longest x1 39.8 us: local(): lax.all_gather(activations, 'tensor', axis=1, tiled=True)[0]]
    reshape x9 -> x0, local copies, waits for them, and re-layouts: 27.1 us -> none  [the longest x8 18.8 us: replace(): values.reshape(per_owner, 128).at[own_ids].set(update).reshape(values.shape)]
    scatter x3 -> x0, other arithmetic: 21.9 us -> none  [replace(): values.reshape(per_owner, 128).at[own_ids].set(update).reshape(values.shape)]
    unnamed x12 -> x0, local copies, waits for them, and re-layouts: 17.8 us -> none
    dot_general x1 -> x0, matrix products: 14.7 us -> none  [local(): lax.dot_general(lax.all_gather(activations, 'tensor', axis=1, tiled=True)...]
    ppermute x0 -> x14, starting transfers between devices: none -> 13.2 us  [the longest x3 4.95 us: local(): lax.ppermute(front, 'tensor', ahead)]
  transfers between devices with their start and end apart: 3 -> 14, of which waited for: 2 -> 3; matrix products, arithmetic and copies ran while one was open for 33% -> 1% of each run, Pallas kernels for 0% -> 60%
where the time goes in v2:
time: 65.3 us; the launch traced here: 65.2 us
  Pallas kernels  47.1 us (72%)
  starting transfers between devices  13.2 us (20%)
  waiting for transfers between devices  2.78 us (4%)
  between operations  0.81 us (1%)
  local copies, waits for them, and re-layouts  0.71 us (1%)
    pallas_call x13, Pallas kernels, call(): pl.pallas_call(body, out_shape=[pltpu.VMEM(shape, kind) if held else jax....  47.1 us
    ppermute x3, starting transfers between devices, local(): lax.ppermute(front, 'tensor', ahead)  4.95 us
    ppermute x1, starting transfers between devices, local(): lax.ppermute(own, 'tensor', ahead)  3.02 us
    ppermute x2, starting transfers between devices, send(): lax.ppermute(values, 'dp', [(d, (d // 2 + k) % chips * 2 + d % 2) for d i...  2.66 us
    ppermute x3, waiting for transfers between devices, local(): lax.ppermute(front, 'tensor', ahead)  1.99 us
  transfers between devices with their start and end apart: 14, of which 3 were waited for; matrix products, arithmetic and copies ran while one was open for 1% of the time, Pallas kernels for 60%

profile of v2, /device:TPU:0, one launch (start us, length us, event | category | flops | bytes accessed | tf_op | source)
XLA Modules:
  0.0 65.2 jit_solution(13215731047896462879)
XLA Ops:
  0.6 3.0 %collective-permute-start = (bf16[256,512]{1,0:T(8,128)(2,1)}, bf16[256,512]{1,0:T(8,128)(2,1)S(1)}, u32[]{:S(2)}, u32[]{:S(2)}) collective-permute-start(bf16[256,512]{1,0:T(8,128)(2,1)} %bitcast.73), channel_id=1, source_target_pairs={{1,3},{3,5},{5,7},{7,6},{6,4},{4,2},{2,0},{0,1},{9,11},{11,13},{13... | collective-permute-start | bytes 786440 | tf_op jit(solution)/shard_map/ppermute | solution.py:474
  3.8 0.7 %dynamic-slice_bitcast_fusion.plan_ref = s32[12]{0:T(128)S(1)} fusion(s32[4,8,12]{2,1,0:T(8,128)} %constant.34.clone, s32[]{:T(128)S(6)} %select_n.6, s32[]{:T(128)S(6)} %select_n.7), kind=kLoop, calls=%fused_computation.5 | loop fusion | bytes 104 | tf_op jit(solution)/shard_map/squeeze | solution.py:459
  4.5 6.4 %load.1 = (f32[512,3584]{1,0:T(8,128)S(1)}, bf16[2048,3584]{1,0:T(8,128)(2,1)S(1)}, s32[4,1,1024]{2,1,0:T(1,128)S(1)}) custom-call(s32[12]{0:T(128)S(1)} %dynamic-slice_bitcast_fusion.plan_ref, f32[512,3584]{1,0:T(8,128)} %bitcast.64, bf16[2048,3584]{1,0:T(8,128)(2,1)} %bitcast.60, bf16[256,512]{1,0:T(8,128)(2,1)} %bitcast.75, s32[4,1,896]{2,1,0:T(1,128)} %spans_ref.1), custom_call_target="tpu_custom_call" | custom-call | flops 11274289152 | bytes 44040192 | tf_op jit(solution)/shard_map/load/pallas_call | solution.py:134
  10.9 2.0 %collective-permute-start.2 = (bf16[256,512]{1,0:T(8,128)(2,1)S(1)}, bf16[256,512]{1,0:T(8,128)(2,1)S(1)}, u32[]{:S(2)}, u32[]{:S(2)}) collective-permute-start(bf16[256,512]{1,0:T(8,128)(2,1)S(1)} %collective-permute-done.refs_0_), channel_id=1, source_target_pairs={{1,3},{3,5},{5,7},{7,6},{6,4},{4,2},{2,0},{0,1},{9,11},{11,13},{13... | collective-permute-start | bytes 786440 | tf_op jit(solution)/shard_map/ppermute | solution.py:483
  13.0 4.3 %accumulate.3 = (f32[512,3584]{1,0:T(8,128)S(1)}, bf16[2048,3584]{1,0:T(8,128)(2,1)S(1)}, f32[3584,128]{1,0:T(8,128)S(1)}, f32[3584,128]{1,0:T(8,128)S(1)}, f32[3584,128]{1,0:T(8,128)S(1)}) custom-call(s32[12]{0:T(128)S(1)} %dynamic-slice_bitcast_fusion.plan_ref, ...), custom_call_target="tpu_custom_call", output_to_operand_aliasing={{0}: (1, {}), {1}: (2, {})} | custom-call | flops 22548578304 | bytes 44040192 | tf_op jit(solution)/shard_map/accumulate/pallas_call | solution.py:134
  17.2 1.5 %collective-permute-done.2.refs_0_ = bf16[256,512]{1,0:T(8,128)(2,1)S(1)} collective-permute-done((bf16[256,512]{1,0:T(8,128)(2,1)S(1)}, bf16[256,512]{1,0:T(8,128)(2,1)S(1)}, u32[]{:S(2)}, u32[]{:S(2)}) %collective-permute-start.2) | collective-permute-done | bytes 262176 | tf_op jit(solution)/shard_map/ppermute | solution.py:483
  18.7 1.6 %collective-permute-start.4 = (bf16[256,512]{1,0:T(8,128)(2,1)S(1)}, bf16[256,512]{1,0:T(8,128)(2,1)S(1)}, u32[]{:S(2)}, u32[]{:S(2)}) collective-permute-start(bf16[256,512]{1,0:T(8,128)(2,1)S(1)} %collective-permute-done.2.refs_0_), channel_id=1, source_target_pairs={{1,3},{3,5},{5,7},{7,6},{6,4},{4,2},{2,0},{0,1},{9,11},{11,13},{13... | collective-permute-start | bytes 786440 | tf_op jit(solution)/shard_map/ppermute | solution.py:483
  20.7 4.3 %accumulate.4 = (f32[512,3584]{1,0:T(8,128)S(1)}, bf16[2048,3584]{1,0:T(8,128)(2,1)S(1)}, f32[14336,128]{1,0:T(8,128)S(1)}) custom-call(s32[12]{0:T(128)S(1)} %dynamic-slice_bitcast_fusion.plan_ref, f32[512,3584]{1,0:T(8,128)S(1)} %get-tuple-element.35.total_in, ...), custom_call_target="tpu_custom_call", output_to_operand_aliasing={{0}: (1, {}), {1}: (2, {})} | custom-call | flops 22548578304 | bytes 44040192 | tf_op jit(solution)/shard_map/accumulate/pallas_call | solution.py:134
  25.6 1.4 %collective-permute-start.6 = (bf16[128,512]{1,0:T(8,128)(2,1)S(1)}, bf16[128,512]{1,0:T(8,128)(2,1)S(1)}, u32[]{:S(2)}, u32[]{:S(2)}) collective-permute-start(bf16[128,512]{1,0:T(8,128)(2,1)S(1)} %slice.8), channel_id=1, source_target_pairs={{1,3},{3,5},{5,7},{7,6},{6,4},{4,2},{2,0},{0,1},{9,11},{11,13},{13... | collective-permute-start | bytes 393224 | tf_op jit(solution)/shard_map/ppermute | solution.py:483
  27.0 0.8 %collective-permute-start.7 = (bf16[128,512]{1,0:T(8,128)(2,1)S(1)}, bf16[128,512]{1,0:T(8,128)(2,1)S(1)}, u32[]{:S(2)}, u32[]{:S(2)}) collective-permute-start(bf16[128,512]{1,0:T(8,128)(2,1)S(1)} %slice.9), channel_id=1, source_target_pairs={{3,1},{5,3},{7,5},{6,7},{4,6},{2,4},{0,2},{1,0},{11,9},{13,11},{15... | collective-permute-start | bytes 393224 | tf_op jit(solution)/shard_map/ppermute | solution.py:483
  27.7 6.7 %accumulate.5 = (f32[512,3584]{1,0:T(8,128)S(1)}, bf16[2048,3584]{1,0:T(8,128)(2,1)S(1)}, f32[896,128]{1,0:T(8,128)S(1)}, f32[896,128]{1,0:T(8,128)S(1)}, f32[896,128]{1,0:T(8,128)S(1)}) custom-call(s32[12]{0:T(128)S(1)} %dynamic-slice_bitcast_fusion.plan_ref, ...), custom_call_target="tpu_custom_call", output_to_operand_aliasing={{0}: (1, {}), {1}: (2, {})} | custom-call | flops 22548578304 | bytes 44040192 | tf_op jit(solution)/shard_map/accumulate/pallas_call | solution.py:134
  34.5 2.5 %last.1 = f32[512,3584]{1,0:T(8,128)S(1)} custom-call(s32[12]{0:T(128)S(1)} %dynamic-slice_bitcast_fusion.plan_ref, f32[512,3584]{1,0:T(8,128)S(1)} %get-tuple-element.42.total_in, bf16[2048,3584]{1,0:T(8,128)(2,1)S(1)} %get-tuple-element.43.grad_ref, bf16[128,512]{1,0:T(8,128)(2,1)S(1)} %collective-permute-done.6.front_ref, ...), custom_call_target="tpu_custom_call", output_to_operand_aliasing={{}: (1, {})} | custom-call | flops 939524096 | bytes 14680064 | tf_op jit(solution)/shard_map/last/pallas_call | solution.py:134
  37.0 1.6 %pack.4 = bf16[896,128]{1,0:T(8,128)(2,1)S(1)} custom-call(s32[4,1,1024]{2,1,0:T(1,128)S(1)} %get-tuple-element.32.refs_5_.ids_ref.own_ids.refs_0_.refs_1_.refs_2_, f32[14336,128]{1,0:T(8,128)S(1)} %bitcast.55), custom_call_target="tpu_custom_call" | custom-call | bytes 4587520 | tf_op jit(solution)/shard_map/pack/pallas_call | solution.py:134
  38.6 1.5 %pack.3 = f32[896,128]{1,0:T(8,128)S(1)} custom-call(s32[4,1,1024]{2,1,0:T(1,128)S(1)} %get-tuple-element.32.refs_5_.ids_ref.own_ids.refs_0_.refs_1_.refs_2_, f32[14336,128]{1,0:T(8,128)S(1)} %bitcast.56), custom_call_target="tpu_custom_call" | custom-call | bytes 4587520 | tf_op jit(solution)/shard_map/pack/pallas_call | solution.py:134
  40.2 1.6 %pack.5.refs_5_ = bf16[896,128]{1,0:T(8,128)(2,1)S(1)} custom-call(s32[4,1,1024]{2,1,0:T(1,128)S(1)} %get-tuple-element.32.refs_5_.ids_ref.own_ids.refs_0_.refs_1_.refs_2_, f32[14336,128]{1,0:T(8,128)S(1)} %bitcast.57, bf16[896,128]{1,0:T(8,128)(2,1)S(1)} %add_convert_fusion.refs_0_.refs_4_), custom_call_target="tpu_custom_call" | custom-call | bytes 4587520 | tf_op jit(solution)/shard_map/pack/pallas_call | solution.py:134
  41.8 0.6 collective-permute-start.10
  42.4 1.3 %collective-permute-start.9 = (bf16[896,128]{1,0:T(8,128)(2,1)S(1)}, bf16[896,128]{1,0:T(8,128)(2,1)S(1)}, u32[]{:S(2)}, u32[]{:S(2)}) collective-permute-start(bf16[896,128]{1,0:T(8,128)(2,1)S(1)} %add_convert_fusion.refs_0_.refs_4_), channel_id=1, source_target_pairs={{0,16},{8,24},{16,0},{24,8},{1,17},{9,25},{17,1},{25,9},{2,18},{10... | collective-permute-start | bytes 688136 | tf_op jit(solution)/shard_map/ppermute | solution.py:470
  43.7 5.5 %close.1 = (f32[14336,128]{1,0:T(8,128)S(1)}, f32[896,128]{1,0:T(8,128)S(1)}) custom-call(s32[4,1,1024]{2,1,0:T(1,128)S(1)} %get-tuple-element.32.refs_5_.ids_ref.own_ids.refs_0_.refs_1_.refs_2_, s32[4,1,1024]{2,1,0:T(1,128)S(1)} %get-tuple-element.32.refs_5_.ids_ref.own_ids.refs_0_.refs_1_.refs_2_, ...), custom_call_target="tpu_custom_call", output_to_operand_aliasing={{0}: (4, {})} | custom-call | bytes 44040192 | tf_op jit(solution)/shard_map/close/pallas_call | solution.py:134
  49.2 0.8 %collective-permute-done.9 = bf16[896,128]{1,0:T(8,128)(2,1)S(1)} collective-permute-done((bf16[896,128]{1,0:T(8,128)(2,1)S(1)}, bf16[896,128]{1,0:T(8,128)(2,1)S(1)}, u32[]{:S(2)}, u32[]{:S(2)}) %collective-permute-start.9) | collective-permute-done | bytes 229408 | tf_op jit(solution)/shard_map/ppermute | solution.py:470
  50.4 1.4 %collective-permute-start.12 = (bf16[896,128]{1,0:T(8,128)(2,1)S(1)}, bf16[896,128]{1,0:T(8,128)(2,1)S(1)}, u32[]{:S(2)}, u32[]{:S(2)}) collective-permute-start(bf16[896,128]{1,0:T(8,128)(2,1)S(1)} %get-tuple-element.59.refs_7_), channel_id=1, source_target_pairs={{0,16},{8,24},{16,0},{24,8},{1,17},{9,25},{17,1},{25,9},{2,18},{10... | collective-permute-start | bytes 688136 | tf_op jit(solution)/shard_map/ppermute | solution.py:470
  51.8 6.4 %store.1 = (f32[3584,128]{1,0:T(8,128)S(1)}, f32[3584,128]{1,0:T(8,128)S(1)}, f32[3584,128]{1,0:T(8,128)S(1)}, f32[14336,128]{1,0:T(8,128)S(1)}, f32[14336,128]{...) custom-call(s32[4,1,1024]{2,1,0:T(1,128)S(1)} %get-tuple-element.32., ...), custom_call_target="tpu_custom_call", output_to_operand_aliasing={{0}: (2, {}), {1}: (3, {}), {2}: (4, {}), {3}: (8, {})} | custom-call | bytes 44040192 | tf_op jit(solution)/shard_map/store/pallas_call | solution.py:134
  58.1 0.6 collective-permute-start.13
  58.7 3.8 %spread.2 = (f32[14336,128]{1,0:T(8,128)S(1)}, bf16[14336,128]{1,0:T(8,128)(2,1)}) custom-call(s32[4,1,1024]{2,1,0:T(1,128)S(1)} %get-tuple-element.32.refs_5_.ids_ref.own_ids.refs_0_.refs_1_.refs_2_, s32[4,1,1024]{2,1,0:T(1,128)S(1)} %get-tuple-element.32.refs_5_.ids_ref.own_ids.refs_0_.refs_1_.refs_2_, ...), custom_call_target="tpu_custom_call", output_to_operand_aliasing={{0}: (2, {}), {1}: (5, {})} | custom-call | bytes 44040192 | tf_op jit(solution)/shard_map/spread/pallas_call | solution.py:134
  62.5 2.6 %spread.3 = (f32[14336,128]{1,0:T(8,128)S(1)}, bf16[14336,128]{1,0:T(8,128)(2,1)}) custom-call(s32[4,1,1024]{2,1,0:T(1,128)S(1)} %get-tuple-element.32.refs_5_.ids_ref.own_ids.refs_0_.refs_1_.refs_2_, f32[14336,128]{1,0:T(8,128)S(1)} %get-tuple-element.56.refs_1_, ...), custom_call_target="tpu_custom_call", output_to_operand_aliasing={{0}: (1, {}), {1}: (3, {})} | custom-call | bytes 44040192 | tf_op jit(solution)/shard_map/spread/pallas_call | solution.py:134
  (22 shorter events, 1.8 us)
Async XLA Ops:
  0.6 10.2 %collective-permute-start = (bf16[256,512]{1,0:T(8,128)(2,1)}, bf16[256,512]{1,0:T(8,128)(2,1)S(1)}, u32[]{:S(2)}, u32[]{:S(2)}) collective-permute-start(bf16[256,512]{1,0:T(8,128)(2,1)} %bitcast.73), channel_id=1, source_target_pairs={{1,3},{3,5},{5,7},{7,6},{6,4},{4,2},{2,0},{0,1},{9,11},{11,13},{13... | collective-permute-start | bytes 786440 | tf_op jit(solution)/shard_map/ppermute | solution.py:474
  3.6 9.2 %collective-permute-start.1 = (bf16[256,512]{1,0:T(8,128)(2,1)}, bf16[256,512]{1,0:T(8,128)(2,1)S(1)}, u32[]{:S(2)}, u32[]{:S(2)}) collective-permute-start(bf16[256,512]{1,0:T(8,128)(2,1)} %bitcast.74), channel_id=1, source_target_pairs={{3,1},{5,3},{7,5},{6,7},{4,6},{2,4},{0,2},{1,0},{11,9},{13,11},{15... | collective-permute-start | bytes 786440 | tf_op jit(solution)/shard_map/ppermute | solution.py:474
  10.9 7.8 %collective-permute-start.2 = (bf16[256,512]{1,0:T(8,128)(2,1)S(1)}, bf16[256,512]{1,0:T(8,128)(2,1)S(1)}, u32[]{:S(2)}, u32[]{:S(2)}) collective-permute-start(bf16[256,512]{1,0:T(8,128)(2,1)S(1)} %collective-permute-done.refs_0_), channel_id=1, source_target_pairs={{1,3},{3,5},{5,7},{7,6},{6,4},{4,2},{2,0},{0,1},{9,11},{11,13},{13... | collective-permute-start | bytes 786440 | tf_op jit(solution)/shard_map/ppermute | solution.py:483
  12.8 7.5 %collective-permute-start.3 = (bf16[256,512]{1,0:T(8,128)(2,1)S(1)}, bf16[256,512]{1,0:T(8,128)(2,1)S(1)}, u32[]{:S(2)}, u32[]{:S(2)}) collective-permute-start(bf16[256,512]{1,0:T(8,128)(2,1)S(1)} %collective-permute-done.1.refs_1_), channel_id=1, source_target_pairs={{3,1},{5,3},{7,5},{6,7},{4,6},{2,4},{0,2},{1,0},{11,9},{13,11},{15... | collective-permute-start | bytes 786440 | tf_op jit(solution)/shard_map/ppermute | solution.py:483
  18.7 6.9 %collective-permute-start.4 = (bf16[256,512]{1,0:T(8,128)(2,1)S(1)}, bf16[256,512]{1,0:T(8,128)(2,1)S(1)}, u32[]{:S(2)}, u32[]{:S(2)}) collective-permute-start(bf16[256,512]{1,0:T(8,128)(2,1)S(1)} %collective-permute-done.2.refs_0_), channel_id=1, source_target_pairs={{1,3},{3,5},{5,7},{7,6},{6,4},{4,2},{2,0},{0,1},{9,11},{11,13},{13... | collective-permute-start | bytes 786440 | tf_op jit(solution)/shard_map/ppermute | solution.py:483
  20.3 6.6 %collective-permute-start.5 = (bf16[256,512]{1,0:T(8,128)(2,1)S(1)}, bf16[256,512]{1,0:T(8,128)(2,1)S(1)}, u32[]{:S(2)}, u32[]{:S(2)}) collective-permute-start(bf16[256,512]{1,0:T(8,128)(2,1)S(1)} %collective-permute-done.3.refs_1_), channel_id=1, source_target_pairs={{3,1},{5,3},{7,5},{6,7},{4,6},{2,4},{0,2},{1,0},{11,9},{13,11},{15... | collective-permute-start | bytes 786440 | tf_op jit(solution)/shard_map/ppermute | solution.py:483
  25.6 8.9 %collective-permute-start.6 = (bf16[128,512]{1,0:T(8,128)(2,1)S(1)}, bf16[128,512]{1,0:T(8,128)(2,1)S(1)}, u32[]{:S(2)}, u32[]{:S(2)}) collective-permute-start(bf16[128,512]{1,0:T(8,128)(2,1)S(1)} %slice.8), channel_id=1, source_target_pairs={{1,3},{3,5},{5,7},{7,6},{6,4},{4,2},{2,0},{0,1},{9,11},{11,13},{13... | collective-permute-start | bytes 393224 | tf_op jit(solution)/shard_map/ppermute | solution.py:483
  27.0 7.5 %collective-permute-start.7 = (bf16[128,512]{1,0:T(8,128)(2,1)S(1)}, bf16[128,512]{1,0:T(8,128)(2,1)S(1)}, u32[]{:S(2)}, u32[]{:S(2)}) collective-permute-start(bf16[128,512]{1,0:T(8,128)(2,1)S(1)} %slice.9), channel_id=1, source_target_pairs={{3,1},{5,3},{7,5},{6,7},{4,6},{2,4},{0,2},{1,0},{11,9},{13,11},{15... | collective-permute-start | bytes 393224 | tf_op jit(solution)/shard_map/ppermute | solution.py:483
  38.5 1.6 %collective-permute-start.8 = (bf16[896,128]{1,0:T(8,128)(2,1)S(1)}, bf16[896,128]{1,0:T(8,128)(2,1)S(1)}, u32[]{:S(2)}, u32[]{:S(2)}) collective-permute-start(bf16[896,128]{1,0:T(8,128)(2,1)S(1)} %pack.4), channel_id=1, source_target_pairs={{0,8},{8,0},{16,24},{24,16},{1,9},{9,1},{17,25},{25,17},{2,10},{10... | collective-permute-start | bytes 688136 | tf_op jit(solution)/shard_map/ppermute | solution.py:467
  41.8 7.4 %collective-permute-start.10 = (bf16[896,128]{1,0:T(8,128)(2,1)S(1)}, bf16[896,128]{1,0:T(8,128)(2,1)S(1)}, u32[]{:S(2)}, u32[]{:S(2)}) collective-permute-start(bf16[896,128]{1,0:T(8,128)(2,1)S(1)} %pack.5.refs_5_), channel_id=1, source_target_pairs={{0,8},{8,0},{16,24},{24,16},{1,9},{9,1},{17,25},{25,17},{2,10},{10... | collective-permute-start | bytes 688136 | tf_op jit(solution)/shard_map/ppermute | solution.py:467
  42.4 7.6 %collective-permute-start.9 = (bf16[896,128]{1,0:T(8,128)(2,1)S(1)}, bf16[896,128]{1,0:T(8,128)(2,1)S(1)}, u32[]{:S(2)}, u32[]{:S(2)}) collective-permute-start(bf16[896,128]{1,0:T(8,128)(2,1)S(1)} %add_convert_fusion.refs_0_.refs_4_), channel_id=1, source_target_pairs={{0,16},{8,24},{16,0},{24,8},{1,17},{9,25},{17,1},{25,9},{2,18},{10... | collective-permute-start | bytes 688136 | tf_op jit(solution)/shard_map/ppermute | solution.py:470
  50.4 7.7 %collective-permute-start.12 = (bf16[896,128]{1,0:T(8,128)(2,1)S(1)}, bf16[896,128]{1,0:T(8,128)(2,1)S(1)}, u32[]{:S(2)}, u32[]{:S(2)}) collective-permute-start(bf16[896,128]{1,0:T(8,128)(2,1)S(1)} %get-tuple-element.59.refs_7_), channel_id=1, source_target_pairs={{0,16},{8,24},{16,0},{24,8},{1,17},{9,25},{17,1},{25,9},{2,18},{10... | collective-permute-start | bytes 688136 | tf_op jit(solution)/shard_map/ppermute | solution.py:470
  51.8 7.0 %collective-permute-start.11 = (bf16[896,128]{1,0:T(8,128)(2,1)S(1)}, bf16[896,128]{1,0:T(8,128)(2,1)S(1)}, u32[]{:S(2)}, u32[]{:S(2)}) collective-permute-start(bf16[896,128]{1,0:T(8,128)(2,1)S(1)} %get-tuple-element.59.refs_7_), channel_id=1, source_target_pairs={{0,8},{8,0},{16,24},{24,16},{1,9},{9,1},{17,25},{25,17},{2,10},{10... | collective-permute-start | bytes 688136 | tf_op jit(solution)/shard_map/ppermute | solution.py:467
  58.1 4.4 %collective-permute-start.13 = (bf16[896,128]{1,0:T(8,128)(2,1)S(1)}, bf16[896,128]{1,0:T(8,128)(2,1)S(1)}, u32[]{:S(2)}, u32[]{:S(2)}) collective-permute-start(bf16[896,128]{1,0:T(8,128)(2,1)S(1)} %relay.1.refs_4_), channel_id=1, source_target_pairs={{0,8},{8,0},{16,24},{24,16},{1,9},{9,1},{17,25},{25,17},{2,10},{10... | collective-permute-start | bytes 688136 | tf_op jit(solution)/shard_map/ppermute | solution.py:467

commit v3 on v2

--- a/solution.py
+++ b/solution.py
@@ -14,7 +14,7 @@
 epsilon = 1e-08
 LANES = 128
 SUBLANES = 8
-UNROLL = 16
+UNROLL = 32
 
 
 def ring_order(count):
@@ -55,8 +55,9 @@
 HELD = pl.BlockSpec(memory_space=VMEM)
 AWAY = pl.BlockSpec(memory_space=pl.ANY)
 DMA = pltpu.SemaphoreType.DMA
-WIDTH = 896
+WIDTH = 1792
 WEIGHT = 24
+PARTS = 4
 
 
 def each_group(count, body):
@@ -93,7 +94,7 @@
     return lax.dot_general(a, b, (((0,), (0,)), ((), ())), preferred_element_type=jnp.float32)
 
 
-def add_products(total_in, total_out, grad_ref, terms):
+def add_products(total_in, total_out, grad_ref, terms, beside=None):
     columns = grad_ref.shape[1]
     width = WIDTH if columns % WIDTH == 0 else LANES
 
@@ -103,6 +104,8 @@
         for chunk, start in terms:
             total = total + product(chunk[...], grad_ref[pl.ds(start, chunk.shape[0]), at])
         total_out[:, at] = total
+        if beside is not None:
+            beside(i, columns // width)
         return carry
 
     lax.fori_loop(0, columns // width, step, 0)
@@ -145,7 +148,7 @@
         ),
         input_output_aliases={len(scalars) + k: v for k, v in (aliases or {}).items()},
         cost_estimate=pl.CostEstimate(flops=flops, bytes_accessed=traffic, transcendentals=0),
-        compiler_params=pltpu.CompilerParams(vmem_limit_bytes=6 << 20),
+        compiler_params=pltpu.CompilerParams(vmem_limit_bytes=14 << 20),
         name=name,
     )(*scalars, *(values for values, _ in operands))
 
@@ -154,16 +157,11 @@
     return lambda i: ids_ref[0, i]
 
 
-def look_from(ids_ref, per_owner, count):
-    begin = ids_ref[0, count] * per_owner
-    return lambda i: ids_ref[0, i] - begin
-
-
 def ids_of(ids, place):
     return ids, pl.BlockSpec((None, *ids.shape[1:]), lambda i, *_: (place, 0, 0), memory_space=pltpu.SMEM)
 
 
-def order_ids(plan_ref, spans_ref, ids_ref, columns, rows):
+def order_ids(plan_ref, spans_ref, ids_ref, own_ids_ref, columns, rows):
     dp_count, _, count = spans_ref.shape
     blocks = columns // LANES
     per_owner = rows // dp_count * blocks
@@ -175,39 +173,46 @@
         row = lax.shift_right_logical(spans * factor, 18)
         column = spans - row * blocks
         tile = lax.shift_right_logical(row, 3) * blocks + column
-        ids_ref[p, :, :count] = tile * SUBLANES + (row & 7) + owner * per_owner
+        place = tile * SUBLANES + (row & 7)
+        ids_ref[p, :, :count] = place + owner * per_owner
+        if p == 0:
+            own_ids_ref[0] = place
         ids_ref[p, :, count:] = jnp.full((1, LANES), 1, jnp.int32) * owner
+
+
+def slot_of(place, tensor_count):
+    if place in (0, tensor_count // 2):
+        return 0 if place == 0 else tensor_count - 1
+    return 2 * place if place < tensor_count // 2 else 2 * (tensor_count - place) - 1
 
 
 def grad_copies(plan_ref, places, tokens, grad_ref, held_ref, sems, first=0):
     half, copies = tokens // 2, []
     for n, j in enumerate(places):
+        slot = slot_of(j, held_ref.shape[0] // tokens)
         for k in range(2):
             at = pl.ds(pl.multiple_of(plan_ref[j] * tokens + k * half, half), half)
-            copies.append(pltpu.make_async_copy(grad_ref.at[at], held_ref.at[at], sems.at[first + 2 * n + k]))
+            to = pl.ds(slot * tokens + k * half, half)
+            copies.append(pltpu.make_async_copy(grad_ref.at[at], held_ref.at[to], sems.at[first + 2 * n + k]))
     return copies
 
 
-def load_body(
-    places, plan_ref, residual_ref, grad_ref, own_ref, spans_ref, total_ref, held_ref, ids_ref, own_held, spans_held, sems, own_sems
-):
+def load_body(places, plan_ref, residual_ref, grad_ref, own_ref, spans_ref, *refs):
+    total_ref, held_ref, own_held, ids_ref, own_ids_ref, spans_held, sems, own_sems = refs
     tokens = own_ref.shape[0]
     spans_copy = pltpu.make_async_copy(spans_ref, spans_held, own_sems.at[1])
     spans_copy.start()
-    first = [pltpu.make_async_copy(own_ref, own_held, own_sems.at[0])]
-    first += grad_copies(plan_ref, [0], tokens, grad_ref, held_ref, sems, 8)
-    first += split_copies(residual_ref, total_ref, 8, sems)
-    later = grad_copies(plan_ref, places, tokens, grad_ref, held_ref, sems, 10)
-    start_all(first)
+    copies = [pltpu.make_async_copy(own_ref, own_held, own_sems.at[0])]
+    copies += split_copies(residual_ref, total_ref, 8, sems)
+    copies += grad_copies(plan_ref, places, tokens, grad_ref, held_ref, sems, 8)
+    start_all(copies)
     spans_copy.wait()
-    order_ids(plan_ref, spans_held, ids_ref, total_ref.shape[1], total_ref.shape[0])
-    wait_all(first)
-    start_all(later)
-    add_products(total_ref, total_ref, held_ref, [(own_held, pl.multiple_of(plan_ref[0] * tokens, tokens))])
-    wait_all(later)
+    order_ids(plan_ref, spans_held, ids_ref, own_ids_ref, total_ref.shape[1], total_ref.shape[0])
+    wait_all(copies)
 
 
 def load(plan, residual, token_grad, own, spans, places):
+    dp_count, _, count = spans.shape
     return call(
         functools.partial(load_body, places),
         "load",
@@ -216,14 +221,11 @@
         [
             (residual.shape, jnp.float32, True),
             (token_grad.shape, token_grad.dtype, True),
-            ((*spans.shape[:2], spans.shape[2] + LANES), jnp.int32, True),
+            (own.shape, own.dtype, True),
+            ((dp_count, 1, count + LANES), jnp.int32, True),
+            ((1, 1, count), jnp.int32, True),
         ],
-        [
-            pltpu.VMEM(own.shape, own.dtype),
-            pltpu.VMEM(spans.shape, jnp.int32),
-            DMA((10 + 2 * len(places),)),
-            DMA((2,)),
-        ],
+        [pltpu.VMEM(spans.shape, jnp.int32), DMA((8 + 2 * len(places),)), DMA((2,))],
         flops=WEIGHT * own.size * residual.shape[1],
         traffic=WEIGHT * residual.size,
     )
@@ -231,7 +233,7 @@
 
 def accumulate_body(places, coming, tokens, side, plan_ref, total_in, held_in, grad_ref, *refs):
     chunks, refs = refs[: len(places)], refs[len(places) :]
-    starts = [pl.multiple_of(plan_ref[j] * tokens, tokens) for j in places]
+    starts = [slot_of(j, held_in.shape[0] // tokens) * tokens for j in places]
     extra = {"states": 3, "params": 1, "pick": 4}.get(side, 0)
     sources, (total_out, held_ref), refs = refs[:extra], refs[extra : extra + 2], refs[extra + 2 :]
     sems = refs[-1]
@@ -243,11 +245,21 @@
         wide_ref, narrow_ref = refs[:2]
         copies += split_copies(sources[0], narrow_ref, 4, sems)
     start_all(copies)
-    add_products(total_in, total_out, held_ref, list(zip(chunks, starts)))
+    beside = None
+    if side == "pick":
+
+        def beside(i, steps):
+            share = refs[0].shape[0] // steps
+            for first in range(0, share, UNROLL):
+                rows = [i * share + first + k for k in range(UNROLL)]
+                at = [sources[3][0, row] for row in rows]
+                for source, target in zip(sources[:3], refs[:3]):
+                    values = [source[pl.ds(a, 1), :] for a in at]
+                    for row, value in zip(rows, values):
+                        target[pl.ds(row, 1), :] = value
+
+    add_products(total_in, total_out, held_ref, list(zip(chunks, starts)), beside)
     wait_all(copies)
-    if side == "pick":
-        count = refs[0].shape[0]
-        gather_rows(look_from(sources[3], sources[0].shape[0], count), count, list(zip(sources[:3], refs[:3])))
     if side == "params":
         wide_ref[...] = narrow_ref[...].astype(jnp.float32)
 
@@ -260,7 +272,7 @@
         inputs = [(away(v), False) for v in sources]
         outs += [(sources[0].shape, jnp.float32, True)] * 3
     if side == "pick":
-        count = sources[3][0].shape[2] - LANES
+        count = sources[3][0].shape[2]
         inputs = [(v, True) for v in sources[:3]] + [sources[3]]
         outs += [((count, LANES), jnp.float32, True)] * 3
     if side == "params":
@@ -280,19 +292,19 @@
     )
 
 
-def last_body(place, plan_ref, total_in, grad_ref, front_ref, back_ref, total_out, chunk_ref):
+def last_body(total_in, grad_ref, front_ref, back_ref, total_out, chunk_ref):
     half = front_ref.shape[0]
     chunk_ref[:half] = front_ref[...]
     chunk_ref[half:] = back_ref[...]
-    add_products(total_in, total_out, grad_ref, [(chunk_ref, pl.multiple_of(plan_ref[place] * 2 * half, 2 * half))])
-
-
-def last(plan, total, front, back, place, held_grad):
+    add_products(total_in, total_out, grad_ref, [(chunk_ref, grad_ref.shape[0] - 2 * half)])
+
+
+def last(total, front, back, held_grad):
     half, rows = front.shape
     return call(
-        functools.partial(last_body, place),
+        last_body,
         "last",
-        [plan],
+        [],
         [(total, True), (held_grad, True), (front, True), (back, True)],
         [(total.shape, jnp.float32, True)],
         [pltpu.VMEM((2 * half, rows), front.dtype)],
@@ -350,7 +362,7 @@
         [(total.shape, jnp.float32, True), ((ids.shape[2] - LANES, LANES), jnp.float32, True)],
         (),
         {1 + len(others): 0},
-        traffic=WEIGHT * total.size,
+        traffic=total.size // 4,
     )
 
 
@@ -359,52 +371,69 @@
     at = pl.ds(pl.multiple_of(ids_ref[0, count] * per_owner, 2 * SUBLANES), per_owner)
     rows_ref[...] = update_ref[...].astype(jnp.float32)
     scatter_rows(look_in(ids_ref), count, [(rows_ref, wide_ref)])
-    block_ref[...] = wide_ref[at, :].astype(block_ref.dtype)
-    copies = split_copies(block_ref, out_ref.at[at], 2, sems, first)
-    start_all(copies)
+    return narrow(wide_ref.at[at], block_ref, out_ref.at[at], sems, first)
+
+
+def narrow(source, block_ref, target, sems, first):
+    copies = split_copies(block_ref, target, PARTS, sems, first)
+    size = block_ref.shape[0] // PARTS
+    for k, copy in enumerate(copies):
+        block_ref[k * size : (k + 1) * size, :] = source[k * size : (k + 1) * size, :].astype(block_ref.dtype)
+        copy.start()
     return copies
 
 
-def store_body(dp_count, ids_ref, total_ref, *refs):
-    refs = refs[3:]
+def store_body(dp_count, own_ids_ref, *refs):
+    ids, total_in, refs = refs[:dp_count], refs[dp_count], refs[dp_count + 1 + 3 :]
     new, update_ref, refs = refs[:3], refs[4], refs[5:]
-    helds, wide_ref, residual_ref, outs, out_ref = refs[:3], refs[3], refs[4], refs[5:8], refs[8]
-    rows_ref, block_ref, sems = refs[9:]
+    total_ref, helds, wide_ref, residual_ref, outs, out_ref = refs[0], refs[1:4], refs[4], refs[5], refs[6:9], refs[9]
+    rows_ref, block_ref, sems = refs[10:]
     per_owner, count = block_ref.shape[0], update_ref.shape[0]
     copies = []
-    used = 0
-
-    def begin(source, target, parts):
-        nonlocal used
-        copies.extend(split_copies(source, target, parts, sems, used))
-        start_all(copies[-parts:])
-        used += parts
-
-    begin(total_ref, residual_ref, 2 * dp_count)
-    begin_at = look_from(ids_ref, per_owner, count)
-    for n in range(3):
-        scatter_rows(begin_at, count, [(new[n], helds[n])])
-        begin(helds[n], outs[n], 2)
-    copies.extend(spread_one(ids_ref, update_ref, wide_ref, out_ref, rows_ref, block_ref, sems, used))
+
+    def begin(source, target):
+        copies.extend(split_copies(source, target, 2, sems, len(copies)))
+        start_all(copies[-2:])
+
+    def block(p):
+        return pl.ds(pl.multiple_of(ids[p][0, count] * per_owner, 2 * SUBLANES), per_owner)
+
+    def flush(p):
+        begin(total_ref.at[block(p)], residual_ref.at[block(p)])
+
+    for p in (0, *range(2, dp_count)):
+        flush(p)
+    clear(ids[1], total_ref)
+    flush(1)
+    rows_ref[...] = update_ref[...].astype(jnp.float32)
+    pairs = [*zip(new, helds), (rows_ref, wide_ref.at[block(0)])]
+    scatter_rows(look_in(own_ids_ref), count, pairs)
+    for held, out in zip(helds, outs):
+        begin(held, out)
+    copies += narrow(wide_ref.at[block(0)], block_ref, out_ref.at[block(0)], sems, len(copies))
     wait_all(copies)
 
 
-def store(ids, total, helds, updates, wide, rounded, place):
-    size, count, dp_count = helds[0].shape, ids.shape[2] - LANES, ids.shape[0]
+def store(ids, own_ids, total, helds, updates, wide, rounded):
+    size, count, dp_count = helds[0].shape, own_ids.shape[2], ids.shape[0]
+    n = dp_count + 1
     out = call(
         functools.partial(store_body, dp_count),
         "store",
         [],
-        [ids_of(ids, place)] + [(v, True) for v in [total, *helds, *updates, wide, rounded]],
-        [(size, jnp.float32, True)] * 3
+        [ids_of(own_ids, 0)]
+        + [ids_of(ids, p) for p in range(dp_count)]
+        + [(v, True) for v in [total, *helds, *updates, wide, rounded]],
+        [(total.shape, jnp.float32, True)]
+        + [(size, jnp.float32, True)] * 3
         + [(wide.shape, jnp.float32, True), (total.shape, jnp.float32, False)]
         + [(size, jnp.float32, False)] * 3
         + [(wide.shape, rounded.dtype, False)],
-        [pltpu.VMEM((count, LANES), jnp.float32), pltpu.VMEM(size, rounded.dtype), DMA((8 + 2 * dp_count,))],
-        {2: 0, 3: 1, 4: 2, 8: 3},
+        [pltpu.VMEM((count, LANES), jnp.float32), pltpu.VMEM(size, rounded.dtype), DMA((6 + PARTS + 2 * dp_count,))],
+        {n: 0, n + 1: 1, n + 2: 2, n + 3: 3, n + 7: 4},
         traffic=4 * WEIGHT * size[0] * LANES,
     )
-    return out[4], out[5:8], out[3], out[8]
+    return out[5], out[6:9], out[4], out[9]
 
 
 def relay(values, after):
@@ -412,7 +441,7 @@
         lambda *_: None,
         "relay",
         [],
-        [(values, True), (away(after), False)],
+        [(values, True), after],
         [(values.shape, values.dtype, True)],
         (),
         {0: 0},
@@ -424,7 +453,7 @@
     wide_ref, out_ref, rows_ref, blocks_ref, sems = refs[2 * count + 2 :]
     copies = []
     for n in range(count):
-        copies += spread_one(ids[n], updates[n], wide_ref, out_ref, rows_ref, blocks_ref.at[n], sems, 2 * n)
+        copies += spread_one(ids[n], updates[n], wide_ref, out_ref, rows_ref, blocks_ref.at[n], sems, PARTS * n)
     wait_all(copies)
 
 
@@ -440,7 +469,7 @@
         [
             pltpu.VMEM(updates[0].shape, jnp.float32),
             pltpu.VMEM((n, wide.shape[0] // dp_count, LANES), kind),
-            DMA((2 * n,)),
+            DMA((PARTS * n,)),
         ],
         {n: 0, 1 + 2 * n: 1},
         traffic=WEIGHT * wide.size,
@@ -475,21 +504,23 @@
     def chunks_of(hop):
         return [tensor_count - hop, hop] if hop < tensor_count // 2 else [hop]
 
-    total, held_grad, ids = load(plan, residual[0], token_grad, own, chosen, chunks_of(1))
+    total, held_grad, own, ids, own_ids = load(plan, residual[0], token_grad, own, chosen, [0, *chunks_of(1)])
     for hop in range(1, tensor_count // 2):
-        chunks = [front, back]
+        chunks, places = [front, back], chunks_of(hop)
+        if hop == 1:
+            chunks, places = [own, *chunks], [0, *places]
         if hop == tensor_count // 2 - 1:
             front, back = front[: tokens // 2], back[tokens // 2 :]
         front, back = lax.ppermute(front, "tensor", ahead), lax.ppermute(back, "tensor", behind)
         side, sources = None, ()
         if hop == tensor_count // 2 - 1:
-            side, sources = "pick", [*helds, ids_of(ids, own_place)]
+            side, sources = "pick", [*helds, ids_of(own_ids, 0)]
         elif hop == 1:
             side, sources = "states", states
         elif hop == 2:
             side, sources = "params", [tiles(params)]
         total, held_grad, *fetched = accumulate(
-            plan, total, chunks, chunks_of(hop), held_grad, token_grad, chunks_of(hop + 1), side, sources
+            plan, total, chunks, places, held_grad, token_grad, chunks_of(hop + 1), side, sources
         )
         if side == "states":
             helds = fetched
@@ -497,7 +528,7 @@
             (wide,) = fetched
         if side == "pick":
             picked = fetched
-    total = tiles(last(plan, total, front, back, tensor_count // 2, held_grad))
+    total = tiles(last(total, front, back, held_grad))
 
     received, sums = [], []
     for k in range(1, chips):
@@ -507,7 +538,8 @@
         received.append(send(sums[-1], k))
     other = pack(ids, total, place_of(0, 1), jnp.bfloat16, sums)
     received.append(swap(other))
-    total, mine = close(ids, total, own_place, range(1, dp_count), [*sums, other])
+    total, mine = close(ids, total, own_place, range(2, dp_count), [*sums, other])
+    received[0] = relay(received[0], (mine, True))
     for part in received:
         mine = mine + part.astype(jnp.float32)
     mean_grad = mine / dp_count
@@ -521,10 +553,10 @@
     far = [send(rounded, k) for k in range(1, chips)]
     near = swap(rounded)
     new_residual, fresh, wide, out = store(
-        ids, total, helds, [one, two, weights], wide, rounded, own_place
+        ids, own_ids, total, helds, [one, two, weights], wide, rounded
     )
     for k in range(1, chips):
-        direct = relay(far[k - 1], out)
+        direct = relay(far[k - 1], (away(out), False))
         across = swap(direct)
         updates, places = [direct], [place_of(chips - k, 0)]
         if k == 1:

time: 65.3 us -> 59.8 us (0.916)
  Pallas kernels: 47.1 us -> 41.6 us
    pallas_call x13 -> x14, Pallas kernels: 47.1 us -> 41.6 us  [call(): pl.pallas_call(body, out_shape=[pltpu.VMEM(shape, kind) if held else jax....]
  transfers between devices with their start and end apart: 14 -> 14, of which waited for: 3 -> 4; matrix products, arithmetic and copies ran while one was open for 1% -> 1% of each run, Pallas kernels for 60% -> 60%
where the time goes in v3:
time: 59.8 us; the launch traced here: 59.6 us
  Pallas kernels  41.6 us (70%)
  starting transfers between devices  13.4 us (22%)
  waiting for transfers between devices  2.62 us (4%)
  between operations  0.79 us (1%)
  local copies, waits for them, and re-layouts  0.71 us (1%)
    pallas_call x14, Pallas kernels, call(): pl.pallas_call(body, out_shape=[pltpu.VMEM(shape, kind) if held else jax....  41.6 us
    ppermute x3, starting transfers between devices, local(): lax.ppermute(front, 'tensor', ahead)  4.92 us
    ppermute x2, starting transfers between devices, send(): lax.ppermute(values, 'dp', [(d, (d // 2 + k) % chips * 2 + d % 2) for d i...  3.21 us
    ppermute x1, starting transfers between devices, local(): lax.ppermute(own, 'tensor', ahead)  3.02 us
    ppermute x3, waiting for transfers between devices, local(): lax.ppermute(front, 'tensor', ahead)  1.47 us
    ppermute x3, starting transfers between devices, local(): lax.ppermute(back, 'tensor', behind)  1.27 us
  transfers between devices with their start and end apart: 14, of which 4 were waited for; matrix products, arithmetic and copies ran while one was open for 1% of the time, Pallas kernels for 60%

profile of v3, /device:TPU:0, one launch (start us, length us, event | category | flops | bytes accessed | tf_op | source)
XLA Modules:
  0.0 59.6 jit_solution(2476901442748843951)
XLA Ops:
  0.6 3.0 %collective-permute-start = (bf16[256,512]{1,0:T(8,128)(2,1)}, bf16[256,512]{1,0:T(8,128)(2,1)S(1)}, u32[]{:S(2)}, u32[]{:S(2)}) collective-permute-start(bf16[256,512]{1,0:T(8,128)(2,1)} %bitcast.73), channel_id=1, source_target_pairs={{1,3},{3,5},{5,7},{7,6},{6,4},{4,2},{2,0},{0,1},{9,11},{11,13},{13... | collective-permute-start | bytes 786440 | tf_op jit(solution)/shard_map/ppermute | solution.py:503
  3.8 0.7 %dynamic-slice_bitcast_fusion.plan_ref = s32[12]{0:T(128)S(1)} fusion(s32[4,8,12]{2,1,0:T(8,128)} %constant.34.clone, s32[]{:T(128)S(6)} %select_n.6, s32[]{:T(128)S(6)} %select_n.7), kind=kLoop, calls=%fused_computation.5 | loop fusion | bytes 104 | tf_op jit(solution)/shard_map/squeeze | solution.py:488
  4.5 5.4 %load.1 = (f32[512,3584]{1,0:T(8,128)S(1)}, bf16[2048,3584]{1,0:T(8,128)(2,1)S(1)}, bf16[256,512]{1,0:T(8,128)(2,1)S(1)}, s32[4,1,1024]{2,1,0:T(1,128)S(1)}, s32[1,1,896]{2,1,0:T(1,128)S(1)}) custom-call(s32[12]{0:T(128)S(1)} %dynamic-slice_bitcast_fusion.plan_ref, f32[512,3584]{1,0:T(8,128)} %bitcast.64, bf16[2048,3584]{1,0:T(8,128)(2,1)} %bitcast.60, ...), custom_call_target="tpu_custom_call" | custom-call | flops 11274289152 | bytes 44040192 | tf_op jit(solution)/shard_map/load/pallas_call | solution.py:137
  10.2 1.7 %collective-permute-start.2 = (bf16[256,512]{1,0:T(8,128)(2,1)S(1)}, bf16[256,512]{1,0:T(8,128)(2,1)S(1)}, u32[]{:S(2)}, u32[]{:S(2)}) collective-permute-start(bf16[256,512]{1,0:T(8,128)(2,1)S(1)} %collective-permute-done.refs_1_), channel_id=1, source_target_pairs={{1,3},{3,5},{5,7},{7,6},{6,4},{4,2},{2,0},{0,1},{9,11},{11,13},{13... | collective-permute-start | bytes 786440 | tf_op jit(solution)/shard_map/ppermute | solution.py:514
  12.3 4.3 %accumulate.3 = (f32[512,3584]{1,0:T(8,128)S(1)}, bf16[2048,3584]{1,0:T(8,128)(2,1)S(1)}, f32[3584,128]{1,0:T(8,128)S(1)}, f32[3584,128]{1,0:T(8,128)S(1)}, f32[3584,128]{1,0:T(8,128)S(1)}) custom-call(s32[12]{0:T(128)S(1)} %dynamic-slice_bitcast_fusion.plan_ref, ...), custom_call_target="tpu_custom_call", output_to_operand_aliasing={{0}: (1, {}), {1}: (2, {})} | custom-call | flops 33822867456 | bytes 44040192 | tf_op jit(solution)/shard_map/accumulate/pallas_call | solution.py:137
  16.5 1.2 %collective-permute-done.2.refs_0_ = bf16[256,512]{1,0:T(8,128)(2,1)S(1)} collective-permute-done((bf16[256,512]{1,0:T(8,128)(2,1)S(1)}, bf16[256,512]{1,0:T(8,128)(2,1)S(1)}, u32[]{:S(2)}, u32[]{:S(2)}) %collective-permute-start.2) | collective-permute-done | bytes 262176 | tf_op jit(solution)/shard_map/ppermute | solution.py:514
  17.7 1.6 %collective-permute-start.4 = (bf16[256,512]{1,0:T(8,128)(2,1)S(1)}, bf16[256,512]{1,0:T(8,128)(2,1)S(1)}, u32[]{:S(2)}, u32[]{:S(2)}) collective-permute-start(bf16[256,512]{1,0:T(8,128)(2,1)S(1)} %collective-permute-done.2.refs_0_), channel_id=1, source_target_pairs={{1,3},{3,5},{5,7},{7,6},{6,4},{4,2},{2,0},{0,1},{9,11},{11,13},{13... | collective-permute-start | bytes 786440 | tf_op jit(solution)/shard_map/ppermute | solution.py:514
  19.8 4.3 %accumulate.4 = (f32[512,3584]{1,0:T(8,128)S(1)}, bf16[2048,3584]{1,0:T(8,128)(2,1)S(1)}, f32[14336,128]{1,0:T(8,128)S(1)}) custom-call(s32[12]{0:T(128)S(1)} %dynamic-slice_bitcast_fusion.plan_ref, f32[512,3584]{1,0:T(8,128)S(1)} %get-tuple-element.39.total_in, ...), custom_call_target="tpu_custom_call", output_to_operand_aliasing={{0}: (1, {}), {1}: (2, {})} | custom-call | flops 22548578304 | bytes 44040192 | tf_op jit(solution)/shard_map/accumulate/pallas_call | solution.py:137
  24.3 1.6 %collective-permute-start.6 = (bf16[128,512]{1,0:T(8,128)(2,1)S(1)}, bf16[128,512]{1,0:T(8,128)(2,1)S(1)}, u32[]{:S(2)}, u32[]{:S(2)}) collective-permute-start(bf16[128,512]{1,0:T(8,128)(2,1)S(1)} %slice.8), channel_id=1, source_target_pairs={{1,3},{3,5},{5,7},{7,6},{6,4},{4,2},{2,0},{0,1},{9,11},{11,13},{13... | collective-permute-start | bytes 393224 | tf_op jit(solution)/shard_map/ppermute | solution.py:514
  25.9 0.5 collective-permute-start.7
  26.5 5.3 %accumulate.5 = (f32[512,3584]{1,0:T(8,128)S(1)}, bf16[2048,3584]{1,0:T(8,128)(2,1)S(1)}, f32[896,128]{1,0:T(8,128)S(1)}, f32[896,128]{1,0:T(8,128)S(1)}, f32[896,128]{1,0:T(8,128)S(1)}) custom-call(s32[12]{0:T(128)S(1)} %dynamic-slice_bitcast_fusion.plan_ref, ...), custom_call_target="tpu_custom_call", output_to_operand_aliasing={{0}: (1, {}), {1}: (2, {})} | custom-call | flops 22548578304 | bytes 44040192 | tf_op jit(solution)/shard_map/accumulate/pallas_call | solution.py:137
  31.8 2.0 %last.1 = f32[512,3584]{1,0:T(8,128)S(1)} custom-call(f32[512,3584]{1,0:T(8,128)S(1)} %get-tuple-element.46.total_in, bf16[2048,3584]{1,0:T(8,128)(2,1)S(1)} %get-tuple-element.47.grad_ref, bf16[128,512]{1,0:T(8,128)(2,1)S(1)} %collective-permute-done.6.front_ref, bf16[128,512]{1,0:T(8,128)(2,1)S(1)} %collective-permute-done.7.back_ref), custom_call_target="tpu_custom_call", output_to_operand_aliasing={{}: (0, {})} | custom-call | flops 939524096 | bytes 14680064 | tf_op jit(solution)/shard_map/last/pallas_call | solution.py:137
  33.8 1.5 %pack.4 = bf16[896,128]{1,0:T(8,128)(2,1)S(1)} custom-call(s32[4,1,1024]{2,1,0:T(1,128)S(1)} %get-tuple-element.35.ids_ref.own_ids.refs_0_.refs_1_.refs_2_.refs_3_, f32[14336,128]{1,0:T(8,128)S(1)} %bitcast.55), custom_call_target="tpu_custom_call" | custom-call | bytes 4587520 | tf_op jit(solution)/shard_map/pack/pallas_call | solution.py:137
  35.4 1.4 %pack.3 = f32[896,128]{1,0:T(8,128)S(1)} custom-call(s32[4,1,1024]{2,1,0:T(1,128)S(1)} %get-tuple-element.35.ids_ref.own_ids.refs_0_.refs_1_.refs_2_.refs_3_, f32[14336,128]{1,0:T(8,128)S(1)} %bitcast.56), custom_call_target="tpu_custom_call" | custom-call | bytes 4587520 | tf_op jit(solution)/shard_map/pack/pallas_call | solution.py:137
  36.9 1.6 %collective-permute-start.9 = (bf16[896,128]{1,0:T(8,128)(2,1)S(1)}, bf16[896,128]{1,0:T(8,128)(2,1)S(1)}, u32[]{:S(2)}, u32[]{:S(2)}) collective-permute-start(bf16[896,128]{1,0:T(8,128)(2,1)S(1)} %add_convert_fusion.refs_0_.refs_3_), channel_id=1, source_target_pairs={{0,16},{8,24},{16,0},{24,8},{1,17},{9,25},{17,1},{25,9},{2,18},{10... | collective-permute-start | bytes 688136 | tf_op jit(solution)/shard_map/ppermute | solution.py:499
  38.5 1.4 %pack.5.refs_4_ = bf16[896,128]{1,0:T(8,128)(2,1)S(1)} custom-call(s32[4,1,1024]{2,1,0:T(1,128)S(1)} %get-tuple-element.35.ids_ref.own_ids.refs_0_.refs_1_.refs_2_.refs_3_, f32[14336,128]{1,0:T(8,128)S(1)} %bitcast.57, bf16[896,128]{1,0:T(8,128)(2,1)S(1)} %add_convert_fusion.refs_0_.refs_3_), custom_call_target="tpu_custom_call" | custom-call | bytes 4587520 | tf_op jit(solution)/shard_map/pack/pallas_call | solution.py:137
  40.2 4.0 %close.1 = (f32[14336,128]{1,0:T(8,128)S(1)}, f32[896,128]{1,0:T(8,128)S(1)}) custom-call(s32[4,1,1024]{2,1,0:T(1,128)S(1)} %get-tuple-element.35.ids_ref.own_ids.refs_0_.refs_1_.refs_2_.refs_3_, s32[4,1,1024]{2,1,0:T(1,128)S(1)} %get-tuple-element.35.ids_ref.own_ids.refs_0_.refs_1_.refs_2_.refs_3_, ...), custom_call_target="tpu_custom_call", output_to_operand_aliasing={{0}: (3, {})} | custom-call | bytes 458752 | tf_op jit(solution)/shard_map/close/pallas_call | solution.py:137
  44.2 0.8 %collective-permute-done.9.__0_ = bf16[896,128]{1,0:T(8,128)(2,1)S(1)} collective-permute-done((bf16[896,128]{1,0:T(8,128)(2,1)S(1)}, bf16[896,128]{1,0:T(8,128)(2,1)S(1)}, u32[]{:S(2)}, u32[]{:S(2)}) %collective-permute-start.9) | collective-permute-done | bytes 229408 | tf_op jit(solution)/shard_map/ppermute | solution.py:499
  45.0 0.4 fusion
  45.4 1.6 %collective-permute-start.12 = (bf16[896,128]{1,0:T(8,128)(2,1)S(1)}, bf16[896,128]{1,0:T(8,128)(2,1)S(1)}, u32[]{:S(2)}, u32[]{:S(2)}) collective-permute-start(bf16[896,128]{1,0:T(8,128)(2,1)S(1)} %get-tuple-element.63.refs_12_), channel_id=1, source_target_pairs={{0,16},{8,24},{16,0},{24,8},{1,17},{9,25},{17,1},{25,9},{2,18},{10... | collective-permute-start | bytes 688136 | tf_op jit(solution)/shard_map/ppermute | solution.py:499
  47.0 6.0 %store.1 = (f32[14336,128]{1,0:T(8,128)S(1)}, f32[3584,128]{1,0:T(8,128)S(1)}, f32[3584,128]{1,0:T(8,128)S(1)}, f32[3584,128]{1,0:T(8,128)S(1)}, f32[14336,128]{...) custom-call(s32[1,1,896]{2,1,0:T(1,128)S(1)} %get-tuple-element.34.r, ...), custom_call_target="tpu_custom_call", output_to_operand_aliasing={{0}: (5, {}), {1}: (6, {}), {2}: (7, {}), {3}: (8, {}), {4}... | custom-call | bytes 44040192 | tf_op jit(solution)/shard_map/store/pallas_call | solution.py:137
  53.0 0.6 collective-permute-start.13
  53.6 3.5 %spread.2 = (f32[14336,128]{1,0:T(8,128)S(1)}, bf16[14336,128]{1,0:T(8,128)(2,1)}) custom-call(s32[4,1,1024]{2,1,0:T(1,128)S(1)} %get-tuple-element.35.ids_ref.own_ids.refs_0_.refs_1_.refs_2_.refs_3_, s32[4,1,1024]{2,1,0:T(1,128)S(1)} %get-tuple-element.35.ids_ref.own_ids.refs_0_.refs_1_.refs_2_.refs_3_, ...), custom_call_target="tpu_custom_call", output_to_operand_aliasing={{0}: (2, {}), {1}: (5, {})} | custom-call | bytes 44040192 | tf_op jit(solution)/shard_map/spread/pallas_call | solution.py:137
  57.1 2.4 %spread.3 = (f32[14336,128]{1,0:T(8,128)S(1)}, bf16[14336,128]{1,0:T(8,128)(2,1)}) custom-call(s32[4,1,1024]{2,1,0:T(1,128)S(1)} %get-tuple-element.35.ids_ref.own_ids.refs_0_.refs_1_.refs_2_.refs_3_, f32[14336,128]{1,0:T(8,128)S(1)} %get-tuple-element.60.refs_1_, ...), custom_call_target="tpu_custom_call", output_to_operand_aliasing={{0}: (1, {}), {1}: (3, {})} | custom-call | bytes 44040192 | tf_op jit(solution)/shard_map/spread/pallas_call | solution.py:137
  (23 shorter events, 1.9 us)
Async XLA Ops:
  0.6 9.6 %collective-permute-start = (bf16[256,512]{1,0:T(8,128)(2,1)}, bf16[256,512]{1,0:T(8,128)(2,1)S(1)}, u32[]{:S(2)}, u32[]{:S(2)}) collective-permute-start(bf16[256,512]{1,0:T(8,128)(2,1)} %bitcast.73), channel_id=1, source_target_pairs={{1,3},{3,5},{5,7},{7,6},{6,4},{4,2},{2,0},{0,1},{9,11},{11,13},{13... | collective-permute-start | bytes 786440 | tf_op jit(solution)/shard_map/ppermute | solution.py:503
  3.6 8.3 %collective-permute-start.1 = (bf16[256,512]{1,0:T(8,128)(2,1)}, bf16[256,512]{1,0:T(8,128)(2,1)S(1)}, u32[]{:S(2)}, u32[]{:S(2)}) collective-permute-start(bf16[256,512]{1,0:T(8,128)(2,1)} %bitcast.74), channel_id=1, source_target_pairs={{3,1},{5,3},{7,5},{6,7},{4,6},{2,4},{0,2},{1,0},{11,9},{13,11},{15... | collective-permute-start | bytes 786440 | tf_op jit(solution)/shard_map/ppermute | solution.py:503
  10.2 7.5 %collective-permute-start.2 = (bf16[256,512]{1,0:T(8,128)(2,1)S(1)}, bf16[256,512]{1,0:T(8,128)(2,1)S(1)}, u32[]{:S(2)}, u32[]{:S(2)}) collective-permute-start(bf16[256,512]{1,0:T(8,128)(2,1)S(1)} %collective-permute-done.refs_1_), channel_id=1, source_target_pairs={{1,3},{3,5},{5,7},{7,6},{6,4},{4,2},{2,0},{0,1},{9,11},{11,13},{13... | collective-permute-start | bytes 786440 | tf_op jit(solution)/shard_map/ppermute | solution.py:514
  11.9 7.4 %collective-permute-start.3 = (bf16[256,512]{1,0:T(8,128)(2,1)S(1)}, bf16[256,512]{1,0:T(8,128)(2,1)S(1)}, u32[]{:S(2)}, u32[]{:S(2)}) collective-permute-start(bf16[256,512]{1,0:T(8,128)(2,1)S(1)} %collective-permute-done.1.refs_2_), channel_id=1, source_target_pairs={{3,1},{5,3},{7,5},{6,7},{4,6},{2,4},{0,2},{1,0},{11,9},{13,11},{15... | collective-permute-start | bytes 786440 | tf_op jit(solution)/shard_map/ppermute | solution.py:514
  17.7 6.6 %collective-permute-start.4 = (bf16[256,512]{1,0:T(8,128)(2,1)S(1)}, bf16[256,512]{1,0:T(8,128)(2,1)S(1)}, u32[]{:S(2)}, u32[]{:S(2)}) collective-permute-start(bf16[256,512]{1,0:T(8,128)(2,1)S(1)} %collective-permute-done.2.refs_0_), channel_id=1, source_target_pairs={{1,3},{3,5},{5,7},{7,6},{6,4},{4,2},{2,0},{0,1},{9,11},{11,13},{13... | collective-permute-start | bytes 786440 | tf_op jit(solution)/shard_map/ppermute | solution.py:514
  19.4 6.6 %collective-permute-start.5 = (bf16[256,512]{1,0:T(8,128)(2,1)S(1)}, bf16[256,512]{1,0:T(8,128)(2,1)S(1)}, u32[]{:S(2)}, u32[]{:S(2)}) collective-permute-start(bf16[256,512]{1,0:T(8,128)(2,1)S(1)} %collective-permute-done.3.refs_1_), channel_id=1, source_target_pairs={{3,1},{5,3},{7,5},{6,7},{4,6},{2,4},{0,2},{1,0},{11,9},{13,11},{15... | collective-permute-start | bytes 786440 | tf_op jit(solution)/shard_map/ppermute | solution.py:514
  24.3 7.5 %collective-permute-start.6 = (bf16[128,512]{1,0:T(8,128)(2,1)S(1)}, bf16[128,512]{1,0:T(8,128)(2,1)S(1)}, u32[]{:S(2)}, u32[]{:S(2)}) collective-permute-start(bf16[128,512]{1,0:T(8,128)(2,1)S(1)} %slice.8), channel_id=1, source_target_pairs={{1,3},{3,5},{5,7},{7,6},{6,4},{4,2},{2,0},{0,1},{9,11},{11,13},{13... | collective-permute-start | bytes 393224 | tf_op jit(solution)/shard_map/ppermute | solution.py:514
  25.9 5.9 %collective-permute-start.7 = (bf16[128,512]{1,0:T(8,128)(2,1)S(1)}, bf16[128,512]{1,0:T(8,128)(2,1)S(1)}, u32[]{:S(2)}, u32[]{:S(2)}) collective-permute-start(bf16[128,512]{1,0:T(8,128)(2,1)S(1)} %slice.9), channel_id=1, source_target_pairs={{3,1},{5,3},{7,5},{6,7},{4,6},{2,4},{0,2},{1,0},{11,9},{13,11},{15... | collective-permute-start | bytes 393224 | tf_op jit(solution)/shard_map/ppermute | solution.py:514
  35.3 1.6 %collective-permute-start.8 = (bf16[896,128]{1,0:T(8,128)(2,1)S(1)}, bf16[896,128]{1,0:T(8,128)(2,1)S(1)}, u32[]{:S(2)}, u32[]{:S(2)}) collective-permute-start(bf16[896,128]{1,0:T(8,128)(2,1)S(1)} %pack.4), channel_id=1, source_target_pairs={{0,8},{8,0},{16,24},{24,16},{1,9},{9,1},{17,25},{25,17},{2,10},{10... | collective-permute-start | bytes 688136 | tf_op jit(solution)/shard_map/ppermute | solution.py:496
  36.9 8.0 %collective-permute-start.9 = (bf16[896,128]{1,0:T(8,128)(2,1)S(1)}, bf16[896,128]{1,0:T(8,128)(2,1)S(1)}, u32[]{:S(2)}, u32[]{:S(2)}) collective-permute-start(bf16[896,128]{1,0:T(8,128)(2,1)S(1)} %add_convert_fusion.refs_0_.refs_3_), channel_id=1, source_target_pairs={{0,16},{8,24},{16,0},{24,8},{1,17},{9,25},{17,1},{25,9},{2,18},{10... | collective-permute-start | bytes 688136 | tf_op jit(solution)/shard_map/ppermute | solution.py:499
  40.0 5.0 %collective-permute-start.10 = (bf16[896,128]{1,0:T(8,128)(2,1)S(1)}, bf16[896,128]{1,0:T(8,128)(2,1)S(1)}, u32[]{:S(2)}, u32[]{:S(2)}) collective-permute-start(bf16[896,128]{1,0:T(8,128)(2,1)S(1)} %pack.5.refs_4_), channel_id=1, source_target_pairs={{0,8},{8,0},{16,24},{24,16},{1,9},{9,1},{17,25},{25,17},{2,10},{10... | collective-permute-start | bytes 688136 | tf_op jit(solution)/shard_map/ppermute | solution.py:496
  45.4 7.6 %collective-permute-start.12 = (bf16[896,128]{1,0:T(8,128)(2,1)S(1)}, bf16[896,128]{1,0:T(8,128)(2,1)S(1)}, u32[]{:S(2)}, u32[]{:S(2)}) collective-permute-start(bf16[896,128]{1,0:T(8,128)(2,1)S(1)} %get-tuple-element.63.refs_12_), channel_id=1, source_target_pairs={{0,16},{8,24},{16,0},{24,8},{1,17},{9,25},{17,1},{25,9},{2,18},{10... | collective-permute-start | bytes 688136 | tf_op jit(solution)/shard_map/ppermute | solution.py:499
  47.0 6.6 %collective-permute-start.11 = (bf16[896,128]{1,0:T(8,128)(2,1)S(1)}, bf16[896,128]{1,0:T(8,128)(2,1)S(1)}, u32[]{:S(2)}, u32[]{:S(2)}) collective-permute-start(bf16[896,128]{1,0:T(8,128)(2,1)S(1)} %get-tuple-element.63.refs_12_), channel_id=1, source_target_pairs={{0,8},{8,0},{16,24},{24,16},{1,9},{9,1},{17,25},{25,17},{2,10},{10... | collective-permute-start | bytes 688136 | tf_op jit(solution)/shard_map/ppermute | solution.py:496
  53.0 4.1 %collective-permute-start.13 = (bf16[896,128]{1,0:T(8,128)(2,1)S(1)}, bf16[896,128]{1,0:T(8,128)(2,1)S(1)}, u32[]{:S(2)}, u32[]{:S(2)}) collective-permute-start(bf16[896,128]{1,0:T(8,128)(2,1)S(1)} %relay.3.refs_4_), channel_id=1, source_target_pairs={{0,8},{8,0},{16,24},{24,16},{1,9},{9,1},{17,25},{25,17},{2,10},{10... | collective-permute-start | bytes 688136 | tf_op jit(solution)/shard_map/ppermute | solution.py:496

commit v4 on v3

--- a/solution.py
+++ b/solution.py
@@ -383,57 +383,43 @@
     return copies
 
 
-def store_body(dp_count, own_ids_ref, *refs):
-    ids, total_in, refs = refs[:dp_count], refs[dp_count], refs[dp_count + 1 + 3 :]
-    new, update_ref, refs = refs[:3], refs[4], refs[5:]
-    total_ref, helds, wide_ref, residual_ref, outs, out_ref = refs[0], refs[1:4], refs[4], refs[5], refs[6:9], refs[9]
-    rows_ref, block_ref, sems = refs[10:]
+def store_body(dp_count, own_ids_ref, ids_ref, total_ref, *refs):
+    new, update_ref, refs = refs[3:6], refs[7], refs[8:]
+    helds, wide_ref, residual_ref, outs, out_ref = refs[:3], refs[3], refs[4], refs[5:8], refs[8]
+    rows_ref, block_ref, sems = refs[9:]
     per_owner, count = block_ref.shape[0], update_ref.shape[0]
-    copies = []
-
-    def begin(source, target):
-        copies.extend(split_copies(source, target, 2, sems, len(copies)))
+    copies = split_copies(total_ref, residual_ref, 2 * dp_count, sems)
+    start_all(copies)
+    mine = pl.ds(pl.multiple_of(ids_ref[0, 0] * per_owner, 2 * SUBLANES), per_owner)
+    rows_ref[...] = update_ref[...].astype(jnp.float32)
+    scatter_rows(look_in(own_ids_ref), count, [*zip(new, helds), (rows_ref, wide_ref.at[mine])])
+    for held, out in zip(helds, outs):
+        copies += split_copies(held, out, 2, sems, len(copies))
         start_all(copies[-2:])
-
-    def block(p):
-        return pl.ds(pl.multiple_of(ids[p][0, count] * per_owner, 2 * SUBLANES), per_owner)
-
-    def flush(p):
-        begin(total_ref.at[block(p)], residual_ref.at[block(p)])
-
-    for p in (0, *range(2, dp_count)):
-        flush(p)
-    clear(ids[1], total_ref)
-    flush(1)
-    rows_ref[...] = update_ref[...].astype(jnp.float32)
-    pairs = [*zip(new, helds), (rows_ref, wide_ref.at[block(0)])]
-    scatter_rows(look_in(own_ids_ref), count, pairs)
-    for held, out in zip(helds, outs):
-        begin(held, out)
-    copies += narrow(wide_ref.at[block(0)], block_ref, out_ref.at[block(0)], sems, len(copies))
+    copies += narrow(wide_ref.at[mine], block_ref, out_ref.at[mine], sems, len(copies))
     wait_all(copies)
 
 
 def store(ids, own_ids, total, helds, updates, wide, rounded):
     size, count, dp_count = helds[0].shape, own_ids.shape[2], ids.shape[0]
-    n = dp_count + 1
+    owner = pl.BlockSpec((None, 1, LANES), lambda i: (0, 0, count // LANES), memory_space=pltpu.SMEM)
+    if count % LANES:
+        owner = pl.BlockSpec((None, 1, LANES), lambda i: (0, 0, 0), memory_space=pltpu.SMEM)
+        ids = ids[:, :, count:]
     out = call(
         functools.partial(store_body, dp_count),
         "store",
         [],
-        [ids_of(own_ids, 0)]
-        + [ids_of(ids, p) for p in range(dp_count)]
-        + [(v, True) for v in [total, *helds, *updates, wide, rounded]],
-        [(total.shape, jnp.float32, True)]
-        + [(size, jnp.float32, True)] * 3
+        [ids_of(own_ids, 0), (ids, owner)] + [(v, True) for v in [total, *helds, *updates, wide, rounded]],
+        [(size, jnp.float32, True)] * 3
         + [(wide.shape, jnp.float32, True), (total.shape, jnp.float32, False)]
         + [(size, jnp.float32, False)] * 3
         + [(wide.shape, rounded.dtype, False)],
         [pltpu.VMEM((count, LANES), jnp.float32), pltpu.VMEM(size, rounded.dtype), DMA((6 + PARTS + 2 * dp_count,))],
-        {n: 0, n + 1: 1, n + 2: 2, n + 3: 3, n + 7: 4},
+        {3: 0, 4: 1, 5: 2, 9: 3},
         traffic=4 * WEIGHT * size[0] * LANES,
     )
-    return out[5], out[6:9], out[4], out[9]
+    return out[4], out[5:8], out[3], out[8]
 
 
 def relay(values, after):
@@ -538,7 +524,7 @@
         received.append(send(sums[-1], k))
     other = pack(ids, total, place_of(0, 1), jnp.bfloat16, sums)
     received.append(swap(other))
-    total, mine = close(ids, total, own_place, range(2, dp_count), [*sums, other])
+    total, mine = close(ids, total, own_place, range(1, dp_count), [*sums, other])
     received[0] = relay(received[0], (mine, True))
     for part in received:
         mine = mine + part.astype(jnp.float32)

time: 59.8 us -> 59.6 us (level)
  starting transfers between devices: 13.4 us -> 12.7 us
  transfers between devices with their start and end apart: 14 -> 14, of which waited for: 4 -> 4; matrix products, arithmetic and copies ran while one was open for 1% -> 1% of each run, Pallas kernels for 60% -> 61%
where the time goes in v4:
time: 59.6 us; the launch traced here: 59.4 us
  Pallas kernels  42 us (70%)
  starting transfers between devices  12.7 us (21%)
  waiting for transfers between devices  2.62 us (4%)
  between operations  0.8 us (1%)
  local copies, waits for them, and re-layouts  0.71 us (1%)
    pallas_call x14, Pallas kernels, call(): pl.pallas_call(body, out_shape=[pltpu.VMEM(shape, kind) if held else jax....  42 us
    ppermute x3, starting transfers between devices, local(): lax.ppermute(front, 'tensor', ahead)  4.92 us
    ppermute x2, starting transfers between devices, send(): lax.ppermute(values, 'dp', [(d, (d // 2 + k) % chips * 2 + d % 2) for d i...  3.05 us
    ppermute x1, starting transfers between devices, local(): lax.ppermute(own, 'tensor', ahead)  3.02 us
    ppermute x3, waiting for transfers between devices, local(): lax.ppermute(front, 'tensor', ahead)  1.47 us
    ppermute x3, starting transfers between devices, local(): lax.ppermute(back, 'tensor', behind)  1.27 us
  transfers between devices with their start and end apart: 14, of which 4 were waited for; matrix products, arithmetic and copies ran while one was open for 1% of the time, Pallas kernels for 61%

profile of v4, /device:TPU:0, one launch (start us, length us, event | category | flops | bytes accessed | tf_op | source)
XLA Modules:
  0.0 59.4 jit_solution(1374555768159544261)
XLA Ops:
  0.6 3.0 %collective-permute-start = (bf16[256,512]{1,0:T(8,128)(2,1)}, bf16[256,512]{1,0:T(8,128)(2,1)S(1)}, u32[]{:S(2)}, u32[]{:S(2)}) collective-permute-start(bf16[256,512]{1,0:T(8,128)(2,1)} %bitcast.73), channel_id=1, source_target_pairs={{1,3},{3,5},{5,7},{7,6},{6,4},{4,2},{2,0},{0,1},{9,11},{11,13},{13... | collective-permute-start | bytes 786440 | tf_op jit(solution)/shard_map/ppermute | solution.py:489
  3.8 0.7 %dynamic-slice_bitcast_fusion.plan_ref = s32[12]{0:T(128)S(1)} fusion(s32[4,8,12]{2,1,0:T(8,128)} %constant.34.clone, s32[]{:T(128)S(6)} %select_n.6, s32[]{:T(128)S(6)} %select_n.7), kind=kLoop, calls=%fused_computation.5 | loop fusion | bytes 104 | tf_op jit(solution)/shard_map/squeeze | solution.py:474
  4.5 5.4 %load.1 = (f32[512,3584]{1,0:T(8,128)S(1)}, bf16[2048,3584]{1,0:T(8,128)(2,1)S(1)}, bf16[256,512]{1,0:T(8,128)(2,1)S(1)}, s32[4,1,1024]{2,1,0:T(1,128)S(1)}, s32[1,1,896]{2,1,0:T(1,128)S(1)}) custom-call(s32[12]{0:T(128)S(1)} %dynamic-slice_bitcast_fusion.plan_ref, f32[512,3584]{1,0:T(8,128)} %bitcast.64, bf16[2048,3584]{1,0:T(8,128)(2,1)} %bitcast.60, ...), custom_call_target="tpu_custom_call" | custom-call | flops 11274289152 | bytes 44040192 | tf_op jit(solution)/shard_map/load/pallas_call | solution.py:137
  10.2 1.7 %collective-permute-start.2 = (bf16[256,512]{1,0:T(8,128)(2,1)S(1)}, bf16[256,512]{1,0:T(8,128)(2,1)S(1)}, u32[]{:S(2)}, u32[]{:S(2)}) collective-permute-start(bf16[256,512]{1,0:T(8,128)(2,1)S(1)} %collective-permute-done.refs_1_), channel_id=1, source_target_pairs={{1,3},{3,5},{5,7},{7,6},{6,4},{4,2},{2,0},{0,1},{9,11},{11,13},{13... | collective-permute-start | bytes 786440 | tf_op jit(solution)/shard_map/ppermute | solution.py:500
  12.3 4.3 %accumulate.3 = (f32[512,3584]{1,0:T(8,128)S(1)}, bf16[2048,3584]{1,0:T(8,128)(2,1)S(1)}, f32[3584,128]{1,0:T(8,128)S(1)}, f32[3584,128]{1,0:T(8,128)S(1)}, f32[3584,128]{1,0:T(8,128)S(1)}) custom-call(s32[12]{0:T(128)S(1)} %dynamic-slice_bitcast_fusion.plan_ref, ...), custom_call_target="tpu_custom_call", output_to_operand_aliasing={{0}: (1, {}), {1}: (2, {})} | custom-call | flops 33822867456 | bytes 44040192 | tf_op jit(solution)/shard_map/accumulate/pallas_call | solution.py:137
  16.5 1.2 %collective-permute-done.2.refs_0_ = bf16[256,512]{1,0:T(8,128)(2,1)S(1)} collective-permute-done((bf16[256,512]{1,0:T(8,128)(2,1)S(1)}, bf16[256,512]{1,0:T(8,128)(2,1)S(1)}, u32[]{:S(2)}, u32[]{:S(2)}) %collective-permute-start.2) | collective-permute-done | bytes 262176 | tf_op jit(solution)/shard_map/ppermute | solution.py:500
  17.7 1.6 %collective-permute-start.4 = (bf16[256,512]{1,0:T(8,128)(2,1)S(1)}, bf16[256,512]{1,0:T(8,128)(2,1)S(1)}, u32[]{:S(2)}, u32[]{:S(2)}) collective-permute-start(bf16[256,512]{1,0:T(8,128)(2,1)S(1)} %collective-permute-done.2.refs_0_), channel_id=1, source_target_pairs={{1,3},{3,5},{5,7},{7,6},{6,4},{4,2},{2,0},{0,1},{9,11},{11,13},{13... | collective-permute-start | bytes 786440 | tf_op jit(solution)/shard_map/ppermute | solution.py:500
  19.4 0.4 collective-permute-start.5
  19.8 4.3 %accumulate.4 = (f32[512,3584]{1,0:T(8,128)S(1)}, bf16[2048,3584]{1,0:T(8,128)(2,1)S(1)}, f32[14336,128]{1,0:T(8,128)S(1)}) custom-call(s32[12]{0:T(128)S(1)} %dynamic-slice_bitcast_fusion.plan_ref, f32[512,3584]{1,0:T(8,128)S(1)} %get-tuple-element.39.total_in, ...), custom_call_target="tpu_custom_call", output_to_operand_aliasing={{0}: (1, {}), {1}: (2, {})} | custom-call | flops 22548578304 | bytes 44040192 | tf_op jit(solution)/shard_map/accumulate/pallas_call | solution.py:137
  24.3 1.6 %collective-permute-start.6 = (bf16[128,512]{1,0:T(8,128)(2,1)S(1)}, bf16[128,512]{1,0:T(8,128)(2,1)S(1)}, u32[]{:S(2)}, u32[]{:S(2)}) collective-permute-start(bf16[128,512]{1,0:T(8,128)(2,1)S(1)} %slice.8), channel_id=1, source_target_pairs={{1,3},{3,5},{5,7},{7,6},{6,4},{4,2},{2,0},{0,1},{9,11},{11,13},{13... | collective-permute-start | bytes 393224 | tf_op jit(solution)/shard_map/ppermute | solution.py:500
  25.9 0.5 collective-permute-start.7
  26.5 5.3 %accumulate.5 = (f32[512,3584]{1,0:T(8,128)S(1)}, bf16[2048,3584]{1,0:T(8,128)(2,1)S(1)}, f32[896,128]{1,0:T(8,128)S(1)}, f32[896,128]{1,0:T(8,128)S(1)}, f32[896,128]{1,0:T(8,128)S(1)}) custom-call(s32[12]{0:T(128)S(1)} %dynamic-slice_bitcast_fusion.plan_ref, ...), custom_call_target="tpu_custom_call", output_to_operand_aliasing={{0}: (1, {}), {1}: (2, {})} | custom-call | flops 22548578304 | bytes 44040192 | tf_op jit(solution)/shard_map/accumulate/pallas_call | solution.py:137
  31.8 2.0 %last.1 = f32[512,3584]{1,0:T(8,128)S(1)} custom-call(f32[512,3584]{1,0:T(8,128)S(1)} %get-tuple-element.46.total_in, bf16[2048,3584]{1,0:T(8,128)(2,1)S(1)} %get-tuple-element.47.grad_ref, bf16[128,512]{1,0:T(8,128)(2,1)S(1)} %collective-permute-done.6.front_ref, bf16[128,512]{1,0:T(8,128)(2,1)S(1)} %collective-permute-done.7.back_ref), custom_call_target="tpu_custom_call", output_to_operand_aliasing={{}: (0, {})} | custom-call | flops 939524096 | bytes 14680064 | tf_op jit(solution)/shard_map/last/pallas_call | solution.py:137
  33.9 1.5 %pack.4 = bf16[896,128]{1,0:T(8,128)(2,1)S(1)} custom-call(s32[4,1,1024]{2,1,0:T(1,128)S(1)} %get-tuple-element.35.ids_ref.own_ids.refs_0_.refs_1_.refs_2_, f32[14336,128]{1,0:T(8,128)S(1)} %bitcast.55), custom_call_target="tpu_custom_call" | custom-call | bytes 4587520 | tf_op jit(solution)/shard_map/pack/pallas_call | solution.py:137
  35.4 1.4 %pack.3 = f32[896,128]{1,0:T(8,128)S(1)} custom-call(s32[4,1,1024]{2,1,0:T(1,128)S(1)} %get-tuple-element.35.ids_ref.own_ids.refs_0_.refs_1_.refs_2_, f32[14336,128]{1,0:T(8,128)S(1)} %bitcast.56), custom_call_target="tpu_custom_call" | custom-call | bytes 4587520 | tf_op jit(solution)/shard_map/pack/pallas_call | solution.py:137
  36.9 1.6 %collective-permute-start.9 = (bf16[896,128]{1,0:T(8,128)(2,1)S(1)}, bf16[896,128]{1,0:T(8,128)(2,1)S(1)}, u32[]{:S(2)}, u32[]{:S(2)}) collective-permute-start(bf16[896,128]{1,0:T(8,128)(2,1)S(1)} %add_convert_fusion.refs_0_.refs_4_), channel_id=1, source_target_pairs={{0,16},{8,24},{16,0},{24,8},{1,17},{9,25},{17,1},{25,9},{2,18},{10... | collective-permute-start | bytes 688136 | tf_op jit(solution)/shard_map/ppermute | solution.py:485
  38.5 1.4 %pack.5.refs_5_ = bf16[896,128]{1,0:T(8,128)(2,1)S(1)} custom-call(s32[4,1,1024]{2,1,0:T(1,128)S(1)} %get-tuple-element.35.ids_ref.own_ids.refs_0_.refs_1_.refs_2_, f32[14336,128]{1,0:T(8,128)S(1)} %bitcast.57, bf16[896,128]{1,0:T(8,128)(2,1)S(1)} %add_convert_fusion.refs_0_.refs_4_), custom_call_target="tpu_custom_call" | custom-call | bytes 4587520 | tf_op jit(solution)/shard_map/pack/pallas_call | solution.py:137
  40.2 4.8 %close.1 = (f32[14336,128]{1,0:T(8,128)S(1)}, f32[896,128]{1,0:T(8,128)S(1)}) custom-call(s32[4,1,1024]{2,1,0:T(1,128)S(1)} %get-tuple-element.35.ids_ref.own_ids.refs_0_.refs_1_.refs_2_, s32[4,1,1024]{2,1,0:T(1,128)S(1)} %get-tuple-element.35.ids_ref.own_ids.refs_0_.refs_1_.refs_2_, ...), custom_call_target="tpu_custom_call", output_to_operand_aliasing={{0}: (4, {})} | custom-call | bytes 458752 | tf_op jit(solution)/shard_map/close/pallas_call | solution.py:137
  45.1 0.4 fusion
  45.5 1.5 %collective-permute-start.12 = (bf16[896,128]{1,0:T(8,128)(2,1)S(1)}, bf16[896,128]{1,0:T(8,128)(2,1)S(1)}, u32[]{:S(2)}, u32[]{:S(2)}) collective-permute-start(bf16[896,128]{1,0:T(8,128)(2,1)S(1)} %get-tuple-element.63.refs_7_), channel_id=1, source_target_pairs={{0,16},{8,24},{16,0},{24,8},{1,17},{9,25},{17,1},{25,9},{2,18},{10... | collective-permute-start | bytes 688136 | tf_op jit(solution)/shard_map/ppermute | solution.py:485
  47.0 5.6 %store.1 = (f32[3584,128]{1,0:T(8,128)S(1)}, f32[3584,128]{1,0:T(8,128)S(1)}, f32[3584,128]{1,0:T(8,128)S(1)}, f32[14336,128]{1,0:T(8,128)S(1)}, f32[14336,128]{...) custom-call(s32[1,1,896]{2,1,0:T(1,128)S(1)} %get-tuple-element.34.r, ...), custom_call_target="tpu_custom_call", output_to_operand_aliasing={{0}: (3, {}), {1}: (4, {}), {2}: (5, {}), {3}: (9, {})} | custom-call | bytes 44040192 | tf_op jit(solution)/shard_map/store/pallas_call | solution.py:137
  52.6 0.8 %collective-permute-done.12.__0_ = bf16[896,128]{1,0:T(8,128)(2,1)S(1)} collective-permute-done((bf16[896,128]{1,0:T(8,128)(2,1)S(1)}, bf16[896,128]{1,0:T(8,128)(2,1)S(1)}, u32[]{:S(2)}, u32[]{:S(2)}) %collective-permute-start.12) | collective-permute-done | bytes 229408 | tf_op jit(solution)/shard_map/ppermute | solution.py:485
  53.4 3.5 %spread.2 = (f32[14336,128]{1,0:T(8,128)S(1)}, bf16[14336,128]{1,0:T(8,128)(2,1)}) custom-call(s32[4,1,1024]{2,1,0:T(1,128)S(1)} %get-tuple-element.35.ids_ref.own_ids.refs_0_.refs_1_.refs_2_, s32[4,1,1024]{2,1,0:T(1,128)S(1)} %get-tuple-element.35.ids_ref.own_ids.refs_0_.refs_1_.refs_2_, ...), custom_call_target="tpu_custom_call", output_to_operand_aliasing={{0}: (2, {}), {1}: (5, {})} | custom-call | bytes 44040192 | tf_op jit(solution)/shard_map/spread/pallas_call | solution.py:137
  56.9 2.4 %spread.3 = (f32[14336,128]{1,0:T(8,128)S(1)}, bf16[14336,128]{1,0:T(8,128)(2,1)}) custom-call(s32[4,1,1024]{2,1,0:T(1,128)S(1)} %get-tuple-element.35.ids_ref.own_ids.refs_0_.refs_1_.refs_2_, f32[14336,128]{1,0:T(8,128)S(1)} %get-tuple-element.60.refs_1_, ...), custom_call_target="tpu_custom_call", output_to_operand_aliasing={{0}: (1, {}), {1}: (3, {})} | custom-call | bytes 44040192 | tf_op jit(solution)/shard_map/spread/pallas_call | solution.py:137
  (23 shorter events, 1.5 us)
Async XLA Ops:
  0.6 9.6 %collective-permute-start = (bf16[256,512]{1,0:T(8,128)(2,1)}, bf16[256,512]{1,0:T(8,128)(2,1)S(1)}, u32[]{:S(2)}, u32[]{:S(2)}) collective-permute-start(bf16[256,512]{1,0:T(8,128)(2,1)} %bitcast.73), channel_id=1, source_target_pairs={{1,3},{3,5},{5,7},{7,6},{6,4},{4,2},{2,0},{0,1},{9,11},{11,13},{13... | collective-permute-start | bytes 786440 | tf_op jit(solution)/shard_map/ppermute | solution.py:489
  3.6 8.3 %collective-permute-start.1 = (bf16[256,512]{1,0:T(8,128)(2,1)}, bf16[256,512]{1,0:T(8,128)(2,1)S(1)}, u32[]{:S(2)}, u32[]{:S(2)}) collective-permute-start(bf16[256,512]{1,0:T(8,128)(2,1)} %bitcast.74), channel_id=1, source_target_pairs={{3,1},{5,3},{7,5},{6,7},{4,6},{2,4},{0,2},{1,0},{11,9},{13,11},{15... | collective-permute-start | bytes 786440 | tf_op jit(solution)/shard_map/ppermute | solution.py:489
  10.2 7.5 %collective-permute-start.2 = (bf16[256,512]{1,0:T(8,128)(2,1)S(1)}, bf16[256,512]{1,0:T(8,128)(2,1)S(1)}, u32[]{:S(2)}, u32[]{:S(2)}) collective-permute-start(bf16[256,512]{1,0:T(8,128)(2,1)S(1)} %collective-permute-done.refs_1_), channel_id=1, source_target_pairs={{1,3},{3,5},{5,7},{7,6},{6,4},{4,2},{2,0},{0,1},{9,11},{11,13},{13... | collective-permute-start | bytes 786440 | tf_op jit(solution)/shard_map/ppermute | solution.py:500
  11.9 7.4 %collective-permute-start.3 = (bf16[256,512]{1,0:T(8,128)(2,1)S(1)}, bf16[256,512]{1,0:T(8,128)(2,1)S(1)}, u32[]{:S(2)}, u32[]{:S(2)}) collective-permute-start(bf16[256,512]{1,0:T(8,128)(2,1)S(1)} %collective-permute-done.1.refs_2_), channel_id=1, source_target_pairs={{3,1},{5,3},{7,5},{6,7},{4,6},{2,4},{0,2},{1,0},{11,9},{13,11},{15... | collective-permute-start | bytes 786440 | tf_op jit(solution)/shard_map/ppermute | solution.py:500
  17.7 6.6 %collective-permute-start.4 = (bf16[256,512]{1,0:T(8,128)(2,1)S(1)}, bf16[256,512]{1,0:T(8,128)(2,1)S(1)}, u32[]{:S(2)}, u32[]{:S(2)}) collective-permute-start(bf16[256,512]{1,0:T(8,128)(2,1)S(1)} %collective-permute-done.2.refs_0_), channel_id=1, source_target_pairs={{1,3},{3,5},{5,7},{7,6},{6,4},{4,2},{2,0},{0,1},{9,11},{11,13},{13... | collective-permute-start | bytes 786440 | tf_op jit(solution)/shard_map/ppermute | solution.py:500
  19.4 6.6 %collective-permute-start.5 = (bf16[256,512]{1,0:T(8,128)(2,1)S(1)}, bf16[256,512]{1,0:T(8,128)(2,1)S(1)}, u32[]{:S(2)}, u32[]{:S(2)}) collective-permute-start(bf16[256,512]{1,0:T(8,128)(2,1)S(1)} %collective-permute-done.3.refs_1_), channel_id=1, source_target_pairs={{3,1},{5,3},{7,5},{6,7},{4,6},{2,4},{0,2},{1,0},{11,9},{13,11},{15... | collective-permute-start | bytes 786440 | tf_op jit(solution)/shard_map/ppermute | solution.py:500
  24.3 7.5 %collective-permute-start.6 = (bf16[128,512]{1,0:T(8,128)(2,1)S(1)}, bf16[128,512]{1,0:T(8,128)(2,1)S(1)}, u32[]{:S(2)}, u32[]{:S(2)}) collective-permute-start(bf16[128,512]{1,0:T(8,128)(2,1)S(1)} %slice.8), channel_id=1, source_target_pairs={{1,3},{3,5},{5,7},{7,6},{6,4},{4,2},{2,0},{0,1},{9,11},{11,13},{13... | collective-permute-start | bytes 393224 | tf_op jit(solution)/shard_map/ppermute | solution.py:500
  25.9 5.9 %collective-permute-start.7 = (bf16[128,512]{1,0:T(8,128)(2,1)S(1)}, bf16[128,512]{1,0:T(8,128)(2,1)S(1)}, u32[]{:S(2)}, u32[]{:S(2)}) collective-permute-start(bf16[128,512]{1,0:T(8,128)(2,1)S(1)} %slice.9), channel_id=1, source_target_pairs={{3,1},{5,3},{7,5},{6,7},{4,6},{2,4},{0,2},{1,0},{11,9},{13,11},{15... | collective-permute-start | bytes 393224 | tf_op jit(solution)/shard_map/ppermute | solution.py:500
  35.3 1.6 %collective-permute-start.8 = (bf16[896,128]{1,0:T(8,128)(2,1)S(1)}, bf16[896,128]{1,0:T(8,128)(2,1)S(1)}, u32[]{:S(2)}, u32[]{:S(2)}) collective-permute-start(bf16[896,128]{1,0:T(8,128)(2,1)S(1)} %pack.4), channel_id=1, source_target_pairs={{0,8},{8,0},{16,24},{24,16},{1,9},{9,1},{17,25},{25,17},{2,10},{10... | collective-permute-start | bytes 688136 | tf_op jit(solution)/shard_map/ppermute | solution.py:482
  36.9 8.1 %collective-permute-start.9 = (bf16[896,128]{1,0:T(8,128)(2,1)S(1)}, bf16[896,128]{1,0:T(8,128)(2,1)S(1)}, u32[]{:S(2)}, u32[]{:S(2)}) collective-permute-start(bf16[896,128]{1,0:T(8,128)(2,1)S(1)} %add_convert_fusion.refs_0_.refs_4_), channel_id=1, source_target_pairs={{0,16},{8,24},{16,0},{24,8},{1,17},{9,25},{17,1},{25,9},{2,18},{10... | collective-permute-start | bytes 688136 | tf_op jit(solution)/shard_map/ppermute | solution.py:485
  39.9 5.1 %collective-permute-start.10 = (bf16[896,128]{1,0:T(8,128)(2,1)S(1)}, bf16[896,128]{1,0:T(8,128)(2,1)S(1)}, u32[]{:S(2)}, u32[]{:S(2)}) collective-permute-start(bf16[896,128]{1,0:T(8,128)(2,1)S(1)} %pack.5.refs_5_), channel_id=1, source_target_pairs={{0,8},{8,0},{16,24},{24,16},{1,9},{9,1},{17,25},{25,17},{2,10},{10... | collective-permute-start | bytes 688136 | tf_op jit(solution)/shard_map/ppermute | solution.py:482
  45.5 7.9 %collective-permute-start.12 = (bf16[896,128]{1,0:T(8,128)(2,1)S(1)}, bf16[896,128]{1,0:T(8,128)(2,1)S(1)}, u32[]{:S(2)}, u32[]{:S(2)}) collective-permute-start(bf16[896,128]{1,0:T(8,128)(2,1)S(1)} %get-tuple-element.63.refs_7_), channel_id=1, source_target_pairs={{0,16},{8,24},{16,0},{24,8},{1,17},{9,25},{17,1},{25,9},{2,18},{10... | collective-permute-start | bytes 688136 | tf_op jit(solution)/shard_map/ppermute | solution.py:485
  47.0 6.4 %collective-permute-start.11 = (bf16[896,128]{1,0:T(8,128)(2,1)S(1)}, bf16[896,128]{1,0:T(8,128)(2,1)S(1)}, u32[]{:S(2)}, u32[]{:S(2)}) collective-permute-start(bf16[896,128]{1,0:T(8,128)(2,1)S(1)} %get-tuple-element.63.refs_7_), channel_id=1, source_target_pairs={{0,8},{8,0},{16,24},{24,16},{1,9},{9,1},{17,25},{25,17},{2,10},{10... | collective-permute-start | bytes 688136 | tf_op jit(solution)/shard_map/ppermute | solution.py:482
  53.4 3.5 %collective-permute-start.13 = (bf16[896,128]{1,0:T(8,128)(2,1)S(1)}, bf16[896,128]{1,0:T(8,128)(2,1)S(1)}, u32[]{:S(2)}, u32[]{:S(2)}) collective-permute-start(bf16[896,128]{1,0:T(8,128)(2,1)S(1)} %relay.3.refs_4_), channel_id=1, source_target_pairs={{0,8},{8,0},{16,24},{24,16},{1,9},{9,1},{17,25},{25,17},{2,10},{10... | collective-permute-start | bytes 688136 | tf_op jit(solution)/shard_map/ppermute | solution.py:482

commit v5 on v4

--- a/solution.py
+++ b/solution.py
@@ -15,6 +15,7 @@
 LANES = 128
 SUBLANES = 8
 UNROLL = 32
+GROUP = 8
 
 
 def ring_order(count):
@@ -250,8 +251,8 @@
 
         def beside(i, steps):
             share = refs[0].shape[0] // steps
-            for first in range(0, share, UNROLL):
-                rows = [i * share + first + k for k in range(UNROLL)]
+            for first in range(0, share, GROUP):
+                rows = [i * share + first + k for k in range(GROUP)]
                 at = [sources[3][0, row] for row in rows]
                 for source, target in zip(sources[:3], refs[:3]):
                     values = [source[pl.ds(a, 1), :] for a in at]

time: 59.6 us -> 59 us (0.990)
  Pallas kernels: 42 us -> 41.4 us
    pallas_call x14, Pallas kernels: 42 us -> 41.4 us  [call(): pl.pallas_call(body, out_shape=[pltpu.VMEM(shape, kind) if held else jax....]
  transfers between devices with their start and end apart: 14 -> 14, of which waited for: 4 -> 4; matrix products, arithmetic and copies ran while one was open for 1% -> 1% of each run, Pallas kernels for 61% -> 60%
where the time goes in v5:
time: 59 us; the launch traced here: 58.7 us
  Pallas kernels  41.4 us (70%)
  starting transfers between devices  12.7 us (22%)
  waiting for transfers between devices  2.62 us (4%)
  between operations  0.8 us (1%)
  local copies, waits for them, and re-layouts  0.71 us (1%)
    pallas_call x14, Pallas kernels, call(): pl.pallas_call(body, out_shape=[pltpu.VMEM(shape, kind) if held else jax....  41.4 us
    ppermute x3, starting transfers between devices, local(): lax.ppermute(front, 'tensor', ahead)  4.92 us
    ppermute x2, starting transfers between devices, send(): lax.ppermute(values, 'dp', [(d, (d // 2 + k) % chips * 2 + d % 2) for d i...  3.09 us
    ppermute x1, starting transfers between devices, local(): lax.ppermute(own, 'tensor', ahead)  3.02 us
    ppermute x3, waiting for transfers between devices, local(): lax.ppermute(front, 'tensor', ahead)  1.47 us
    ppermute x3, starting transfers between devices, local(): lax.ppermute(back, 'tensor', behind)  1.27 us
  transfers between devices with their start and end apart: 14, of which 4 were waited for; matrix products, arithmetic and copies ran while one was open for 1% of the time, Pallas kernels for 60%

profile of v5, /device:TPU:0, one launch (start us, length us, event | category | flops | bytes accessed | tf_op | source)
XLA Modules:
  0.0 58.7 jit_solution(8098909239079330891)
XLA Ops:
  0.6 3.0 %collective-permute-start = (bf16[256,512]{1,0:T(8,128)(2,1)}, bf16[256,512]{1,0:T(8,128)(2,1)S(1)}, u32[]{:S(2)}, u32[]{:S(2)}) collective-permute-start(bf16[256,512]{1,0:T(8,128)(2,1)} %bitcast.73), channel_id=1, source_target_pairs={{1,3},{3,5},{5,7},{7,6},{6,4},{4,2},{2,0},{0,1},{9,11},{11,13},{13... | collective-permute-start | bytes 786440 | tf_op jit(solution)/shard_map/ppermute | solution.py:490
  3.8 0.7 %dynamic-slice_bitcast_fusion.plan_ref = s32[12]{0:T(128)S(1)} fusion(s32[4,8,12]{2,1,0:T(8,128)} %constant.34.clone, s32[]{:T(128)S(6)} %select_n.6, s32[]{:T(128)S(6)} %select_n.7), kind=kLoop, calls=%fused_computation.5 | loop fusion | bytes 104 | tf_op jit(solution)/shard_map/squeeze | solution.py:475
  4.5 5.4 %load.1 = (f32[512,3584]{1,0:T(8,128)S(1)}, bf16[2048,3584]{1,0:T(8,128)(2,1)S(1)}, bf16[256,512]{1,0:T(8,128)(2,1)S(1)}, s32[4,1,1024]{2,1,0:T(1,128)S(1)}, s32[1,1,896]{2,1,0:T(1,128)S(1)}) custom-call(s32[12]{0:T(128)S(1)} %dynamic-slice_bitcast_fusion.plan_ref, f32[512,3584]{1,0:T(8,128)} %bitcast.64, bf16[2048,3584]{1,0:T(8,128)(2,1)} %bitcast.60, ...), custom_call_target="tpu_custom_call" | custom-call | flops 11274289152 | bytes 44040192 | tf_op jit(solution)/shard_map/load/pallas_call | solution.py:138
  10.2 1.7 %collective-permute-start.2 = (bf16[256,512]{1,0:T(8,128)(2,1)S(1)}, bf16[256,512]{1,0:T(8,128)(2,1)S(1)}, u32[]{:S(2)}, u32[]{:S(2)}) collective-permute-start(bf16[256,512]{1,0:T(8,128)(2,1)S(1)} %collective-permute-done.refs_1_), channel_id=1, source_target_pairs={{1,3},{3,5},{5,7},{7,6},{6,4},{4,2},{2,0},{0,1},{9,11},{11,13},{13... | collective-permute-start | bytes 786440 | tf_op jit(solution)/shard_map/ppermute | solution.py:501
  12.3 4.3 %accumulate.3 = (f32[512,3584]{1,0:T(8,128)S(1)}, bf16[2048,3584]{1,0:T(8,128)(2,1)S(1)}, f32[3584,128]{1,0:T(8,128)S(1)}, f32[3584,128]{1,0:T(8,128)S(1)}, f32[3584,128]{1,0:T(8,128)S(1)}) custom-call(s32[12]{0:T(128)S(1)} %dynamic-slice_bitcast_fusion.plan_ref, ...), custom_call_target="tpu_custom_call", output_to_operand_aliasing={{0}: (1, {}), {1}: (2, {})} | custom-call | flops 33822867456 | bytes 44040192 | tf_op jit(solution)/shard_map/accumulate/pallas_call | solution.py:138
  16.5 1.2 %collective-permute-done.2.refs_0_ = bf16[256,512]{1,0:T(8,128)(2,1)S(1)} collective-permute-done((bf16[256,512]{1,0:T(8,128)(2,1)S(1)}, bf16[256,512]{1,0:T(8,128)(2,1)S(1)}, u32[]{:S(2)}, u32[]{:S(2)}) %collective-permute-start.2) | collective-permute-done | bytes 262176 | tf_op jit(solution)/shard_map/ppermute | solution.py:501
  17.7 1.6 %collective-permute-start.4 = (bf16[256,512]{1,0:T(8,128)(2,1)S(1)}, bf16[256,512]{1,0:T(8,128)(2,1)S(1)}, u32[]{:S(2)}, u32[]{:S(2)}) collective-permute-start(bf16[256,512]{1,0:T(8,128)(2,1)S(1)} %collective-permute-done.2.refs_0_), channel_id=1, source_target_pairs={{1,3},{3,5},{5,7},{7,6},{6,4},{4,2},{2,0},{0,1},{9,11},{11,13},{13... | collective-permute-start | bytes 786440 | tf_op jit(solution)/shard_map/ppermute | solution.py:501
  19.4 0.4 collective-permute-start.5
  19.8 4.3 %accumulate.4 = (f32[512,3584]{1,0:T(8,128)S(1)}, bf16[2048,3584]{1,0:T(8,128)(2,1)S(1)}, f32[14336,128]{1,0:T(8,128)S(1)}) custom-call(s32[12]{0:T(128)S(1)} %dynamic-slice_bitcast_fusion.plan_ref, f32[512,3584]{1,0:T(8,128)S(1)} %get-tuple-element.39.total_in, ...), custom_call_target="tpu_custom_call", output_to_operand_aliasing={{0}: (1, {}), {1}: (2, {})} | custom-call | flops 22548578304 | bytes 44040192 | tf_op jit(solution)/shard_map/accumulate/pallas_call | solution.py:138
  24.3 1.6 %collective-permute-start.6 = (bf16[128,512]{1,0:T(8,128)(2,1)S(1)}, bf16[128,512]{1,0:T(8,128)(2,1)S(1)}, u32[]{:S(2)}, u32[]{:S(2)}) collective-permute-start(bf16[128,512]{1,0:T(8,128)(2,1)S(1)} %slice.8), channel_id=1, source_target_pairs={{1,3},{3,5},{5,7},{7,6},{6,4},{4,2},{2,0},{0,1},{9,11},{11,13},{13... | collective-permute-start | bytes 393224 | tf_op jit(solution)/shard_map/ppermute | solution.py:501
  25.9 0.5 collective-permute-start.7
  26.5 4.7 %accumulate.5 = (f32[512,3584]{1,0:T(8,128)S(1)}, bf16[2048,3584]{1,0:T(8,128)(2,1)S(1)}, f32[896,128]{1,0:T(8,128)S(1)}, f32[896,128]{1,0:T(8,128)S(1)}, f32[896,128]{1,0:T(8,128)S(1)}) custom-call(s32[12]{0:T(128)S(1)} %dynamic-slice_bitcast_fusion.plan_ref, ...), custom_call_target="tpu_custom_call", output_to_operand_aliasing={{0}: (1, {}), {1}: (2, {})} | custom-call | flops 22548578304 | bytes 44040192 | tf_op jit(solution)/shard_map/accumulate/pallas_call | solution.py:138
  31.2 2.0 %last.1 = f32[512,3584]{1,0:T(8,128)S(1)} custom-call(f32[512,3584]{1,0:T(8,128)S(1)} %get-tuple-element.46.total_in, bf16[2048,3584]{1,0:T(8,128)(2,1)S(1)} %get-tuple-element.47.grad_ref, bf16[128,512]{1,0:T(8,128)(2,1)S(1)} %collective-permute-done.6.front_ref, bf16[128,512]{1,0:T(8,128)(2,1)S(1)} %collective-permute-done.7.back_ref), custom_call_target="tpu_custom_call", output_to_operand_aliasing={{}: (0, {})} | custom-call | flops 939524096 | bytes 14680064 | tf_op jit(solution)/shard_map/last/pallas_call | solution.py:138
  33.2 1.5 %pack.4 = bf16[896,128]{1,0:T(8,128)(2,1)S(1)} custom-call(s32[4,1,1024]{2,1,0:T(1,128)S(1)} %get-tuple-element.35.ids_ref.own_ids.refs_0_.refs_1_.refs_2_, f32[14336,128]{1,0:T(8,128)S(1)} %bitcast.55), custom_call_target="tpu_custom_call" | custom-call | bytes 4587520 | tf_op jit(solution)/shard_map/pack/pallas_call | solution.py:138
  34.7 1.4 %pack.3 = f32[896,128]{1,0:T(8,128)S(1)} custom-call(s32[4,1,1024]{2,1,0:T(1,128)S(1)} %get-tuple-element.35.ids_ref.own_ids.refs_0_.refs_1_.refs_2_, f32[14336,128]{1,0:T(8,128)S(1)} %bitcast.56), custom_call_target="tpu_custom_call" | custom-call | bytes 4587520 | tf_op jit(solution)/shard_map/pack/pallas_call | solution.py:138
  36.3 1.6 %collective-permute-start.9 = (bf16[896,128]{1,0:T(8,128)(2,1)S(1)}, bf16[896,128]{1,0:T(8,128)(2,1)S(1)}, u32[]{:S(2)}, u32[]{:S(2)}) collective-permute-start(bf16[896,128]{1,0:T(8,128)(2,1)S(1)} %add_convert_fusion.refs_0_.refs_4_), channel_id=1, source_target_pairs={{0,16},{8,24},{16,0},{24,8},{1,17},{9,25},{17,1},{25,9},{2,18},{10... | collective-permute-start | bytes 688136 | tf_op jit(solution)/shard_map/ppermute | solution.py:486
  37.9 1.4 %pack.5.refs_5_ = bf16[896,128]{1,0:T(8,128)(2,1)S(1)} custom-call(s32[4,1,1024]{2,1,0:T(1,128)S(1)} %get-tuple-element.35.ids_ref.own_ids.refs_0_.refs_1_.refs_2_, f32[14336,128]{1,0:T(8,128)S(1)} %bitcast.57, bf16[896,128]{1,0:T(8,128)(2,1)S(1)} %add_convert_fusion.refs_0_.refs_4_), custom_call_target="tpu_custom_call" | custom-call | bytes 4587520 | tf_op jit(solution)/shard_map/pack/pallas_call | solution.py:138
  39.6 4.8 %close.1 = (f32[14336,128]{1,0:T(8,128)S(1)}, f32[896,128]{1,0:T(8,128)S(1)}) custom-call(s32[4,1,1024]{2,1,0:T(1,128)S(1)} %get-tuple-element.35.ids_ref.own_ids.refs_0_.refs_1_.refs_2_, s32[4,1,1024]{2,1,0:T(1,128)S(1)} %get-tuple-element.35.ids_ref.own_ids.refs_0_.refs_1_.refs_2_, ...), custom_call_target="tpu_custom_call", output_to_operand_aliasing={{0}: (4, {})} | custom-call | bytes 458752 | tf_op jit(solution)/shard_map/close/pallas_call | solution.py:138
  44.4 0.4 fusion
  44.9 1.5 %collective-permute-start.12 = (bf16[896,128]{1,0:T(8,128)(2,1)S(1)}, bf16[896,128]{1,0:T(8,128)(2,1)S(1)}, u32[]{:S(2)}, u32[]{:S(2)}) collective-permute-start(bf16[896,128]{1,0:T(8,128)(2,1)S(1)} %get-tuple-element.63.refs_7_), channel_id=1, source_target_pairs={{0,16},{8,24},{16,0},{24,8},{1,17},{9,25},{17,1},{25,9},{2,18},{10... | collective-permute-start | bytes 688136 | tf_op jit(solution)/shard_map/ppermute | solution.py:486
  46.3 5.6 %store.1 = (f32[3584,128]{1,0:T(8,128)S(1)}, f32[3584,128]{1,0:T(8,128)S(1)}, f32[3584,128]{1,0:T(8,128)S(1)}, f32[14336,128]{1,0:T(8,128)S(1)}, f32[14336,128]{...) custom-call(s32[1,1,896]{2,1,0:T(1,128)S(1)} %get-tuple-element.34.r, ...), custom_call_target="tpu_custom_call", output_to_operand_aliasing={{0}: (3, {}), {1}: (4, {}), {2}: (5, {}), {3}: (9, {})} | custom-call | bytes 44040192 | tf_op jit(solution)/shard_map/store/pallas_call | solution.py:138
  52.0 0.8 %collective-permute-done.12.__0_ = bf16[896,128]{1,0:T(8,128)(2,1)S(1)} collective-permute-done((bf16[896,128]{1,0:T(8,128)(2,1)S(1)}, bf16[896,128]{1,0:T(8,128)(2,1)S(1)}, u32[]{:S(2)}, u32[]{:S(2)}) %collective-permute-start.12) | collective-permute-done | bytes 229408 | tf_op jit(solution)/shard_map/ppermute | solution.py:486
  52.8 3.5 %spread.2 = (f32[14336,128]{1,0:T(8,128)S(1)}, bf16[14336,128]{1,0:T(8,128)(2,1)}) custom-call(s32[4,1,1024]{2,1,0:T(1,128)S(1)} %get-tuple-element.35.ids_ref.own_ids.refs_0_.refs_1_.refs_2_, s32[4,1,1024]{2,1,0:T(1,128)S(1)} %get-tuple-element.35.ids_ref.own_ids.refs_0_.refs_1_.refs_2_, ...), custom_call_target="tpu_custom_call", output_to_operand_aliasing={{0}: (2, {}), {1}: (5, {})} | custom-call | bytes 44040192 | tf_op jit(solution)/shard_map/spread/pallas_call | solution.py:138
  56.3 2.4 %spread.3 = (f32[14336,128]{1,0:T(8,128)S(1)}, bf16[14336,128]{1,0:T(8,128)(2,1)}) custom-call(s32[4,1,1024]{2,1,0:T(1,128)S(1)} %get-tuple-element.35.ids_ref.own_ids.refs_0_.refs_1_.refs_2_, f32[14336,128]{1,0:T(8,128)S(1)} %get-tuple-element.60.refs_1_, ...), custom_call_target="tpu_custom_call", output_to_operand_aliasing={{0}: (1, {}), {1}: (3, {})} | custom-call | bytes 44040192 | tf_op jit(solution)/shard_map/spread/pallas_call | solution.py:138
  (23 shorter events, 1.5 us)
Async XLA Ops:
  0.6 9.6 %collective-permute-start = (bf16[256,512]{1,0:T(8,128)(2,1)}, bf16[256,512]{1,0:T(8,128)(2,1)S(1)}, u32[]{:S(2)}, u32[]{:S(2)}) collective-permute-start(bf16[256,512]{1,0:T(8,128)(2,1)} %bitcast.73), channel_id=1, source_target_pairs={{1,3},{3,5},{5,7},{7,6},{6,4},{4,2},{2,0},{0,1},{9,11},{11,13},{13... | collective-permute-start | bytes 786440 | tf_op jit(solution)/shard_map/ppermute | solution.py:490
  3.6 8.3 %collective-permute-start.1 = (bf16[256,512]{1,0:T(8,128)(2,1)}, bf16[256,512]{1,0:T(8,128)(2,1)S(1)}, u32[]{:S(2)}, u32[]{:S(2)}) collective-permute-start(bf16[256,512]{1,0:T(8,128)(2,1)} %bitcast.74), channel_id=1, source_target_pairs={{3,1},{5,3},{7,5},{6,7},{4,6},{2,4},{0,2},{1,0},{11,9},{13,11},{15... | collective-permute-start | bytes 786440 | tf_op jit(solution)/shard_map/ppermute | solution.py:490
  10.2 7.5 %collective-permute-start.2 = (bf16[256,512]{1,0:T(8,128)(2,1)S(1)}, bf16[256,512]{1,0:T(8,128)(2,1)S(1)}, u32[]{:S(2)}, u32[]{:S(2)}) collective-permute-start(bf16[256,512]{1,0:T(8,128)(2,1)S(1)} %collective-permute-done.refs_1_), channel_id=1, source_target_pairs={{1,3},{3,5},{5,7},{7,6},{6,4},{4,2},{2,0},{0,1},{9,11},{11,13},{13... | collective-permute-start | bytes 786440 | tf_op jit(solution)/shard_map/ppermute | solution.py:501
  11.9 7.4 %collective-permute-start.3 = (bf16[256,512]{1,0:T(8,128)(2,1)S(1)}, bf16[256,512]{1,0:T(8,128)(2,1)S(1)}, u32[]{:S(2)}, u32[]{:S(2)}) collective-permute-start(bf16[256,512]{1,0:T(8,128)(2,1)S(1)} %collective-permute-done.1.refs_2_), channel_id=1, source_target_pairs={{3,1},{5,3},{7,5},{6,7},{4,6},{2,4},{0,2},{1,0},{11,9},{13,11},{15... | collective-permute-start | bytes 786440 | tf_op jit(solution)/shard_map/ppermute | solution.py:501
  17.7 6.6 %collective-permute-start.4 = (bf16[256,512]{1,0:T(8,128)(2,1)S(1)}, bf16[256,512]{1,0:T(8,128)(2,1)S(1)}, u32[]{:S(2)}, u32[]{:S(2)}) collective-permute-start(bf16[256,512]{1,0:T(8,128)(2,1)S(1)} %collective-permute-done.2.refs_0_), channel_id=1, source_target_pairs={{1,3},{3,5},{5,7},{7,6},{6,4},{4,2},{2,0},{0,1},{9,11},{11,13},{13... | collective-permute-start | bytes 786440 | tf_op jit(solution)/shard_map/ppermute | solution.py:501
  19.4 6.6 %collective-permute-start.5 = (bf16[256,512]{1,0:T(8,128)(2,1)S(1)}, bf16[256,512]{1,0:T(8,128)(2,1)S(1)}, u32[]{:S(2)}, u32[]{:S(2)}) collective-permute-start(bf16[256,512]{1,0:T(8,128)(2,1)S(1)} %collective-permute-done.3.refs_1_), channel_id=1, source_target_pairs={{3,1},{5,3},{7,5},{6,7},{4,6},{2,4},{0,2},{1,0},{11,9},{13,11},{15... | collective-permute-start | bytes 786440 | tf_op jit(solution)/shard_map/ppermute | solution.py:501
  24.3 6.8 %collective-permute-start.6 = (bf16[128,512]{1,0:T(8,128)(2,1)S(1)}, bf16[128,512]{1,0:T(8,128)(2,1)S(1)}, u32[]{:S(2)}, u32[]{:S(2)}) collective-permute-start(bf16[128,512]{1,0:T(8,128)(2,1)S(1)} %slice.8), channel_id=1, source_target_pairs={{1,3},{3,5},{5,7},{7,6},{6,4},{4,2},{2,0},{0,1},{9,11},{11,13},{13... | collective-permute-start | bytes 393224 | tf_op jit(solution)/shard_map/ppermute | solution.py:501
  25.9 5.2 %collective-permute-start.7 = (bf16[128,512]{1,0:T(8,128)(2,1)S(1)}, bf16[128,512]{1,0:T(8,128)(2,1)S(1)}, u32[]{:S(2)}, u32[]{:S(2)}) collective-permute-start(bf16[128,512]{1,0:T(8,128)(2,1)S(1)} %slice.9), channel_id=1, source_target_pairs={{3,1},{5,3},{7,5},{6,7},{4,6},{2,4},{0,2},{1,0},{11,9},{13,11},{15... | collective-permute-start | bytes 393224 | tf_op jit(solution)/shard_map/ppermute | solution.py:501
  34.6 1.6 %collective-permute-start.8 = (bf16[896,128]{1,0:T(8,128)(2,1)S(1)}, bf16[896,128]{1,0:T(8,128)(2,1)S(1)}, u32[]{:S(2)}, u32[]{:S(2)}) collective-permute-start(bf16[896,128]{1,0:T(8,128)(2,1)S(1)} %pack.4), channel_id=1, source_target_pairs={{0,8},{8,0},{16,24},{24,16},{1,9},{9,1},{17,25},{25,17},{2,10},{10... | collective-permute-start | bytes 688136 | tf_op jit(solution)/shard_map/ppermute | solution.py:483
  36.3 8.2 %collective-permute-start.9 = (bf16[896,128]{1,0:T(8,128)(2,1)S(1)}, bf16[896,128]{1,0:T(8,128)(2,1)S(1)}, u32[]{:S(2)}, u32[]{:S(2)}) collective-permute-start(bf16[896,128]{1,0:T(8,128)(2,1)S(1)} %add_convert_fusion.refs_0_.refs_4_), channel_id=1, source_target_pairs={{0,16},{8,24},{16,0},{24,8},{1,17},{9,25},{17,1},{25,9},{2,18},{10... | collective-permute-start | bytes 688136 | tf_op jit(solution)/shard_map/ppermute | solution.py:486
  39.3 5.1 %collective-permute-start.10 = (bf16[896,128]{1,0:T(8,128)(2,1)S(1)}, bf16[896,128]{1,0:T(8,128)(2,1)S(1)}, u32[]{:S(2)}, u32[]{:S(2)}) collective-permute-start(bf16[896,128]{1,0:T(8,128)(2,1)S(1)} %pack.5.refs_5_), channel_id=1, source_target_pairs={{0,8},{8,0},{16,24},{24,16},{1,9},{9,1},{17,25},{25,17},{2,10},{10... | collective-permute-start | bytes 688136 | tf_op jit(solution)/shard_map/ppermute | solution.py:483
  44.9 7.9 %collective-permute-start.12 = (bf16[896,128]{1,0:T(8,128)(2,1)S(1)}, bf16[896,128]{1,0:T(8,128)(2,1)S(1)}, u32[]{:S(2)}, u32[]{:S(2)}) collective-permute-start(bf16[896,128]{1,0:T(8,128)(2,1)S(1)} %get-tuple-element.63.refs_7_), channel_id=1, source_target_pairs={{0,16},{8,24},{16,0},{24,8},{1,17},{9,25},{17,1},{25,9},{2,18},{10... | collective-permute-start | bytes 688136 | tf_op jit(solution)/shard_map/ppermute | solution.py:486
  46.3 6.4 %collective-permute-start.11 = (bf16[896,128]{1,0:T(8,128)(2,1)S(1)}, bf16[896,128]{1,0:T(8,128)(2,1)S(1)}, u32[]{:S(2)}, u32[]{:S(2)}) collective-permute-start(bf16[896,128]{1,0:T(8,128)(2,1)S(1)} %get-tuple-element.63.refs_7_), channel_id=1, source_target_pairs={{0,8},{8,0},{16,24},{24,16},{1,9},{9,1},{17,25},{25,17},{2,10},{10... | collective-permute-start | bytes 688136 | tf_op jit(solution)/shard_map/ppermute | solution.py:483
  52.8 3.5 %collective-permute-start.13 = (bf16[896,128]{1,0:T(8,128)(2,1)S(1)}, bf16[896,128]{1,0:T(8,128)(2,1)S(1)}, u32[]{:S(2)}, u32[]{:S(2)}) collective-permute-start(bf16[896,128]{1,0:T(8,128)(2,1)S(1)} %relay.3.refs_4_), channel_id=1, source_target_pairs={{0,8},{8,0},{16,24},{24,16},{1,9},{9,1},{17,25},{25,17},{2,10},{10... | collective-permute-start | bytes 688136 | tf_op jit(solution)/shard_map/ppermute | solution.py:483
